TPU v7x, 512 devices: a whole 4x4x16 slice. The times are simulated.
512 devices in a mesh: lat: 16 (over x, y_lo, core), lon: 32 (over y_hi, z).
Axes of the slice: x: 4, y: 4 (y_hi: 2, y_lo: 2; y = y_hi * 2 + y_lo), z: 16, core: 2. Of those that a mesh axis runs over, the one named last changes fastest.
Arguments:
- tracer: float32 [64, 1440, 864], P('lat', 'lon'), may hold values from 1 to 9
- east_courant: float32 [64, 1440, 32], P('lat', 'lon'), may hold values from -0.3 to 0.3
- north_courant: float32 [64, 1440, 32], P('lat', 'lon'), may hold values from -0.3 to 0.3
- east_limiter: int32 [64, 1440, 32], P('lat', 'lon'), may hold values from 0 to 2
- north_limiter: int32 [64, 1440, 32], P('lat', 'lon'), may hold values from 0 to 2
- filter_keep: int32 [64], P('lat'), may hold values from 1 to 721, as said below
- seed_aerosol: float32 [64, 1440, 32], P('lat', 'lon'), may hold values from 0.5 to 5
- volatility: float32 [27], replicated, may hold values from 0.01 to 1000
- cotangent: float32 [64, 1440, 864], P('lat', 'lon'), may hold values from -6 to 6
Outputs:
- particle: float32 [64, 1440, 864], P('lat', 'lon')
- tracer_adjoint: float32 [64, 1440, 864], P('lat', 'lon')
Inputs may be any that keep to these rules, and one draw needn't show every extreme that they name: `filter_keep`: with d = min(i, 63 - i) for row i: rows with d < 2 keep 1 to 32 wavenumbers, and the rows with d = 1 keep exactly 32; every other row keeps 1440 // 2 + 1.
All inputs are finite; a program needn't handle non-finite values.
Results may differ from a plain program's by a relative error of at most 0.0003.
Values sent between devices are 32-bit elements; how exact they have to be, the bound alone decides.
A program may use at most 128 MiB of HBM per device.

v0:
```python
import math

import jax
import jax.numpy as jnp
from jax import lax
from jax.sharding import PartitionSpec as P
from jax.experimental import pallas as pl
from jax.experimental.pallas import tpu as pltpu

NEWTON = 4
KMAX = 32
POLAR = 2


def with_halo(cells, sides, width, closed):
    for axis, dim in sides:
        count = lax.axis_size(axis)
        ends = count if closed else count - 1
        head = lax.slice_in_dim(cells, 0, width, axis=dim)
        tail = lax.slice_in_dim(cells, cells.shape[dim] - width, cells.shape[dim], axis=dim)
        cells = jnp.concatenate(
            [
                lax.ppermute(tail, axis, [(i, (i + 1) % count) for i in range(ends)]),
                cells,
                lax.ppermute(head, axis, [((i + 1) % count, i) for i in range(ends)]),
            ],
            axis=dim,
        )
    return cells


def spread(values, copies):
    return jnp.repeat(values, copies, axis=-1)


def face_weights(courant, limiter):
    upwind = courant >= 0.0
    half = 0.5 * courant
    inner = courant * (7.0 / 12.0)
    outer = jnp.where(limiter == 0, courant * (-1.0 / 12.0), 0.0)
    near_left = jnp.where(
        limiter == 0, inner, jnp.where(limiter == 1, jnp.where(upwind, courant, 0.0), half)
    )
    near_right = jnp.where(
        limiter == 0, inner, jnp.where(limiter == 1, jnp.where(upwind, 0.0, courant), half)
    )
    return jnp.stack([outer, near_left, near_right], axis=0)


def spread_weights(weights, species):
    levels = weights.shape[-1]
    spread_m = level_table(levels, species).T
    return jnp.einsum("...l,lq->...q", weights, spread_m, precision=lax.Precision.HIGHEST)


def zonal_window(window, courant, limiter, species):
    inner_count = window.shape[1] - 4
    weights = spread_weights(
        face_weights(courant[:, 2 : inner_count + 3], limiter[:, 2 : inner_count + 3]), species
    )
    fluxes = (
        weights[0] * (window[:, 0 : inner_count + 1] + window[:, 3 : inner_count + 4])
        + weights[1] * window[:, 1 : inner_count + 2]
        + weights[2] * window[:, 2 : inner_count + 3]
    )
    return window[:, 2 : inner_count + 2] - (fluxes[:, 1:] - fluxes[:, :-1])


def meridional_window(window, courant, limiter, first_row, species):
    inner_count = window.shape[0] - 4
    face_rows = first_row + jnp.arange(inner_count + 1, dtype=jnp.int32)
    opened = jnp.where(face_rows[:, None, None] > 0, courant[2 : inner_count + 3], 0.0)
    weights = spread_weights(face_weights(opened, limiter[2 : inner_count + 3]), species)
    fluxes = (
        weights[0] * (window[0 : inner_count + 1] + window[3 : inner_count + 4])
        + weights[1] * window[1 : inner_count + 2]
        + weights[2] * window[2 : inner_count + 3]
    )
    return window[2 : inner_count + 2] - (fluxes[1:] - fluxes[:-1])


def positive(field):
    return 0.5 * (field + jnp.sqrt(field * field + 1.0))


def level_table(levels, species):
    channel_level = jnp.arange(levels * species, dtype=jnp.int32) // species
    return (channel_level[:, None] == jnp.arange(levels, dtype=jnp.int32)[None, :]).astype(
        jnp.float32
    )


def partition(total_mass, seed_aerosol, volatility):
    levels = seed_aerosol.shape[-1]
    species = volatility.shape[0]
    grouping = level_table(levels, species)
    saturation = jnp.tile(volatility, levels)
    aerosol = seed_aerosol
    for newton_step in range(NEWTON):
        denominator = spread(aerosol, species) + saturation
        fraction = total_mass / denominator
        first_sum = jnp.dot(fraction, grouping, precision=lax.Precision.HIGHEST)
        second_sum = jnp.dot(fraction / denominator, grouping, precision=lax.Precision.HIGHEST)
        residue = 1.0 - seed_aerosol / aerosol - first_sum
        derivative = seed_aerosol / (aerosol * aerosol) + second_sum
        aerosol = aerosol - residue / derivative
    aerosol_q = spread(aerosol, species)
    return total_mass * aerosol_q / (aerosol_q + saturation)


def east_west(field):
    return with_halo(field, (("lon", 1),), 2, True)


def north_south(field):
    return with_halo(field, (("lat", 0),), 2, False)


def fold_rows(gradient):
    inner_rows = gradient.shape[0] - 4
    rim_cells = jnp.concatenate([gradient[:2], gradient[inner_rows + 2 :]], axis=0)
    arrived = north_south(rim_cells)
    middle = gradient[2 : inner_rows + 2]
    return jnp.concatenate(
        [
            middle[:2] + arrived[:2],
            middle[2 : inner_rows - 2],
            middle[inner_rows - 2 :] + arrived[6:],
        ],
        axis=0,
    )


def fold_columns(gradient):
    inner_cols = gradient.shape[1] - 4
    rim_cells = jnp.concatenate([gradient[:, :2], gradient[:, inner_cols + 2 :]], axis=1)
    arrived = east_west(rim_cells)
    middle = gradient[:, 2 : inner_cols + 2]
    return jnp.concatenate(
        [
            middle[:, :2] + arrived[:, :2],
            middle[:, 2 : inner_cols - 2],
            middle[:, inner_cols - 2 :] + arrived[:, 6:],
        ],
        axis=1,
    )


def wave_table(column_count, length):
    position = jnp.arange(column_count, dtype=jnp.int32)
    numbers = jnp.arange(KMAX, dtype=jnp.int32)
    phases = position[:, None] * numbers[None, :] % length
    angles = phases.astype(jnp.float32) * (2.0 * math.pi / length)
    return jnp.concatenate([jnp.cos(angles), jnp.sin(angles)], axis=1)


def wave_weights(keep_values, length):
    numbers = jnp.arange(2 * KMAX, dtype=jnp.int32) % KMAX
    scaling = jnp.where(numbers == 0, 1.0, 2.0) / length
    kept_mask = numbers[None, :] < keep_values[:, None]
    return jnp.where(kept_mask, scaling[None, :], 0.0)


def lowpass_circles(circles, keep_values):
    length = circles.shape[2]
    table_full = wave_table(length, length)
    coefficient = jnp.einsum("rqn,nk->rqk", circles, table_full, precision=lax.Precision.HIGHEST)
    coefficient = coefficient * wave_weights(keep_values, length)[:, None, :]
    lowpass = jnp.einsum("rqk,nk->rqn", coefficient, table_full, precision=lax.Precision.HIGHEST)
    return jnp.where((keep_values <= KMAX)[:, None, None], lowpass, circles)


def polar_kernel(x_ref, w_ref, t_ref, y_ref, out_go, land_go, out_back, land_back,
                 sem_a, sem_b, sem_c, sem_d):
    count = t_ref.shape[0]
    polar_count, col_count, channels = x_ref.shape
    chunk = channels // count
    padded = out_go.shape[1]
    me = lax.axis_index("lon")
    band = lax.axis_index("lat")
    bands = lax.axis_size("lat")
    active = jnp.logical_or(band == 0, band == bands - 1)
    hi = lax.Precision.HIGHEST
    mesh_id = pl.DeviceIdType.MESH

    def remote(src, dst, send_sem, recv_sem, peer):
        return pltpu.make_async_remote_copy(
            src_ref=src, dst_ref=dst, send_sem=send_sem, recv_sem=recv_sem,
            device_id=(band, peer), device_id_type=mesh_id,
        )

    def round_trip(outbox, inbox, send_sems, recv_sems):
        for offset in range(1, count):
            peer = lax.rem(me + offset, count)
            remote(outbox.at[peer], inbox.at[me], send_sems.at[offset], recv_sems.at[me], peer).start()
        inbox[pl.ds(me, 1)] = outbox[pl.ds(me, 1)]
        for offset in range(1, count):
            peer = lax.rem(me + offset, count)
            remote(outbox.at[peer], inbox.at[me], send_sems.at[offset], recv_sems.at[me], peer).wait_send()
        for offset in range(1, count):
            peer = lax.rem(me + count - offset, count)
            remote(outbox.at[peer], inbox.at[peer], send_sems.at[offset], recv_sems.at[peer], peer).wait_recv()

    @pl.when(active)
    def _():
        barrier = pltpu.get_barrier_semaphore()
        for offset in range(1, count):
            peer = lax.rem(me + offset, count)
            pl.semaphore_signal(barrier, 1, device_id=(band, peer), device_id_type=mesh_id)
        pl.semaphore_wait(barrier, count - 1)
        rows = jnp.concatenate([x_ref[r] for r in range(polar_count)], axis=0)
        slot = lax.broadcasted_iota(jnp.int32, (count * padded, channels), 0)
        channel = lax.broadcasted_iota(jnp.int32, (count * padded, channels), 1)
        target = (channel // chunk) * padded + channel % chunk
        packer = jnp.where(slot == target, 1.0, 0.0).astype(jnp.float32)
        packed = lax.dot_general(packer, rows, (((1,), (1,)), ((), ())), precision=hi,
                                 preferred_element_type=jnp.float32)
        out_go[...] = packed.reshape(count, padded, polar_count * col_count)
        round_trip(out_go, land_go, sem_a, sem_b)

        def analyse(s, acc):
            return acc + jnp.dot(land_go[s], t_ref[s], precision=hi,
                                 preferred_element_type=jnp.float32)

        coefficient = lax.fori_loop(
            0, count, analyse, jnp.zeros((padded, t_ref.shape[2]), jnp.float32)
        )
        coefficient = coefficient * w_ref[...]

        def synthesise(s, carry):
            out_back[s] = lax.dot_general(coefficient, t_ref[s], (((1,), (1,)), ((), ())),
                                          precision=hi, preferred_element_type=jnp.float32)
            return carry

        lax.fori_loop(0, count, synthesise, 0)
        round_trip(out_back, land_back, sem_c, sem_d)
        back = land_back[...].reshape(count * padded, polar_count * col_count)
        result = lax.dot_general(back, packer, (((0,), (0,)), ((), ())), precision=hi,
                                 preferred_element_type=jnp.float32)
        for r in range(polar_count):
            y_ref[r] = result[r * col_count : (r + 1) * col_count]

    @pl.when(jnp.logical_not(active))
    def _():
        y_ref[...] = x_ref[...]


def polar_lowpass(end_rows, weights, blocks, call_id):
    polar_count, col_count, channels = end_rows.shape
    count = blocks.shape[0]
    padded = -(-(channels // count) // 8) * 8
    slab = (count, padded, polar_count * col_count)
    vmem = pl.BlockSpec(memory_space=pltpu.VMEM)
    return pl.pallas_call(
        polar_kernel,
        out_shape=jax.ShapeDtypeStruct(end_rows.shape, end_rows.dtype),
        in_specs=[vmem, vmem, vmem],
        out_specs=vmem,
        scratch_shapes=[
            pltpu.VMEM(slab, jnp.float32),
            pltpu.VMEM(slab, jnp.float32),
            pltpu.VMEM(slab, jnp.float32),
            pltpu.VMEM(slab, jnp.float32),
            pltpu.SemaphoreType.DMA((count,)),
            pltpu.SemaphoreType.DMA((count,)),
            pltpu.SemaphoreType.DMA((count,)),
            pltpu.SemaphoreType.DMA((count,)),
        ],
        compiler_params=pltpu.CompilerParams(collective_id=call_id, has_side_effects=True),
    )(end_rows, weights, blocks)


def filter_field(field, filter_keep, call_id):
    row_count, col_count, channels = field.shape
    count = lax.axis_size("lon")
    length = col_count * count
    polar_count = POLAR
    band = lax.axis_index("lat")
    at_north_end = band == 0
    at_south_end = band == lax.axis_size("lat") - 1
    top_rows = field[:polar_count]
    bottom_rows = field[row_count - polar_count :]
    end_rows = jnp.where(at_north_end, top_rows, bottom_rows)
    end_keep = jnp.where(
        at_north_end, filter_keep[:polar_count], filter_keep[row_count - polar_count :]
    )
    table = wave_table(length, length).reshape(count, col_count, 2 * KMAX)
    blocks = jnp.einsum(
        "sjk,rR->srjRk", table, jnp.eye(polar_count, dtype=jnp.float32)
    ).reshape(count, polar_count * col_count, polar_count * 2 * KMAX)
    weights = wave_weights(end_keep, length).reshape(1, polar_count * 2 * KMAX)
    lowpass = polar_lowpass(end_rows, weights, blocks, call_id)
    smoothed = jnp.where((end_keep <= KMAX)[:, None, None], lowpass, end_rows)
    new_top = jnp.where(at_north_end, smoothed, top_rows)
    new_bottom = jnp.where(at_south_end, smoothed, bottom_rows)
    return jnp.concatenate(
        [new_top, field[polar_count : row_count - polar_count], new_bottom], axis=0
    )


def chem_kernel(x_ref, seed_ref, cot_ref, sat_ref, spread_ref, group_ref, p_ref, g_ref):
    hi = lax.Precision.HIGHEST
    x = x_ref[0]
    seed = seed_ref[0]
    cot = cot_ref[0]
    sat = sat_ref[...]
    spread_m = spread_ref[...]
    group_m = group_ref[...]

    def up(v):
        return jnp.dot(v, spread_m, precision=hi, preferred_element_type=jnp.float32)

    def down(v):
        return jnp.dot(v, group_m, precision=hi, preferred_element_type=jnp.float32)

    root = jnp.sqrt(x * x + 1.0)
    mass = 0.5 * (x + root)
    aerosol = seed
    history = []
    for newton_step in range(NEWTON):
        denominator = up(aerosol) + sat
        fraction = mass / denominator
        first_sum = down(fraction)
        second_sum = down(fraction / denominator)
        residue = 1.0 - seed / aerosol - first_sum
        derivative = seed / (aerosol * aerosol) + second_sum
        history.append((aerosol, residue, derivative))
        aerosol = aerosol - residue / derivative
    aerosol_q = up(aerosol)
    final_den = aerosol_q + sat
    p_ref[0] = mass * aerosol_q / final_den
    mass_bar = cot * aerosol_q / final_den
    aerosol_bar = down(cot * mass * sat / (final_den * final_den))
    for newton_step in reversed(range(NEWTON)):
        a_n, residue, derivative = history[newton_step]
        inverse = 1.0 / (up(a_n) + sat)
        third_sum = down(mass * inverse * inverse * inverse)
        slope = -2.0 * (seed / (a_n * a_n * a_n) + third_sum)
        over_g = aerosol_bar / derivative
        over_g2 = over_g * residue / derivative
        mass_bar = mass_bar + up(over_g) * inverse + up(over_g2) * inverse * inverse
        aerosol_bar = over_g2 * slope
    g_ref[0] = mass_bar * 0.5 * (1.0 + x / root)


def chemistry_step(filtered, seed_aerosol, volatility, cotangent):
    rows, cols, channels = filtered.shape
    levels = seed_aerosol.shape[-1]
    species = volatility.shape[0]
    group_m = level_table(levels, species)
    spread_m = group_m.T
    sat = jnp.tile(volatility, levels)[None, :]
    big = pl.BlockSpec((1, cols, channels), lambda i: (i, 0, 0))
    small = pl.BlockSpec((1, cols, levels), lambda i: (i, 0, 0))
    return pl.pallas_call(
        chem_kernel,
        grid=(rows,),
        in_specs=[
            big,
            small,
            big,
            pl.BlockSpec((1, channels), lambda i: (0, 0)),
            pl.BlockSpec((levels, channels), lambda i: (0, 0)),
            pl.BlockSpec((channels, levels), lambda i: (0, 0)),
        ],
        out_specs=[big, big],
        out_shape=[
            jax.ShapeDtypeStruct(filtered.shape, jnp.float32),
            jax.ShapeDtypeStruct(filtered.shape, jnp.float32),
        ],
    )(filtered, seed_aerosol, cotangent, sat, spread_m, group_m)


def local(
    tracer,
    east_courant,
    north_courant,
    east_limiter,
    north_limiter,
    filter_keep,
    seed_aerosol,
    volatility,
    cotangent,
):
    row_count = tracer.shape[0]
    channels = tracer.shape[2]
    levels = east_courant.shape[2]
    species = volatility.shape[0]
    first_row = lax.axis_index("lat") * row_count
    packed = jnp.concatenate([tracer, east_courant, east_limiter.astype(jnp.float32)], axis=2)
    widened = east_west(packed)
    east_speed = widened[:, :, channels : channels + levels]
    east_choice = widened[:, :, channels + levels :].astype(jnp.int32)

    def zonal_only(window):
        return zonal_window(window, east_speed, east_choice, species)

    after_east, east_back = jax.vjp(zonal_only, widened[:, :, :channels])
    stacked = jnp.concatenate(
        [after_east, north_courant, north_limiter.astype(jnp.float32)], axis=2
    )
    tall_window = north_south(stacked)
    north_speed = tall_window[:, :, channels : channels + levels]
    north_choice = tall_window[:, :, channels + levels :].astype(jnp.int32)

    def meridional_only(window):
        return meridional_window(window, north_speed, north_choice, first_row, species)

    after_north, north_back = jax.vjp(meridional_only, tall_window[:, :, :channels])
    filtered = filter_field(after_north, filter_keep, 0)

    particle, chem_grad = chemistry_step(filtered, seed_aerosol, volatility, cotangent)
    adjoint_filtered = filter_field(chem_grad, filter_keep, 1)
    return (particle, fold_columns(east_back(fold_rows(north_back(adjoint_filtered)[0]))[0]))


def solution(mesh):
    in_specs = (
        P("lat", "lon", None),
        P("lat", "lon", None),
        P("lat", "lon", None),
        P("lat", "lon", None),
        P("lat", "lon", None),
        P("lat"),
        P("lat", "lon", None),
        P(),
        P("lat", "lon", None),
    )
    out_specs = (P("lat", "lon", None), P("lat", "lon", None))
    return jax.shard_map(local, mesh=mesh, in_specs=in_specs, out_specs=out_specs, check_vma=False)
```

profile of v0, /device:TPU:1, one launch (start us, length us, event | category | flops | bytes accessed | tf_op | source)
XLA Modules:
  0.0 225.6 jit_solution(1894287486707525755)
XLA Ops:
  0.6 1.2 copy.47
  2.2 4.4 %collective-permute-start = (f32[4,2,928]{2,1,0:T(2,128)S(1)}, f32[4,2,928]{2,1,0:T(2,128)S(1)}, u32[]{:S(2)}, u32[]{:S(2)}) collective-permute-start(f32[4,2,928]{2,1,0:T(2,128)S(1)} %get-tuple-element.46), channel_id=1, source_target_pairs={{0,1},{1,2},{2,3},{3,4},{4,5},{5,6},{6,7},{7,8},{8,9},{9,10},{10,1... | collective-permute-start | bytes 89096 | tf_op jit(solution)/shard_map/ppermute | solution.py:23
  6.6 12.1 %collective-permute-start.1 = (f32[4,2,928]{2,1,0:T(2,128)S(1)}, f32[4,2,928]{2,1,0:T(2,128)S(1)}, u32[]{:S(2)}, u32[]{:S(2)}) collective-permute-start(f32[4,2,928]{2,1,0:T(2,128)S(1)} %get-tuple-element.47), channel_id=1, source_target_pairs={{1,0},{2,1},{3,2},{4,3},{5,4},{6,5},{7,6},{8,7},{9,8},{10,9},{11,1... | collective-permute-start | bytes 89096 | tf_op jit(solution)/shard_map/ppermute | solution.py:25
  18.8 3.1 %fusion.11 = (f32[32,45,32]{2,0,1:T(8,128)S(1)}, f32[32,45,32]{2,0,1:T(8,128)S(1)}) fusion(s32[32,45]{0,1:T(8,128)S(1)} %multiply_add_fusion), kind=kLoop, calls=%fused_computation.29 | loop fusion | flops 414720 | bytes 374400 | tf_op jit(solution)/shard_map/cos | solution.py:154
  21.9 0.7 fusion.46.spread_ref
  22.6 0.3 pad_maximum_fusion.3
  22.9 1.5 multiply_bitcast_fusion
  24.8 0.6 select_n.193.w_ref
  25.3 2.6 %reshape.104 = f32[32,90,128]{2,0,1:T(8,128)} reshape(f32[32,2,45,2,64]{4,3,0,2,1:T(2,128)S(1)} %multiply_bitcast_fusion) | data formatting | bytes 2949120 | tf_op jit(solution)/shard_map/reshape | solution.py:290
  27.9 3.4 %copy.52.t_ref = f32[32,90,128]{2,1,0:T(8,128)} copy(f32[32,90,128]{2,0,1:T(8,128)} %reshape.104) | data formatting | bytes 2949120 | tf_op jit(solution)/shard_map/reshape | solution.py:290
  31.4 0.9 copy.54.cot_ref
  32.3 0.7 copy.53.seed_ref
  33.0 0.7 broadcast_in_dim_tile.3.sat_ref
  34.0 1.1 fusion.25
  35.0 0.2 maximum_maximum_fusion.1
  35.3 0.2 fusion.15
  35.6 0.8 copy-done
  36.4 0.5 copy-done.5
  37.2 3.2 %collective-permute-start.2 = (f32[2,45,928]{2,1,0:T(8,128)S(1)}, f32[2,45,928]{2,1,0:T(8,128)S(1)}, u32[]{:S(2)}, u32[]{:S(2)}) collective-permute-start(f32[2,45,928]{2,1,0:T(8,128)S(1)} %get-tuple-element.48), channel_id=1, source_target_pairs={{0,32},{32,64},{64,96},{96,128},{128,160},{160,192},{192,224},{224... | collective-permute-start | bytes 1002248 | tf_op jit(solution)/shard_map/ppermute | solution.py:23
  40.3 1.9 collective-permute-start.3
  42.3 0.9 fusion.21.group_ref
  43.2 1.8 collective-permute-done.2
  45.0 4.4 %collective-permute-done.3 = f32[2,45,928]{2,1,0:T(8,128)S(1)} collective-permute-done((f32[2,45,928]{2,1,0:T(8,128)S(1)}, f32[2,45,928]{2,1,0:T(8,128)S(1)}, u32[]{:S(2)}, u32[]{:S(2)}) %collective-permute-start.3) | collective-permute-done | bytes 334112 | tf_op jit(solution)/shard_map/ppermute | solution.py:25
  49.4 0.2 select_bitcast_fusion
  49.7 1.3 fusion.23
  50.9 0.3 maximum_maximum_fusion
  51.3 0.4 fusion
  51.7 0.8 slice_select_fusion.1.x_ref
  52.5 4.1 %shard_map.104 = f32[2,45,864]{2,1,0:T(8,128)} custom-call(f32[2,45,864]{2,1,0:T(8,128)} %slice_select_fusion.1.x_ref, f32[1,128]{1,0:T(1,128)} %select_n.193.w_ref, f32[32,90,128]{2,1,0:T(8,128)} %copy.52.t_ref), custom_call_target="tpu_custom_call" | custom-call | tf_op jit(solution)/shard_map/pallas_call | solution.py:254
  56.6 1.1 slice_select_fusion.2
  57.8 0.9 pad_maximum_fusion.4.x_ref
  58.7 23.7 %shard_map.105 = (f32[4,45,864]{2,1,0:T(8,128)}, f32[4,45,864]{2,1,0:T(8,128)}) custom-call(f32[4,45,864]{2,1,0:T(8,128)} %pad_maximum_fusion.4.x_ref, f32[4,45,32]{2,1,0:T(8,128)} %copy.53.seed_ref, f32[4,45,864]{2,1,0:T(8,128)} %copy.54.cot_ref, f32[1,864]{1,0:T(1,128)} %broadcast_in_dim_tile.3.sat_ref, f32[32,864]{1,0:T(8,128)} %fusion.46.spread_ref, ...), custom_call_target="tpu_custom_call" | custom-call | tf_op jit(solution)/shard_map/pallas_call | solution.py:355
  82.3 1.8 slice_select_fusion.4.x_ref
  84.2 4.2 %shard_map.106 = f32[2,45,864]{2,1,0:T(8,128)} custom-call(f32[2,45,864]{2,1,0:T(8,128)} %slice_select_fusion.4.x_ref, f32[1,128]{1,0:T(1,128)} %select_n.193.w_ref, f32[32,90,128]{2,1,0:T(8,128)} %copy.52.t_ref), custom_call_target="tpu_custom_call" | custom-call | tf_op jit(solution)/shard_map/pallas_call | solution.py:254
  88.4 1.1 slice_select_fusion.5
  89.7 0.3 fusion.5
  89.9 0.2 pad_add_fusion
  90.2 2.1 collective-permute-start.4
  92.3 113.1 %collective-permute-done.4 = f32[2,45,864]{2,1,0:T(8,128)S(1)} collective-permute-done((f32[2,45,864]{2,1,0:T(8,128)S(1)}, f32[2,45,864]{2,1,0:T(8,128)S(1)}, u32[]{:S(2)}, u32[]{:S(2)}) %collective-permute-start.4) | collective-permute-done | bytes 311072 | tf_op jit(solution)/shard_map/ppermute | solution.py:23
  205.4 2.0 collective-permute-start.5
  207.5 1.1 copy.56
  208.5 5.4 %collective-permute-done.5 = f32[2,45,864]{2,1,0:T(8,128)S(1)} collective-permute-done((f32[2,45,864]{2,1,0:T(8,128)S(1)}, f32[2,45,864]{2,1,0:T(8,128)S(1)}, u32[]{:S(2)}, u32[]{:S(2)}) %collective-permute-start.5) | collective-permute-done | bytes 311072 | tf_op jit(solution)/shard_map/ppermute | solution.py:25
  214.1 0.2 fusion.20
  214.4 3.3 %collective-permute-start.6 = (f32[4,2,864]{2,1,0:T(2,128)S(1)}, f32[4,2,864]{2,1,0:T(2,128)S(1)}, u32[]{:S(2)}, u32[]{:S(2)}) collective-permute-start(f32[4,2,864]{2,1,0:T(2,128)S(1)} %get-tuple-element.34), channel_id=1, source_target_pairs={{0,1},{1,2},{2,3},{3,4},{4,5},{5,6},{6,7},{7,8},{8,9},{9,10},{10,1... | collective-permute-start | bytes 82952 | tf_op jit(solution)/shard_map/ppermute | solution.py:23
  217.7 5.6 %collective-permute-start.7 = (f32[4,2,864]{2,1,0:T(2,128)S(1)}, f32[4,2,864]{2,1,0:T(2,128)S(1)}, u32[]{:S(2)}, u32[]{:S(2)}) collective-permute-start(f32[4,2,864]{2,1,0:T(2,128)S(1)} %get-tuple-element.35), channel_id=1, source_target_pairs={{1,0},{2,1},{3,2},{4,3},{5,4},{6,5},{7,6},{8,7},{9,8},{10,9},{11,1... | collective-permute-start | bytes 82952 | tf_op jit(solution)/shard_map/ppermute | solution.py:25
  223.3 0.3 pad_add_fusion.2
  223.8 0.5 collective-permute-done.7
  224.5 1.1 copy.57
  (65 shorter events, 2.1 us)
Async XLA Ops:
  0.6 1.2 copy-start.8
  0.6 1.3 copy-start.9
  1.8 20.1 %copy-start.2 = (f32[4,45,864]{2,1,0:T(8,128)}, f32[4,45,864]{2,1,0:T(8,128)S(1)}, u32[]{:S(2)}) copy-start(f32[4,45,864]{2,1,0:T(8,128)S(1)} %copy.47) | copy-start | bytes 1866244
  2.0 20.6 %copy-start.13 = (s32[4]{0:T(128)S(1)}, s32[4]{0:T(128)}, u32[]{:S(2)}) copy-start(s32[4]{0:T(128)} %param.14) | copy-start | bytes 52
  2.2 31.5 %collective-permute-start = (f32[4,2,928]{2,1,0:T(2,128)S(1)}, f32[4,2,928]{2,1,0:T(2,128)S(1)}, u32[]{:S(2)}, u32[]{:S(2)}) collective-permute-start(f32[4,2,928]{2,1,0:T(2,128)S(1)} %get-tuple-element.46), channel_id=1, source_target_pairs={{0,1},{1,2},{2,3},{3,4},{4,5},{5,6},{6,7},{7,8},{8,9},{9,10},{10,1... | collective-permute-start | bytes 89096 | tf_op jit(solution)/shard_map/ppermute | solution.py:23
  6.6 27.1 %collective-permute-start.1 = (f32[4,2,928]{2,1,0:T(2,128)S(1)}, f32[4,2,928]{2,1,0:T(2,128)S(1)}, u32[]{:S(2)}, u32[]{:S(2)}) collective-permute-start(f32[4,2,928]{2,1,0:T(2,128)S(1)} %get-tuple-element.47), channel_id=1, source_target_pairs={{1,0},{2,1},{3,2},{4,3},{5,4},{6,5},{7,6},{8,7},{9,8},{10,9},{11,1... | collective-permute-start | bytes 89096 | tf_op jit(solution)/shard_map/ppermute | solution.py:25
  22.9 1.6 copy-start.10
  22.9 1.7 copy-start.11
  27.9 3.4 %copy-start.7 = (f32[4,45,864]{2,0,1:T(4,128)S(1)}, f32[4,45,864]{2,0,1:T(4,128)}, u32[]{:S(2)}) copy-start(f32[4,45,864]{2,0,1:T(4,128)} %param.17) | copy-start | bytes 1866244
  31.3 0.9 copy-start.12
  31.3 1.7 copy-start.14
  31.3 2.4 %copy-start.3 = (f32[4,45,864]{2,1,0:T(8,128)S(1)}, f32[4,45,864]{2,1,0:T(8,128)}, u32[]{:S(2)}) copy-start(f32[4,45,864]{2,1,0:T(8,128)} %copy-done.2) | copy-start | bytes 1866244
  35.0 1.3 copy-start
  35.3 1.6 copy-start.5
  37.2 7.9 %collective-permute-start.2 = (f32[2,45,928]{2,1,0:T(8,128)S(1)}, f32[2,45,928]{2,1,0:T(8,128)S(1)}, u32[]{:S(2)}, u32[]{:S(2)}) collective-permute-start(f32[2,45,928]{2,1,0:T(8,128)S(1)} %get-tuple-element.48), channel_id=1, source_target_pairs={{0,32},{32,64},{64,96},{96,128},{128,160},{160,192},{192,224},{224... | collective-permute-start | bytes 1002248 | tf_op jit(solution)/shard_map/ppermute | solution.py:23
  40.3 9.1 %collective-permute-start.3 = (f32[2,45,928]{2,1,0:T(8,128)S(1)}, f32[2,45,928]{2,1,0:T(8,128)S(1)}, u32[]{:S(2)}, u32[]{:S(2)}) collective-permute-start(f32[2,45,928]{2,1,0:T(8,128)S(1)} %get-tuple-element.49), channel_id=1, source_target_pairs={{32,0},{64,32},{96,64},{128,96},{160,128},{192,160},{224,192},{256... | collective-permute-start | bytes 1002248 | tf_op jit(solution)/shard_map/ppermute | solution.py:25
  84.2 4.3 %copy-start.4 = (f32[4,45,864]{2,1,0:T(8,128)S(1)}, f32[4,45,864]{2,1,0:T(8,128)}, u32[]{:S(2)}) copy-start(f32[4,45,864]{2,1,0:T(8,128)} %get-tuple-element.5) | copy-start | bytes 1866244
  90.2 117.3 %copy-start.6 = (f32[4,45,864]{2,1,0:T(8,128)S(1)}, f32[4,45,864]{2,1,0:T(8,128)}, u32[]{:S(2)}) copy-start(f32[4,45,864]{2,1,0:T(8,128)} %get-tuple-element.10) | copy-start | bytes 1866244
  90.2 115.1 %collective-permute-start.4 = (f32[2,45,864]{2,1,0:T(8,128)S(1)}, f32[2,45,864]{2,1,0:T(8,128)S(1)}, u32[]{:S(2)}, u32[]{:S(2)}) collective-permute-start(f32[2,45,864]{2,1,0:T(8,128)S(1)} %slice.234), channel_id=1, source_target_pairs={{0,32},{32,64},{64,96},{96,128},{128,160},{160,192},{192,224},{224... | collective-permute-start | bytes 933128 | tf_op jit(solution)/shard_map/ppermute | solution.py:23
  205.4 8.6 %collective-permute-start.5 = (f32[2,45,864]{2,1,0:T(8,128)S(1)}, f32[2,45,864]{2,1,0:T(8,128)S(1)}, u32[]{:S(2)}, u32[]{:S(2)}) collective-permute-start(f32[2,45,864]{2,1,0:T(8,128)S(1)} %get-tuple-element.41), channel_id=1, source_target_pairs={{32,0},{64,32},{96,64},{128,96},{160,128},{192,160},{224,192},{256... | collective-permute-start | bytes 933128 | tf_op jit(solution)/shard_map/ppermute | solution.py:25
  208.5 5.6 %copy-start.1 = (f32[3,4,46,864]{3,2,1,0:T(8,128)S(1)}, f32[3,4,46,864]{3,2,1,0:T(8,128)}, u32[]{:S(2)}) copy-start(f32[3,4,46,864]{3,2,1,0:T(8,128)} %copy-done) | copy-start | bytes 5723140
  214.4 9.3 %collective-permute-start.6 = (f32[4,2,864]{2,1,0:T(2,128)S(1)}, f32[4,2,864]{2,1,0:T(2,128)S(1)}, u32[]{:S(2)}, u32[]{:S(2)}) collective-permute-start(f32[4,2,864]{2,1,0:T(2,128)S(1)} %get-tuple-element.34), channel_id=1, source_target_pairs={{0,1},{1,2},{2,3},{3,4},{4,5},{5,6},{6,7},{7,8},{8,9},{9,10},{10,1... | collective-permute-start | bytes 82952 | tf_op jit(solution)/shard_map/ppermute | solution.py:23
  217.7 6.6 %collective-permute-start.7 = (f32[4,2,864]{2,1,0:T(2,128)S(1)}, f32[4,2,864]{2,1,0:T(2,128)S(1)}, u32[]{:S(2)}, u32[]{:S(2)}) collective-permute-start(f32[4,2,864]{2,1,0:T(2,128)S(1)} %get-tuple-element.35), channel_id=1, source_target_pairs={{1,0},{2,1},{3,2},{4,3},{5,4},{6,5},{7,6},{8,7},{9,8},{10,9},{11,1... | collective-permute-start | bytes 82952 | tf_op jit(solution)/shard_map/ppermute | solution.py:25
where the time goes:
time: 226 us
  waiting for transfers between devices  125 us (55%)
  starting transfers between devices  34.6 us (15%)
  Pallas kernels  32 us (14%)
  other arithmetic  16.1 us (7%)
  local copies, waits for them, and re-layouts  14.2 us (6%)
  matrix products  2.3 us (1%)
    ppermute x4, waiting for transfers between devices, with_halo(): lax.ppermute(tail, axis, [(i, (i + 1) % count) for i in range(ends)])  115 us
    pallas_call x1, Pallas kernels, chemistry_step(): pl.pallas_call(chem_kernel, grid=(rows,), in_specs=[big, small, big, pl.B...  23.7 us
    ppermute x4, starting transfers between devices, with_halo(): lax.ppermute(head, axis, [((i + 1) % count, i) for i in range(ends)])  21.7 us
    ppermute x4, starting transfers between devices, with_halo(): lax.ppermute(tail, axis, [(i, (i + 1) % count) for i in range(ends)])  12.8 us
    ppermute x4, waiting for transfers between devices, with_halo(): lax.ppermute(head, axis, [((i + 1) % count, i) for i in range(ends)])  10.4 us
    pallas_call x2, Pallas kernels, polar_lowpass(): pl.pallas_call(polar_kernel, out_shape=jax.ShapeDtypeStruct(end_rows.shap...  8.36 us
    unnamed x37, local copies, waits for them, and re-layouts  6.56 us
    reshape x2, local copies, waits for them, and re-layouts, filter_field(): blocks = jnp.einsum('sjk,rR->srjRk', table, jnp.eye(polar_count, dtype=jn...  6.01 us
  transfers between devices with their start and end apart: 8, of which 5 were waited for; matrix products, arithmetic and copies ran while one was open for 8% of the time, Pallas kernels for 0%

commit v1 on v0

--- a/solution.py
+++ b/solution.py
@@ -170,6 +170,30 @@
     return jnp.where((keep_values <= KMAX)[:, None, None], lowpass, circles)
 
 
+def split_three(values):
+    high = values.astype(jnp.bfloat16)
+    rest = values - high.astype(jnp.float32)
+    middle = rest.astype(jnp.bfloat16)
+    low = (rest - middle.astype(jnp.float32)).astype(jnp.bfloat16)
+    return high, middle, low
+
+
+def select_dot(values, selector, dims):
+    total = None
+    for piece in split_three(values):
+        term = lax.dot_general(piece, selector, dims, preferred_element_type=jnp.float32)
+        total = term if total is None else total + term
+    return total
+
+
+def select_dot_left(selector, values, dims):
+    total = None
+    for piece in split_three(values):
+        term = lax.dot_general(selector, piece, dims, preferred_element_type=jnp.float32)
+        total = term if total is None else total + term
+    return total
+
+
 def polar_kernel(x_ref, w_ref, t_ref, y_ref, out_go, land_go, out_back, land_back,
                  sem_a, sem_b, sem_c, sem_d):
     count = t_ref.shape[0]
@@ -212,9 +236,8 @@
         slot = lax.broadcasted_iota(jnp.int32, (count * padded, channels), 0)
         channel = lax.broadcasted_iota(jnp.int32, (count * padded, channels), 1)
         target = (channel // chunk) * padded + channel % chunk
-        packer = jnp.where(slot == target, 1.0, 0.0).astype(jnp.float32)
-        packed = lax.dot_general(packer, rows, (((1,), (1,)), ((), ())), precision=hi,
-                                 preferred_element_type=jnp.float32)
+        packer = jnp.where(slot == target, 1.0, 0.0).astype(jnp.bfloat16)
+        packed = select_dot_left(packer, rows, (((1,), (1,)), ((), ())))
         out_go[...] = packed.reshape(count, padded, polar_count * col_count)
         round_trip(out_go, land_go, sem_a, sem_b)
 
@@ -235,8 +258,7 @@
         lax.fori_loop(0, count, synthesise, 0)
         round_trip(out_back, land_back, sem_c, sem_d)
         back = land_back[...].reshape(count * padded, polar_count * col_count)
-        result = lax.dot_general(back, packer, (((0,), (0,)), ((), ())), precision=hi,
-                                 preferred_element_type=jnp.float32)
+        result = select_dot(back, packer, (((0,), (0,)), ((), ())))
         for r in range(polar_count):
             y_ref[r] = result[r * col_count : (r + 1) * col_count]
 
@@ -304,14 +326,16 @@
     seed = seed_ref[0]
     cot = cot_ref[0]
     sat = sat_ref[...]
-    spread_m = spread_ref[...]
-    group_m = group_ref[...]
+    spread_m = spread_ref[...].astype(jnp.bfloat16)
+    group_m = group_ref[...].astype(jnp.bfloat16)
+
+    plain = (((1,), (0,)), ((), ()))
 
     def up(v):
-        return jnp.dot(v, spread_m, precision=hi, preferred_element_type=jnp.float32)
+        return select_dot(v, spread_m, plain)
 
     def down(v):
-        return jnp.dot(v, group_m, precision=hi, preferred_element_type=jnp.float32)
+        return select_dot(v, group_m, plain)
 
     root = jnp.sqrt(x * x + 1.0)
     mass = 0.5 * (x + root)

time: 226 us -> 214 us (0.947)
  Pallas kernels: 32 us -> 25 us
  waiting for transfers between devices: 125 us -> 120 us
    pallas_call x1, Pallas kernels: 23.7 us -> 16.7 us  [chemistry_step(): pl.pallas_call(chem_kernel, grid=(rows,), in_specs=[big, small, big, pl.B...]
    ppermute x4, waiting for transfers between devices: 115 us -> 109 us  [with_halo(): lax.ppermute(tail, axis, [(i, (i + 1) % count) for i in range(ends)])]
where the time goes in v1:
time: 214 us; the launch traced here: 213 us
  waiting for transfers between devices  120 us (56%)
  starting transfers between devices  34.6 us (16%)
  Pallas kernels  25 us (12%)
  other arithmetic  16.1 us (8%)
  local copies, waits for them, and re-layouts  14.2 us (7%)
  matrix products  2.3 us (1%)
    ppermute x4, waiting for transfers between devices, with_halo(): lax.ppermute(tail, axis, [(i, (i + 1) % count) for i in range(ends)])  109 us
    ppermute x4, starting transfers between devices, with_halo(): lax.ppermute(head, axis, [((i + 1) % count, i) for i in range(ends)])  21.7 us
    pallas_call x1, Pallas kernels, chemistry_step(): pl.pallas_call(chem_kernel, grid=(rows,), in_specs=[big, small, big, pl.B...  16.7 us
    ppermute x4, starting transfers between devices, with_halo(): lax.ppermute(tail, axis, [(i, (i + 1) % count) for i in range(ends)])  12.8 us
    ppermute x4, waiting for transfers between devices, with_halo(): lax.ppermute(head, axis, [((i + 1) % count, i) for i in range(ends)])  10.4 us
    pallas_call x2, Pallas kernels, polar_lowpass(): pl.pallas_call(polar_kernel, out_shape=jax.ShapeDtypeStruct(end_rows.shap...  8.36 us
    unnamed x37, local copies, waits for them, and re-layouts  6.56 us
    reshape x2, local copies, waits for them, and re-layouts, filter_field(): blocks = jnp.einsum('sjk,rR->srjRk', table, jnp.eye(polar_count, dtype=jn...  6.01 us
  transfers between devices with their start and end apart: 8, of which 5 were waited for; matrix products, arithmetic and copies ran while one was open for 8% of the time, Pallas kernels for 0%

profile of v1, /device:TPU:1, one launch (start us, length us, event | category | flops | bytes accessed | tf_op | source)
XLA Modules:
  0.0 213.1 jit_solution(8550102339223042766)
XLA Ops:
  0.6 1.2 copy.47
  2.2 4.4 %collective-permute-start = (f32[4,2,928]{2,1,0:T(2,128)S(1)}, f32[4,2,928]{2,1,0:T(2,128)S(1)}, u32[]{:S(2)}, u32[]{:S(2)}) collective-permute-start(f32[4,2,928]{2,1,0:T(2,128)S(1)} %get-tuple-element.46), channel_id=1, source_target_pairs={{0,1},{1,2},{2,3},{3,4},{4,5},{5,6},{6,7},{7,8},{8,9},{9,10},{10,1... | collective-permute-start | bytes 89096 | tf_op jit(solution)/shard_map/ppermute | solution.py:23
  6.6 12.1 %collective-permute-start.1 = (f32[4,2,928]{2,1,0:T(2,128)S(1)}, f32[4,2,928]{2,1,0:T(2,128)S(1)}, u32[]{:S(2)}, u32[]{:S(2)}) collective-permute-start(f32[4,2,928]{2,1,0:T(2,128)S(1)} %get-tuple-element.47), channel_id=1, source_target_pairs={{1,0},{2,1},{3,2},{4,3},{5,4},{6,5},{7,6},{8,7},{9,8},{10,9},{11,1... | collective-permute-start | bytes 89096 | tf_op jit(solution)/shard_map/ppermute | solution.py:25
  18.8 3.1 %fusion.11 = (f32[32,45,32]{2,0,1:T(8,128)S(1)}, f32[32,45,32]{2,0,1:T(8,128)S(1)}) fusion(s32[32,45]{0,1:T(8,128)S(1)} %multiply_add_fusion), kind=kLoop, calls=%fused_computation.29 | loop fusion | flops 414720 | bytes 374400 | tf_op jit(solution)/shard_map/cos | solution.py:154
  21.9 0.7 fusion.46.spread_ref
  22.6 0.3 pad_maximum_fusion.3
  22.9 1.5 multiply_bitcast_fusion
  24.8 0.6 select_n.193.w_ref
  25.3 2.6 %reshape.104 = f32[32,90,128]{2,0,1:T(8,128)} reshape(f32[32,2,45,2,64]{4,3,0,2,1:T(2,128)S(1)} %multiply_bitcast_fusion) | data formatting | bytes 2949120 | tf_op jit(solution)/shard_map/reshape | solution.py:312
  27.9 3.4 %copy.52.t_ref = f32[32,90,128]{2,1,0:T(8,128)} copy(f32[32,90,128]{2,0,1:T(8,128)} %reshape.104) | data formatting | bytes 2949120 | tf_op jit(solution)/shard_map/reshape | solution.py:312
  31.4 0.9 copy.54.cot_ref
  32.3 0.7 copy.53.seed_ref
  33.0 0.7 broadcast_in_dim_tile.3.sat_ref
  34.0 1.1 fusion.25
  35.0 0.2 maximum_maximum_fusion.1
  35.3 0.2 fusion.15
  35.6 0.8 copy-done
  36.4 0.5 copy-done.5
  37.2 3.2 %collective-permute-start.2 = (f32[2,45,928]{2,1,0:T(8,128)S(1)}, f32[2,45,928]{2,1,0:T(8,128)S(1)}, u32[]{:S(2)}, u32[]{:S(2)}) collective-permute-start(f32[2,45,928]{2,1,0:T(8,128)S(1)} %get-tuple-element.48), channel_id=1, source_target_pairs={{0,32},{32,64},{64,96},{96,128},{128,160},{160,192},{192,224},{224... | collective-permute-start | bytes 1002248 | tf_op jit(solution)/shard_map/ppermute | solution.py:23
  40.3 1.9 collective-permute-start.3
  42.3 0.9 fusion.21.group_ref
  43.2 1.8 collective-permute-done.2
  45.0 4.4 %collective-permute-done.3 = f32[2,45,928]{2,1,0:T(8,128)S(1)} collective-permute-done((f32[2,45,928]{2,1,0:T(8,128)S(1)}, f32[2,45,928]{2,1,0:T(8,128)S(1)}, u32[]{:S(2)}, u32[]{:S(2)}) %collective-permute-start.3) | collective-permute-done | bytes 334112 | tf_op jit(solution)/shard_map/ppermute | solution.py:25
  49.4 0.2 select_bitcast_fusion
  49.7 1.3 fusion.23
  50.9 0.3 maximum_maximum_fusion
  51.3 0.4 fusion
  51.7 0.8 slice_select_fusion.1.x_ref
  52.5 4.1 %shard_map.104 = f32[2,45,864]{2,1,0:T(8,128)} custom-call(f32[2,45,864]{2,1,0:T(8,128)} %slice_select_fusion.1.x_ref, f32[1,128]{1,0:T(1,128)} %select_n.193.w_ref, f32[32,90,128]{2,1,0:T(8,128)} %copy.52.t_ref), custom_call_target="tpu_custom_call" | custom-call | tf_op jit(solution)/shard_map/pallas_call | solution.py:276
  56.6 1.1 slice_select_fusion.2
  57.8 0.9 pad_maximum_fusion.4.x_ref
  58.7 16.7 %shard_map.105 = (f32[4,45,864]{2,1,0:T(8,128)}, f32[4,45,864]{2,1,0:T(8,128)}) custom-call(f32[4,45,864]{2,1,0:T(8,128)} %pad_maximum_fusion.4.x_ref, f32[4,45,32]{2,1,0:T(8,128)} %copy.53.seed_ref, f32[4,45,864]{2,1,0:T(8,128)} %copy.54.cot_ref, f32[1,864]{1,0:T(1,128)} %broadcast_in_dim_tile.3.sat_ref, f32[32,864]{1,0:T(8,128)} %fusion.46.spread_ref, ...), custom_call_target="tpu_custom_call" | custom-call | tf_op jit(solution)/shard_map/pallas_call | solution.py:379
  75.3 1.8 slice_select_fusion.4.x_ref
  77.2 4.2 %shard_map.106 = f32[2,45,864]{2,1,0:T(8,128)} custom-call(f32[2,45,864]{2,1,0:T(8,128)} %slice_select_fusion.4.x_ref, f32[1,128]{1,0:T(1,128)} %select_n.193.w_ref, f32[32,90,128]{2,1,0:T(8,128)} %copy.52.t_ref), custom_call_target="tpu_custom_call" | custom-call | tf_op jit(solution)/shard_map/pallas_call | solution.py:276
  81.4 1.1 slice_select_fusion.5
  82.6 0.3 fusion.5
  82.9 0.2 pad_add_fusion
  83.2 2.1 collective-permute-start.4
  85.3 107.5 %collective-permute-done.4 = f32[2,45,864]{2,1,0:T(8,128)S(1)} collective-permute-done((f32[2,45,864]{2,1,0:T(8,128)S(1)}, f32[2,45,864]{2,1,0:T(8,128)S(1)}, u32[]{:S(2)}, u32[]{:S(2)}) %collective-permute-start.4) | collective-permute-done | bytes 311072 | tf_op jit(solution)/shard_map/ppermute | solution.py:23
  192.9 2.0 collective-permute-start.5
  194.9 1.1 copy.56
  196.0 5.4 %collective-permute-done.5 = f32[2,45,864]{2,1,0:T(8,128)S(1)} collective-permute-done((f32[2,45,864]{2,1,0:T(8,128)S(1)}, f32[2,45,864]{2,1,0:T(8,128)S(1)}, u32[]{:S(2)}, u32[]{:S(2)}) %collective-permute-start.5) | collective-permute-done | bytes 311072 | tf_op jit(solution)/shard_map/ppermute | solution.py:25
  201.6 0.2 fusion.20
  201.9 3.3 %collective-permute-start.6 = (f32[4,2,864]{2,1,0:T(2,128)S(1)}, f32[4,2,864]{2,1,0:T(2,128)S(1)}, u32[]{:S(2)}, u32[]{:S(2)}) collective-permute-start(f32[4,2,864]{2,1,0:T(2,128)S(1)} %get-tuple-element.34), channel_id=1, source_target_pairs={{0,1},{1,2},{2,3},{3,4},{4,5},{5,6},{6,7},{7,8},{8,9},{9,10},{10,1... | collective-permute-start | bytes 82952 | tf_op jit(solution)/shard_map/ppermute | solution.py:23
  205.2 5.6 %collective-permute-start.7 = (f32[4,2,864]{2,1,0:T(2,128)S(1)}, f32[4,2,864]{2,1,0:T(2,128)S(1)}, u32[]{:S(2)}, u32[]{:S(2)}) collective-permute-start(f32[4,2,864]{2,1,0:T(2,128)S(1)} %get-tuple-element.35), channel_id=1, source_target_pairs={{1,0},{2,1},{3,2},{4,3},{5,4},{6,5},{7,6},{8,7},{9,8},{10,9},{11,1... | collective-permute-start | bytes 82952 | tf_op jit(solution)/shard_map/ppermute | solution.py:25
  210.8 0.3 pad_add_fusion.2
  211.2 0.5 collective-permute-done.7
  212.0 1.1 copy.57
  (65 shorter events, 2.1 us)
Async XLA Ops:
  0.6 1.2 copy-start.8
  0.6 1.3 copy-start.9
  1.8 20.1 %copy-start.2 = (f32[4,45,864]{2,1,0:T(8,128)}, f32[4,45,864]{2,1,0:T(8,128)S(1)}, u32[]{:S(2)}) copy-start(f32[4,45,864]{2,1,0:T(8,128)S(1)} %copy.47) | copy-start | bytes 1866244
  2.0 20.6 %copy-start.13 = (s32[4]{0:T(128)S(1)}, s32[4]{0:T(128)}, u32[]{:S(2)}) copy-start(s32[4]{0:T(128)} %param.14) | copy-start | bytes 52
  2.2 31.5 %collective-permute-start = (f32[4,2,928]{2,1,0:T(2,128)S(1)}, f32[4,2,928]{2,1,0:T(2,128)S(1)}, u32[]{:S(2)}, u32[]{:S(2)}) collective-permute-start(f32[4,2,928]{2,1,0:T(2,128)S(1)} %get-tuple-element.46), channel_id=1, source_target_pairs={{0,1},{1,2},{2,3},{3,4},{4,5},{5,6},{6,7},{7,8},{8,9},{9,10},{10,1... | collective-permute-start | bytes 89096 | tf_op jit(solution)/shard_map/ppermute | solution.py:23
  6.6 27.1 %collective-permute-start.1 = (f32[4,2,928]{2,1,0:T(2,128)S(1)}, f32[4,2,928]{2,1,0:T(2,128)S(1)}, u32[]{:S(2)}, u32[]{:S(2)}) collective-permute-start(f32[4,2,928]{2,1,0:T(2,128)S(1)} %get-tuple-element.47), channel_id=1, source_target_pairs={{1,0},{2,1},{3,2},{4,3},{5,4},{6,5},{7,6},{8,7},{9,8},{10,9},{11,1... | collective-permute-start | bytes 89096 | tf_op jit(solution)/shard_map/ppermute | solution.py:25
  22.9 1.6 copy-start.10
  22.9 1.7 copy-start.11
  27.9 3.4 %copy-start.7 = (f32[4,45,864]{2,0,1:T(4,128)S(1)}, f32[4,45,864]{2,0,1:T(4,128)}, u32[]{:S(2)}) copy-start(f32[4,45,864]{2,0,1:T(4,128)} %param.17) | copy-start | bytes 1866244
  31.3 0.9 copy-start.12
  31.3 1.7 copy-start.14
  31.3 2.4 %copy-start.3 = (f32[4,45,864]{2,1,0:T(8,128)S(1)}, f32[4,45,864]{2,1,0:T(8,128)}, u32[]{:S(2)}) copy-start(f32[4,45,864]{2,1,0:T(8,128)} %copy-done.2) | copy-start | bytes 1866244
  35.0 1.3 copy-start
  35.3 1.6 copy-start.5
  37.2 7.9 %collective-permute-start.2 = (f32[2,45,928]{2,1,0:T(8,128)S(1)}, f32[2,45,928]{2,1,0:T(8,128)S(1)}, u32[]{:S(2)}, u32[]{:S(2)}) collective-permute-start(f32[2,45,928]{2,1,0:T(8,128)S(1)} %get-tuple-element.48), channel_id=1, source_target_pairs={{0,32},{32,64},{64,96},{96,128},{128,160},{160,192},{192,224},{224... | collective-permute-start | bytes 1002248 | tf_op jit(solution)/shard_map/ppermute | solution.py:23
  40.3 9.1 %collective-permute-start.3 = (f32[2,45,928]{2,1,0:T(8,128)S(1)}, f32[2,45,928]{2,1,0:T(8,128)S(1)}, u32[]{:S(2)}, u32[]{:S(2)}) collective-permute-start(f32[2,45,928]{2,1,0:T(8,128)S(1)} %get-tuple-element.49), channel_id=1, source_target_pairs={{32,0},{64,32},{96,64},{128,96},{160,128},{192,160},{224,192},{256... | collective-permute-start | bytes 1002248 | tf_op jit(solution)/shard_map/ppermute | solution.py:25
  77.2 4.3 %copy-start.4 = (f32[4,45,864]{2,1,0:T(8,128)S(1)}, f32[4,45,864]{2,1,0:T(8,128)}, u32[]{:S(2)}) copy-start(f32[4,45,864]{2,1,0:T(8,128)} %get-tuple-element.5) | copy-start | bytes 1866244
  83.2 111.8 %copy-start.6 = (f32[4,45,864]{2,1,0:T(8,128)S(1)}, f32[4,45,864]{2,1,0:T(8,128)}, u32[]{:S(2)}) copy-start(f32[4,45,864]{2,1,0:T(8,128)} %get-tuple-element.10) | copy-start | bytes 1866244
  83.2 109.6 %collective-permute-start.4 = (f32[2,45,864]{2,1,0:T(8,128)S(1)}, f32[2,45,864]{2,1,0:T(8,128)S(1)}, u32[]{:S(2)}, u32[]{:S(2)}) collective-permute-start(f32[2,45,864]{2,1,0:T(8,128)S(1)} %slice.234), channel_id=1, source_target_pairs={{0,32},{32,64},{64,96},{96,128},{128,160},{160,192},{192,224},{224... | collective-permute-start | bytes 933128 | tf_op jit(solution)/shard_map/ppermute | solution.py:23
  192.9 8.6 %collective-permute-start.5 = (f32[2,45,864]{2,1,0:T(8,128)S(1)}, f32[2,45,864]{2,1,0:T(8,128)S(1)}, u32[]{:S(2)}, u32[]{:S(2)}) collective-permute-start(f32[2,45,864]{2,1,0:T(8,128)S(1)} %get-tuple-element.41), channel_id=1, source_target_pairs={{32,0},{64,32},{96,64},{128,96},{160,128},{192,160},{224,192},{256... | collective-permute-start | bytes 933128 | tf_op jit(solution)/shard_map/ppermute | solution.py:25
  196.0 5.6 %copy-start.1 = (f32[3,4,46,864]{3,2,1,0:T(8,128)S(1)}, f32[3,4,46,864]{3,2,1,0:T(8,128)}, u32[]{:S(2)}) copy-start(f32[3,4,46,864]{3,2,1,0:T(8,128)} %copy-done) | copy-start | bytes 5723140
  201.9 9.3 %collective-permute-start.6 = (f32[4,2,864]{2,1,0:T(2,128)S(1)}, f32[4,2,864]{2,1,0:T(2,128)S(1)}, u32[]{:S(2)}, u32[]{:S(2)}) collective-permute-start(f32[4,2,864]{2,1,0:T(2,128)S(1)} %get-tuple-element.34), channel_id=1, source_target_pairs={{0,1},{1,2},{2,3},{3,4},{4,5},{5,6},{6,7},{7,8},{8,9},{9,10},{10,1... | collective-permute-start | bytes 82952 | tf_op jit(solution)/shard_map/ppermute | solution.py:23
  205.2 6.6 %collective-permute-start.7 = (f32[4,2,864]{2,1,0:T(2,128)S(1)}, f32[4,2,864]{2,1,0:T(2,128)S(1)}, u32[]{:S(2)}, u32[]{:S(2)}) collective-permute-start(f32[4,2,864]{2,1,0:T(2,128)S(1)} %get-tuple-element.35), channel_id=1, source_target_pairs={{1,0},{2,1},{3,2},{4,3},{5,4},{6,5},{7,6},{8,7},{9,8},{10,9},{11,1... | collective-permute-start | bytes 82952 | tf_op jit(solution)/shard_map/ppermute | solution.py:25

commit v2 on v1

--- a/solution.py
+++ b/solution.py
@@ -290,6 +290,202 @@
         ],
         compiler_params=pltpu.CompilerParams(collective_id=call_id, has_side_effects=True),
     )(end_rows, weights, blocks)
+
+
+def column_chemistry(x, seed, cot, sat, valid):
+    root = jnp.sqrt(x * x + 1.0)
+    mass = jnp.where(valid, 0.5 * (x + root), 0.0)
+    cot = jnp.where(valid, cot, 0.0)
+    aerosol = seed
+    history = []
+    for newton_step in range(NEWTON):
+        denominator = aerosol + sat
+        fraction = mass / denominator
+        first_sum = jnp.sum(fraction, axis=0, keepdims=True)
+        second_sum = jnp.sum(fraction / denominator, axis=0, keepdims=True)
+        residue = 1.0 - seed / aerosol - first_sum
+        derivative = seed / (aerosol * aerosol) + second_sum
+        history.append((aerosol, residue, derivative))
+        aerosol = aerosol - residue / derivative
+    final_den = aerosol + sat
+    particle = mass * aerosol / final_den
+    mass_bar = cot * aerosol / final_den
+    aerosol_bar = jnp.sum(cot * mass * sat / (final_den * final_den), axis=0, keepdims=True)
+    for newton_step in reversed(range(NEWTON)):
+        a_n, residue, derivative = history[newton_step]
+        inverse = 1.0 / (a_n + sat)
+        third_sum = jnp.sum(mass * inverse * inverse * inverse, axis=0, keepdims=True)
+        slope = -2.0 * (seed / (a_n * a_n * a_n) + third_sum)
+        over_g = aerosol_bar / derivative
+        over_g2 = over_g * residue / derivative
+        mass_bar = mass_bar + over_g * inverse + over_g2 * inverse * inverse
+        aerosol_bar = over_g2 * slope
+    gradient = mass_bar * 0.5 * (1.0 + x / root)
+    return jnp.where(valid, particle, 0.0), jnp.where(valid, gradient, 0.0)
+
+
+def owner_kernel(x_ref, c_ref, s_ref, w_ref, m_ref, v_ref, t_ref, p_ref, g_ref,
+                 out_go, land_go, out_back, land_back, field_s, sem_a, sem_b, sem_c, sem_d):
+    count = t_ref.shape[0]
+    polar_count, col_count, channels = x_ref.shape
+    levels = s_ref.shape[2]
+    chunk = channels // count
+    padded = out_go.shape[1] // 2
+    me = lax.axis_index("lon")
+    band = lax.axis_index("lat")
+    bands = lax.axis_size("lat")
+    active = jnp.logical_or(band == 0, band == bands - 1)
+    hi = lax.Precision.HIGHEST
+    mesh_id = pl.DeviceIdType.MESH
+    nt = (((1,), (1,)), ((), ()))
+
+    def remote(src, dst, send_sem, recv_sem, peer):
+        return pltpu.make_async_remote_copy(
+            src_ref=src, dst_ref=dst, send_sem=send_sem, recv_sem=recv_sem,
+            device_id=(band, peer), device_id_type=mesh_id,
+        )
+
+    def round_trip(outbox, inbox, send_sems, recv_sems):
+        for offset in range(1, count):
+            peer = lax.rem(me + offset, count)
+            remote(outbox.at[peer], inbox.at[me], send_sems.at[offset], recv_sems.at[me], peer).start()
+        inbox[pl.ds(me, 1)] = outbox[pl.ds(me, 1)]
+        for offset in range(1, count):
+            peer = lax.rem(me + offset, count)
+            remote(outbox.at[peer], inbox.at[me], send_sems.at[offset], recv_sems.at[me], peer).wait_send()
+        for offset in range(1, count):
+            peer = lax.rem(me + count - offset, count)
+            remote(outbox.at[peer], inbox.at[peer], send_sems.at[offset], recv_sems.at[peer], peer).wait_recv()
+
+    @pl.when(active)
+    def _():
+        barrier = pltpu.get_barrier_semaphore()
+        for offset in range(1, count):
+            peer = lax.rem(me + offset, count)
+            pl.semaphore_signal(barrier, 1, device_id=(band, peer), device_id_type=mesh_id)
+        pl.semaphore_wait(barrier, count - 1)
+        wide = channels + levels
+        slot = lax.broadcasted_iota(jnp.int32, (count * padded, wide), 0)
+        channel = lax.broadcasted_iota(jnp.int32, (count * padded, wide), 1)
+        target = jnp.where(
+            channel < channels,
+            (channel // chunk) * padded + channel % chunk,
+            (channel - channels) * padded + chunk,
+        )
+        packer_wide = jnp.where(slot == target, 1.0, 0.0).astype(jnp.bfloat16)
+        packer = packer_wide[:, :channels]
+        rows = jnp.concatenate(
+            [jnp.concatenate([x_ref[r], s_ref[r]], axis=1) for r in range(polar_count)], axis=0
+        )
+        cots = jnp.concatenate([c_ref[r] for r in range(polar_count)], axis=0)
+        lanes = polar_count * col_count
+        out_go[:, 0:padded, :] = select_dot_left(packer_wide, rows, nt).reshape(count, padded, lanes)
+        out_go[:, padded:, :] = select_dot_left(packer, cots, nt).reshape(count, padded, lanes)
+        round_trip(out_go, land_go, sem_a, sem_b)
+
+        def analyse(s, acc):
+            return acc + jnp.dot(land_go[s, 0:padded, :], t_ref[s], precision=hi,
+                                 preferred_element_type=jnp.float32)
+
+        zero = jnp.zeros((padded, t_ref.shape[2]), jnp.float32)
+        coefficient = lax.fori_loop(0, count, analyse, zero) * w_ref[...]
+        keep_lane = m_ref[...] > 0.5
+        species_row = lax.broadcasted_iota(jnp.int32, (padded, lanes), 0)
+        valid = species_row < chunk
+        sat = v_ref[...]
+
+        def chemistry(s, acc):
+            values = land_go[s, 0:padded, :]
+            smooth = lax.dot_general(coefficient, t_ref[s], nt, precision=hi,
+                                     preferred_element_type=jnp.float32)
+            smooth = jnp.where(keep_lane, smooth, values)
+            seed = land_go[s, pl.ds(chunk, 1), :]
+            particle, gradient = column_chemistry(
+                smooth, seed, land_go[s, padded:, :], sat, valid
+            )
+            out_back[s, 0:padded, :] = particle
+            field_s[s] = gradient
+            return acc + jnp.dot(gradient, t_ref[s], precision=hi,
+                                 preferred_element_type=jnp.float32)
+
+        adjoint_coef = lax.fori_loop(0, count, chemistry, zero) * w_ref[...]
+
+        def synthesise(s, carry):
+            smooth = lax.dot_general(adjoint_coef, t_ref[s], nt, precision=hi,
+                                     preferred_element_type=jnp.float32)
+            out_back[s, padded:, :] = jnp.where(keep_lane, smooth, field_s[s])
+            return carry
+
+        lax.fori_loop(0, count, synthesise, 0)
+        round_trip(out_back, land_back, sem_c, sem_d)
+        particle_back = land_back[:, 0:padded, :].reshape(count * padded, lanes)
+        gradient_back = land_back[:, padded:, :].reshape(count * padded, lanes)
+        particle_rows = select_dot(particle_back, packer, (((0,), (0,)), ((), ())))
+        gradient_rows = select_dot(gradient_back, packer, (((0,), (0,)), ((), ())))
+        for r in range(polar_count):
+            p_ref[r] = particle_rows[r * col_count : (r + 1) * col_count]
+            g_ref[r] = gradient_rows[r * col_count : (r + 1) * col_count]
+
+    @pl.when(jnp.logical_not(active))
+    def _():
+        p_ref[...] = jnp.zeros_like(p_ref)
+        g_ref[...] = jnp.zeros_like(g_ref)
+
+
+def polar_step(field, seed_aerosol, volatility, cotangent, filter_keep, particle, gradient):
+    row_count, col_count, channels = field.shape
+    count = lax.axis_size("lon")
+    length = col_count * count
+    species = volatility.shape[0]
+    polar_count = POLAR
+    band = lax.axis_index("lat")
+    at_north_end = band == 0
+    at_south_end = band == lax.axis_size("lat") - 1
+
+    def ends(values):
+        return jnp.where(at_north_end, values[:polar_count], values[row_count - polar_count :])
+
+    end_keep = ends(filter_keep)
+    table = wave_table(length, length).reshape(count, col_count, 2 * KMAX)
+    blocks = jnp.einsum(
+        "sjk,rR->srjRk", table, jnp.eye(polar_count, dtype=jnp.float32)
+    ).reshape(count, polar_count * col_count, polar_count * 2 * KMAX)
+    weights = wave_weights(end_keep, length).reshape(1, polar_count * 2 * KMAX)
+    lane_mask = jnp.repeat((end_keep <= KMAX).astype(jnp.float32), col_count)[None, :]
+    padded = -(-(channels // count + 1) // 8) * 8
+    sat = jnp.concatenate(
+        [volatility, jnp.ones((padded - species,), jnp.float32)]
+    )[:, None]
+    slab = (count, 2 * padded, polar_count * col_count)
+    vmem = pl.BlockSpec(memory_space=pltpu.VMEM)
+    end_shape = jax.ShapeDtypeStruct((polar_count, col_count, channels), jnp.float32)
+    polar_particle, polar_gradient = pl.pallas_call(
+        owner_kernel,
+        out_shape=[end_shape, end_shape],
+        in_specs=[vmem] * 7,
+        out_specs=[vmem, vmem],
+        scratch_shapes=[
+            pltpu.VMEM(slab, jnp.float32),
+            pltpu.VMEM(slab, jnp.float32),
+            pltpu.VMEM(slab, jnp.float32),
+            pltpu.VMEM(slab, jnp.float32),
+            pltpu.VMEM((count, padded, polar_count * col_count), jnp.float32),
+            pltpu.SemaphoreType.DMA((count,)),
+            pltpu.SemaphoreType.DMA((count,)),
+            pltpu.SemaphoreType.DMA((count,)),
+            pltpu.SemaphoreType.DMA((count,)),
+        ],
+        compiler_params=pltpu.CompilerParams(collective_id=0, has_side_effects=True),
+    )(ends(field), ends(cotangent), ends(seed_aerosol), weights, lane_mask, sat, blocks)
+
+    def merge(values, polar):
+        top = jnp.where(at_north_end, polar, values[:polar_count])
+        bottom = jnp.where(at_south_end, polar, values[row_count - polar_count :])
+        return jnp.concatenate(
+            [top, values[polar_count : row_count - polar_count], bottom], axis=0
+        )
+
+    return merge(particle, polar_particle), merge(gradient, polar_gradient)
 
 
 def filter_field(field, filter_keep, call_id):
@@ -431,10 +627,10 @@
         return meridional_window(window, north_speed, north_choice, first_row, species)
 
     after_north, north_back = jax.vjp(meridional_only, tall_window[:, :, :channels])
-    filtered = filter_field(after_north, filter_keep, 0)
-
-    particle, chem_grad = chemistry_step(filtered, seed_aerosol, volatility, cotangent)
-    adjoint_filtered = filter_field(chem_grad, filter_keep, 1)
+    particle, chem_grad = chemistry_step(after_north, seed_aerosol, volatility, cotangent)
+    particle, adjoint_filtered = polar_step(
+        after_north, seed_aerosol, volatility, cotangent, filter_keep, particle, chem_grad
+    )
     return (particle, fold_columns(east_back(fold_rows(north_back(adjoint_filtered)[0]))[0]))
 
 

time: 214 us -> 204 us (0.953)
  waiting for transfers between devices: 120 us -> 109 us
  local copies, waits for them, and re-layouts: 14.2 us -> 19.6 us
  Pallas kernels: 25 us -> 21.4 us
    ppermute x4, waiting for transfers between devices: 109 us -> 99.1 us  [with_halo(): lax.ppermute(tail, axis, [(i, (i + 1) % count) for i in range(ends)])]
    unnamed x37, local copies, waits for them, and re-layouts: 6.56 us -> 10.5 us
    pallas_call x2 -> x1, Pallas kernels: 8.36 us -> 4.76 us  [polar_step(): pl.pallas_call(owner_kernel, out_shape=[end_shape, end_shape], in_specs=[...]
  transfers between devices with their start and end apart: 8 -> 8, of which waited for: 5 -> 5; matrix products, arithmetic and copies ran while one was open for 8% -> 10% of each run, Pallas kernels for 0% -> 0%
where the time goes in v2:
time: 204 us; the launch traced here: 203 us
  waiting for transfers between devices  109 us (53%)
  starting transfers between devices  34.7 us (17%)
  Pallas kernels  21.4 us (10%)
  local copies, waits for them, and re-layouts  19.6 us (10%)
  other arithmetic  14.7 us (7%)
  matrix products  2.3 us (1%)
    ppermute x4, waiting for transfers between devices, with_halo(): lax.ppermute(tail, axis, [(i, (i + 1) % count) for i in range(ends)])  99.1 us
    ppermute x4, starting transfers between devices, with_halo(): lax.ppermute(head, axis, [((i + 1) % count, i) for i in range(ends)])  23.2 us
    pallas_call x1, Pallas kernels, chemistry_step(): pl.pallas_call(chem_kernel, grid=(rows,), in_specs=[big, small, big, pl.B...  16.7 us
    ppermute x4, starting transfers between devices, with_halo(): lax.ppermute(tail, axis, [(i, (i + 1) % count) for i in range(ends)])  11.5 us
    unnamed x37, local copies, waits for them, and re-layouts  10.5 us
    ppermute x4, waiting for transfers between devices, with_halo(): lax.ppermute(head, axis, [((i + 1) % count, i) for i in range(ends)])  10.2 us
    reshape x2, local copies, waits for them, and re-layouts, polar_step(): blocks = jnp.einsum('sjk,rR->srjRk', table, jnp.eye(polar_count, dtype=jn...  6.05 us
    pallas_call x1, Pallas kernels, polar_step(): pl.pallas_call(owner_kernel, out_shape=[end_shape, end_shape], in_specs=[...  4.76 us
  transfers between devices with their start and end apart: 8, of which 5 were waited for; matrix products, arithmetic and copies ran while one was open for 10% of the time, Pallas kernels for 0%

profile of v2, /device:TPU:1, one launch (start us, length us, event | category | flops | bytes accessed | tf_op | source)
XLA Modules:
  0.0 203.3 jit_solution(13719857557085943414)
XLA Ops:
  0.6 0.9 convert_element_type.30
  1.6 1.0 copy.51
  2.6 1.1 copy.56
  3.7 0.8 copy-done.2
  4.6 0.7 pad_maximum_fusion.19
  5.3 4.4 %collective-permute-start = (f32[4,2,928]{2,1,0:T(2,128)}, f32[4,2,928]{2,1,0:T(2,128)S(1)}, u32[]{:S(2)}, u32[]{:S(2)}) collective-permute-start(f32[4,2,928]{2,1,0:T(2,128)} %get-tuple-element.50), channel_id=1, source_target_pairs={{0,1},{1,2},{2,3},{3,4},{4,5},{5,6},{6,7},{7,8},{8,9},{9,10},{10,1... | collective-permute-start | bytes 89096 | tf_op jit(solution)/shard_map/ppermute | solution.py:23
  9.6 12.1 %collective-permute-start.1 = (f32[4,2,928]{2,1,0:T(2,128)S(1)}, f32[4,2,928]{2,1,0:T(2,128)S(1)}, u32[]{:S(2)}, u32[]{:S(2)}) collective-permute-start(f32[4,2,928]{2,1,0:T(2,128)S(1)} %get-tuple-element.51), channel_id=1, source_target_pairs={{1,0},{2,1},{3,2},{4,3},{5,4},{6,5},{7,6},{8,7},{9,8},{10,9},{11,1... | collective-permute-start | bytes 89096 | tf_op jit(solution)/shard_map/ppermute | solution.py:25
  22.1 0.6 slice_select_fusion.6.s_ref
  22.7 0.6 fusion.46.spread_ref
  23.3 3.1 %fusion.11 = (f32[32,45,32]{2,0,1:T(8,128)S(1)}, f32[32,45,32]{2,0,1:T(8,128)S(1)}) fusion(s32[32,45]{0,1:T(8,128)S(1)} %multiply_add_fusion), kind=kLoop, calls=%fused_computation.29 | loop fusion | flops 414720 | bytes 374400 | tf_op jit(solution)/shard_map/cos | solution.py:154
  26.4 0.3 pad_maximum_fusion.3
  26.7 1.5 multiply_bitcast_fusion
  28.4 0.6 select_n.189.w_ref
  29.0 0.7 broadcast_in_dim_reshape.3.m_ref
  29.7 0.7 copy.65.v_ref
  30.4 0.7 broadcast_in_dim_tile.3.sat_ref
  31.2 1.0 copy.57
  32.1 2.0 copy.61.cot_ref
  34.1 2.6 %reshape.100 = f32[32,90,128]{2,0,1:T(8,128)} reshape(f32[32,2,45,2,64]{4,3,0,2,1:T(2,128)S(1)} %multiply_bitcast_fusion) | data formatting | bytes 2949120 | tf_op jit(solution)/shard_map/reshape | solution.py:452
  36.7 3.5 %copy.66.t_ref = f32[32,90,128]{2,1,0:T(8,128)} copy(f32[32,90,128]{2,0,1:T(8,128)} %reshape.100) | data formatting | bytes 2949120 | tf_op jit(solution)/shard_map/reshape | solution.py:452
  40.5 1.1 fusion.25
  41.5 0.2 maximum_maximum_fusion.1
  42.1 0.8 copy-done
  42.9 0.5 copy-done.6
  43.6 3.1 %collective-permute-start.2 = (f32[2,45,928]{2,1,0:T(8,128)S(1)}, f32[2,45,928]{2,1,0:T(8,128)S(1)}, u32[]{:S(2)}, u32[]{:S(2)}) collective-permute-start(f32[2,45,928]{2,1,0:T(8,128)S(1)} %get-tuple-element.52), channel_id=1, source_target_pairs={{0,32},{32,64},{64,96},{96,128},{128,160},{160,192},{192,224},{224... | collective-permute-start | bytes 1002248 | tf_op jit(solution)/shard_map/ppermute | solution.py:23
  46.8 2.1 %collective-permute-start.3 = (f32[2,45,928]{2,1,0:T(8,128)S(1)}, f32[2,45,928]{2,1,0:T(8,128)S(1)}, u32[]{:S(2)}, u32[]{:S(2)}) collective-permute-start(f32[2,45,928]{2,1,0:T(8,128)S(1)} %get-tuple-element.53), channel_id=1, source_target_pairs={{32,0},{64,32},{96,64},{128,96},{160,128},{192,160},{224,192},{256... | collective-permute-start | bytes 1002248 | tf_op jit(solution)/shard_map/ppermute | solution.py:25
  48.9 0.9 fusion.21.group_ref
  49.9 1.6 collective-permute-done.2
  51.5 4.4 %collective-permute-done.3 = f32[2,45,928]{2,1,0:T(8,128)S(1)} collective-permute-done((f32[2,45,928]{2,1,0:T(8,128)S(1)}, f32[2,45,928]{2,1,0:T(8,128)S(1)}, u32[]{:S(2)}, u32[]{:S(2)}) %collective-permute-start.3) | collective-permute-done | bytes 334112 | tf_op jit(solution)/shard_map/ppermute | solution.py:25
  56.2 1.2 fusion.23
  57.4 0.3 maximum_maximum_fusion
  57.8 0.4 fusion
  58.2 1.0 copy-done.5
  59.2 1.1 slice_select_fusion
  60.3 16.7 %shard_map.105 = (f32[4,45,864]{2,1,0:T(8,128)}, f32[4,45,864]{2,1,0:T(8,128)}) custom-call(f32[4,45,864]{2,1,0:T(8,128)} %copy-done.4, f32[4,45,32]{2,1,0:T(8,128)} %copy-done.7, f32[4,45,864]{2,1,0:T(8,128)} %copy.61.cot_ref, f32[1,864]{1,0:T(1,128)} %broadcast_in_dim_tile.3.sat_ref, f32[32,864]{1,0:T(8,128)} %fusion.46.spread_ref, f32[864,32]{1,0:T(8,128)} %fusion.21.group_ref), custom_call_target="tpu_custom_call" | custom-call | tf_op jit(solution)/shard_map/pallas_call | solution.py:575
  77.0 4.8 %shard_map.104 = (f32[2,45,864]{2,1,0:T(8,128)}, f32[2,45,864]{2,1,0:T(8,128)}) custom-call(f32[2,45,864]{2,1,0:T(8,128)} %get-tuple-element.61.x_ref, f32[2,45,864]{2,1,0:T(8,128)} %get-tuple-element.60.c_ref, f32[2,45,32]{2,1,0:T(8,128)} %slice_select_fusion.6.s_ref, f32[1,128]{1,0:T(1,128)} %select_n.189.w_ref, f32[1,90]{1,0:T(1,128)} %broadcast_in_dim_reshape.3.m_ref, ...), custom_call_target="tpu_custom_call" | custom-call | tf_op jit(solution)/shard_map/pallas_call | solution.py:462
  81.8 1.0 slice_select_fusion.3
  82.9 0.3 fusion.5
  83.5 2.1 %collective-permute-start.4 = (f32[2,45,864]{2,1,0:T(8,128)S(1)}, f32[2,45,864]{2,1,0:T(8,128)S(1)}, u32[]{:S(2)}, u32[]{:S(2)}) collective-permute-start(f32[2,45,864]{2,1,0:T(8,128)S(1)} %slice.260), channel_id=1, source_target_pairs={{0,32},{32,64},{64,96},{96,128},{128,160},{160,192},{192,224},{224... | collective-permute-start | bytes 933128 | tf_op jit(solution)/shard_map/ppermute | solution.py:23
  85.6 97.4 %collective-permute-done.4 = f32[2,45,864]{2,1,0:T(8,128)S(1)} collective-permute-done((f32[2,45,864]{2,1,0:T(8,128)S(1)}, f32[2,45,864]{2,1,0:T(8,128)S(1)}, u32[]{:S(2)}, u32[]{:S(2)}) %collective-permute-start.4) | collective-permute-done | bytes 311072 | tf_op jit(solution)/shard_map/ppermute | solution.py:23
  183.1 2.0 %collective-permute-start.5 = (f32[2,45,864]{2,1,0:T(8,128)S(1)}, f32[2,45,864]{2,1,0:T(8,128)S(1)}, u32[]{:S(2)}, u32[]{:S(2)}) collective-permute-start(f32[2,45,864]{2,1,0:T(8,128)S(1)} %get-tuple-element.41), channel_id=1, source_target_pairs={{32,0},{64,32},{96,64},{128,96},{160,128},{192,160},{224,192},{256... | collective-permute-start | bytes 933128 | tf_op jit(solution)/shard_map/ppermute | solution.py:25
  185.3 1.1 copy.69
  186.4 5.3 %collective-permute-done.5 = f32[2,45,864]{2,1,0:T(8,128)S(1)} collective-permute-done((f32[2,45,864]{2,1,0:T(8,128)S(1)}, f32[2,45,864]{2,1,0:T(8,128)S(1)}, u32[]{:S(2)}, u32[]{:S(2)}) %collective-permute-start.5) | collective-permute-done | bytes 311072 | tf_op jit(solution)/shard_map/ppermute | solution.py:25
  192.1 1.9 collective-permute-start.6
  194.0 7.0 %collective-permute-start.7 = (f32[4,2,864]{2,1,0:T(2,128)S(1)}, f32[4,2,864]{2,1,0:T(2,128)S(1)}, u32[]{:S(2)}, u32[]{:S(2)}) collective-permute-start(f32[4,2,864]{2,1,0:T(2,128)S(1)} %get-tuple-element.39), channel_id=1, source_target_pairs={{1,0},{2,1},{3,2},{4,3},{5,4},{6,5},{7,6},{8,7},{9,8},{10,9},{11,1... | collective-permute-start | bytes 82952 | tf_op jit(solution)/shard_map/ppermute | solution.py:25
  201.0 0.3 pad_add_fusion.2
  201.4 0.5 collective-permute-done.7
  202.2 1.1 copy.70
  (68 shorter events, 3.0 us)
Async XLA Ops:
  0.6 21.2 %copy-start.11 = (f32[4,45,32]{1,2,0:T(8,128)S(1)}, f32[4,45,32]{1,2,0:T(8,128)}, u32[]{:S(2)}) copy-start(f32[4,45,32]{1,2,0:T(8,128)} %param.15) | copy-start | bytes 69124
  1.5 20.5 %copy-start.13 = (s32[4]{0:T(128)S(1)}, s32[4]{0:T(128)}, u32[]{:S(2)}) copy-start(s32[4]{0:T(128)} %param.14) | copy-start | bytes 52
  3.7 0.9 copy-start.2
  5.3 34.9 %collective-permute-start = (f32[4,2,928]{2,1,0:T(2,128)}, f32[4,2,928]{2,1,0:T(2,128)S(1)}, u32[]{:S(2)}, u32[]{:S(2)}) collective-permute-start(f32[4,2,928]{2,1,0:T(2,128)} %get-tuple-element.50), channel_id=1, source_target_pairs={{0,1},{1,2},{2,3},{3,4},{4,5},{5,6},{6,7},{7,8},{8,9},{9,10},{10,1... | collective-permute-start | bytes 89096 | tf_op jit(solution)/shard_map/ppermute | solution.py:23
  9.6 30.6 %collective-permute-start.1 = (f32[4,2,928]{2,1,0:T(2,128)S(1)}, f32[4,2,928]{2,1,0:T(2,128)S(1)}, u32[]{:S(2)}, u32[]{:S(2)}) collective-permute-start(f32[4,2,928]{2,1,0:T(2,128)S(1)} %get-tuple-element.51), channel_id=1, source_target_pairs={{1,0},{2,1},{3,2},{4,3},{5,4},{6,5},{7,6},{8,7},{9,8},{10,9},{11,1... | collective-permute-start | bytes 89096 | tf_op jit(solution)/shard_map/ppermute | solution.py:25
  22.0 4.7 %copy-start.7 = (f32[4,45,32]{2,1,0:T(8,128)}, f32[4,45,32]{2,1,0:T(8,128)S(1)}, u32[]{:S(2)}) copy-start(f32[4,45,32]{2,1,0:T(8,128)S(1)} %copy.63.seed_ref) | copy-start | bytes 69124
  26.7 1.6 copy-start.14
  26.7 4.3 %copy-start.12 = (s32[4,45,32]{1,2,0:T(8,128)S(1)}, s32[4,45,32]{1,2,0:T(8,128)}, u32[]{:S(2)}) copy-start(s32[4,45,32]{1,2,0:T(8,128)} %param.13) | copy-start | bytes 69124
  36.7 3.5 %copy-start.3 = (f32[4,45,864]{2,1,0:T(8,128)S(1)}, f32[4,45,864]{2,1,0:T(8,128)}, u32[]{:S(2)}) copy-start(f32[4,45,864]{2,1,0:T(8,128)} %copy-done.2) | copy-start | bytes 1866244
  41.5 1.4 copy-start
  41.8 1.6 copy-start.6
  43.6 7.8 %collective-permute-start.2 = (f32[2,45,928]{2,1,0:T(8,128)S(1)}, f32[2,45,928]{2,1,0:T(8,128)S(1)}, u32[]{:S(2)}, u32[]{:S(2)}) collective-permute-start(f32[2,45,928]{2,1,0:T(8,128)S(1)} %get-tuple-element.52), channel_id=1, source_target_pairs={{0,32},{32,64},{64,96},{96,128},{128,160},{160,192},{192,224},{224... | collective-permute-start | bytes 1002248 | tf_op jit(solution)/shard_map/ppermute | solution.py:23
  46.8 9.1 %collective-permute-start.3 = (f32[2,45,928]{2,1,0:T(8,128)S(1)}, f32[2,45,928]{2,1,0:T(8,128)S(1)}, u32[]{:S(2)}, u32[]{:S(2)}) collective-permute-start(f32[2,45,928]{2,1,0:T(8,128)S(1)} %get-tuple-element.53), channel_id=1, source_target_pairs={{32,0},{64,32},{96,64},{128,96},{160,128},{192,160},{224,192},{256... | collective-permute-start | bytes 1002248 | tf_op jit(solution)/shard_map/ppermute | solution.py:25
  58.1 1.1 copy-start.5
  59.2 1.1 copy-start.4
  77.0 4.8 %copy-start.9 = (f32[4,45,864]{2,1,0:T(8,128)S(1)}, f32[4,45,864]{2,1,0:T(8,128)}, u32[]{:S(2)}) copy-start(f32[4,45,864]{2,1,0:T(8,128)} %get-tuple-element.9) | copy-start | bytes 1866244
  83.5 101.7 %copy-start.8 = (f32[4,45,864]{2,1,0:T(8,128)S(1)}, f32[4,45,864]{2,1,0:T(8,128)}, u32[]{:S(2)}) copy-start(f32[4,45,864]{2,1,0:T(8,128)} %get-tuple-element.7) | copy-start | bytes 1866244
  83.5 101.7 %copy-start.10 = (f32[2,45,864]{2,1,0:T(8,128)S(1)}, f32[2,45,864]{2,1,0:T(8,128)}, u32[]{:S(2)}) copy-start(f32[2,45,864]{2,1,0:T(8,128)} %get-tuple-element.6) | copy-start | bytes 933124
  83.5 99.5 %collective-permute-start.4 = (f32[2,45,864]{2,1,0:T(8,128)S(1)}, f32[2,45,864]{2,1,0:T(8,128)S(1)}, u32[]{:S(2)}, u32[]{:S(2)}) collective-permute-start(f32[2,45,864]{2,1,0:T(8,128)S(1)} %slice.260), channel_id=1, source_target_pairs={{0,32},{32,64},{64,96},{96,128},{128,160},{160,192},{192,224},{224... | collective-permute-start | bytes 933128 | tf_op jit(solution)/shard_map/ppermute | solution.py:23
  183.1 8.6 %collective-permute-start.5 = (f32[2,45,864]{2,1,0:T(8,128)S(1)}, f32[2,45,864]{2,1,0:T(8,128)S(1)}, u32[]{:S(2)}, u32[]{:S(2)}) collective-permute-start(f32[2,45,864]{2,1,0:T(8,128)S(1)} %get-tuple-element.41), channel_id=1, source_target_pairs={{32,0},{64,32},{96,64},{128,96},{160,128},{192,160},{224,192},{256... | collective-permute-start | bytes 933128 | tf_op jit(solution)/shard_map/ppermute | solution.py:25
  186.4 5.4 %copy-start.1 = (f32[3,4,46,864]{3,2,1,0:T(8,128)S(1)}, f32[3,4,46,864]{3,2,1,0:T(8,128)}, u32[]{:S(2)}) copy-start(f32[3,4,46,864]{3,2,1,0:T(8,128)} %copy-done) | copy-start | bytes 5723140
  192.1 9.3 %collective-permute-start.6 = (f32[4,2,864]{2,1,0:T(2,128)S(1)}, f32[4,2,864]{2,1,0:T(2,128)S(1)}, u32[]{:S(2)}, u32[]{:S(2)}) collective-permute-start(f32[4,2,864]{2,1,0:T(2,128)S(1)} %get-tuple-element.38), channel_id=1, source_target_pairs={{0,1},{1,2},{2,3},{3,4},{4,5},{5,6},{6,7},{7,8},{8,9},{9,10},{10,1... | collective-permute-start | bytes 82952 | tf_op jit(solution)/shard_map/ppermute | solution.py:23
  194.0 7.9 %collective-permute-start.7 = (f32[4,2,864]{2,1,0:T(2,128)S(1)}, f32[4,2,864]{2,1,0:T(2,128)S(1)}, u32[]{:S(2)}, u32[]{:S(2)}) collective-permute-start(f32[4,2,864]{2,1,0:T(2,128)S(1)} %get-tuple-element.39), channel_id=1, source_target_pairs={{1,0},{2,1},{3,2},{4,3},{5,4},{6,5},{7,6},{8,7},{9,8},{10,9},{11,1... | collective-permute-start | bytes 82952 | tf_op jit(solution)/shard_map/ppermute | solution.py:25

commit v3 on v2

--- a/solution.py
+++ b/solution.py
@@ -301,8 +301,8 @@
     for newton_step in range(NEWTON):
         denominator = aerosol + sat
         fraction = mass / denominator
-        first_sum = jnp.sum(fraction, axis=0, keepdims=True)
-        second_sum = jnp.sum(fraction / denominator, axis=0, keepdims=True)
+        first_sum = jnp.sum(fraction, axis=-2, keepdims=True)
+        second_sum = jnp.sum(fraction / denominator, axis=-2, keepdims=True)
         residue = 1.0 - seed / aerosol - first_sum
         derivative = seed / (aerosol * aerosol) + second_sum
         history.append((aerosol, residue, derivative))
@@ -310,11 +310,11 @@
     final_den = aerosol + sat
     particle = mass * aerosol / final_den
     mass_bar = cot * aerosol / final_den
-    aerosol_bar = jnp.sum(cot * mass * sat / (final_den * final_den), axis=0, keepdims=True)
+    aerosol_bar = jnp.sum(cot * mass * sat / (final_den * final_den), axis=-2, keepdims=True)
     for newton_step in reversed(range(NEWTON)):
         a_n, residue, derivative = history[newton_step]
         inverse = 1.0 / (a_n + sat)
-        third_sum = jnp.sum(mass * inverse * inverse * inverse, axis=0, keepdims=True)
+        third_sum = jnp.sum(mass * inverse * inverse * inverse, axis=-2, keepdims=True)
         slope = -2.0 * (seed / (a_n * a_n * a_n) + third_sum)
         over_g = aerosol_bar / derivative
         over_g2 = over_g * residue / derivative
@@ -394,21 +394,28 @@
         valid = species_row < chunk
         sat = v_ref[...]
 
-        def chemistry(s, acc):
-            values = land_go[s, 0:padded, :]
+        def smooth_out(s, carry):
             smooth = lax.dot_general(coefficient, t_ref[s], nt, precision=hi,
                                      preferred_element_type=jnp.float32)
-            smooth = jnp.where(keep_lane, smooth, values)
-            seed = land_go[s, pl.ds(chunk, 1), :]
-            particle, gradient = column_chemistry(
-                smooth, seed, land_go[s, padded:, :], sat, valid
-            )
-            out_back[s, 0:padded, :] = particle
-            field_s[s] = gradient
-            return acc + jnp.dot(gradient, t_ref[s], precision=hi,
+            field_s[s] = jnp.where(keep_lane, smooth, land_go[s, 0:padded, :])
+            return carry
+
+        lax.fori_loop(0, count, smooth_out, 0)
+        particle, gradient = column_chemistry(
+            field_s[...],
+            land_go[:, chunk : chunk + 1, :],
+            land_go[:, padded:, :],
+            sat[None],
+            valid[None],
+        )
+        out_back[:, 0:padded, :] = particle
+        field_s[...] = gradient
+
+        def gather_adjoint(s, acc):
+            return acc + jnp.dot(field_s[s], t_ref[s], precision=hi,
                                  preferred_element_type=jnp.float32)
 
-        adjoint_coef = lax.fori_loop(0, count, chemistry, zero) * w_ref[...]
+        adjoint_coef = lax.fori_loop(0, count, gather_adjoint, zero) * w_ref[...]
 
         def synthesise(s, carry):
             smooth = lax.dot_general(adjoint_coef, t_ref[s], nt, precision=hi,

time: 204 us -> 200 us (0.980)
  waiting for transfers between devices: 109 us -> 105 us
    ppermute x4, waiting for transfers between devices: 99.1 us -> 94.8 us  [with_halo(): lax.ppermute(tail, axis, [(i, (i + 1) % count) for i in range(ends)])]
where the time goes in v3:
time: 200 us; the launch traced here: 199 us
  waiting for transfers between devices  105 us (52%)
  starting transfers between devices  34.7 us (17%)
  Pallas kernels  21.2 us (11%)
  local copies, waits for them, and re-layouts  19.6 us (10%)
  other arithmetic  14.7 us (7%)
  matrix products  2.3 us (1%)
    ppermute x4, waiting for transfers between devices, with_halo(): lax.ppermute(tail, axis, [(i, (i + 1) % count) for i in range(ends)])  94.8 us
    ppermute x4, starting transfers between devices, with_halo(): lax.ppermute(head, axis, [((i + 1) % count, i) for i in range(ends)])  23.2 us
    pallas_call x1, Pallas kernels, chemistry_step(): pl.pallas_call(chem_kernel, grid=(rows,), in_specs=[big, small, big, pl.B...  16.7 us
    ppermute x4, starting transfers between devices, with_halo(): lax.ppermute(tail, axis, [(i, (i + 1) % count) for i in range(ends)])  11.5 us
    unnamed x37, local copies, waits for them, and re-layouts  10.5 us
    ppermute x4, waiting for transfers between devices, with_halo(): lax.ppermute(head, axis, [((i + 1) % count, i) for i in range(ends)])  10.2 us
    reshape x2, local copies, waits for them, and re-layouts, polar_step(): blocks = jnp.einsum('sjk,rR->srjRk', table, jnp.eye(polar_count, dtype=jn...  6.05 us
    pallas_call x1, Pallas kernels, polar_step(): pl.pallas_call(owner_kernel, out_shape=[end_shape, end_shape], in_specs=[...  4.54 us
  transfers between devices with their start and end apart: 8, of which 5 were waited for; matrix products, arithmetic and copies ran while one was open for 10% of the time, Pallas kernels for 0%

profile of v3, /device:TPU:1, one launch (start us, length us, event | category | flops | bytes accessed | tf_op | source)
XLA Modules:
  0.0 198.7 jit_solution(15012469079409552801)
XLA Ops:
  0.6 0.9 convert_element_type.30
  1.6 1.0 copy.51
  2.6 1.1 copy.56
  3.7 0.8 copy-done.2
  4.6 0.7 pad_maximum_fusion.19
  5.3 4.4 %collective-permute-start = (f32[4,2,928]{2,1,0:T(2,128)}, f32[4,2,928]{2,1,0:T(2,128)S(1)}, u32[]{:S(2)}, u32[]{:S(2)}) collective-permute-start(f32[4,2,928]{2,1,0:T(2,128)} %get-tuple-element.50), channel_id=1, source_target_pairs={{0,1},{1,2},{2,3},{3,4},{4,5},{5,6},{6,7},{7,8},{8,9},{9,10},{10,1... | collective-permute-start | bytes 89096 | tf_op jit(solution)/shard_map/ppermute | solution.py:23
  9.6 12.1 %collective-permute-start.1 = (f32[4,2,928]{2,1,0:T(2,128)S(1)}, f32[4,2,928]{2,1,0:T(2,128)S(1)}, u32[]{:S(2)}, u32[]{:S(2)}) collective-permute-start(f32[4,2,928]{2,1,0:T(2,128)S(1)} %get-tuple-element.51), channel_id=1, source_target_pairs={{1,0},{2,1},{3,2},{4,3},{5,4},{6,5},{7,6},{8,7},{9,8},{10,9},{11,1... | collective-permute-start | bytes 89096 | tf_op jit(solution)/shard_map/ppermute | solution.py:25
  22.1 0.6 slice_select_fusion.6.s_ref
  22.7 0.6 fusion.46.spread_ref
  23.3 3.1 %fusion.11 = (f32[32,45,32]{2,0,1:T(8,128)S(1)}, f32[32,45,32]{2,0,1:T(8,128)S(1)}) fusion(s32[32,45]{0,1:T(8,128)S(1)} %multiply_add_fusion), kind=kLoop, calls=%fused_computation.29 | loop fusion | flops 414720 | bytes 374400 | tf_op jit(solution)/shard_map/cos | solution.py:154
  26.4 0.3 pad_maximum_fusion.3
  26.7 1.5 multiply_bitcast_fusion
  28.4 0.6 select_n.189.w_ref
  29.0 0.7 broadcast_in_dim_reshape.3.m_ref
  29.7 0.7 copy.65.v_ref
  30.4 0.7 broadcast_in_dim_tile.3.sat_ref
  31.2 1.0 copy.57
  32.1 2.0 %copy.61.cot_ref = f32[4,45,864]{2,1,0:T(8,128)} copy(f32[4,45,864]{2,0,1:T(4,128)} %param.17) | data formatting | bytes 1244160 | tf_op args[8]
  34.1 2.6 %reshape.100 = f32[32,90,128]{2,0,1:T(8,128)} reshape(f32[32,2,45,2,64]{4,3,0,2,1:T(2,128)S(1)} %multiply_bitcast_fusion) | data formatting | bytes 2949120 | tf_op jit(solution)/shard_map/reshape | solution.py:459
  36.7 3.5 %copy.66.t_ref = f32[32,90,128]{2,1,0:T(8,128)} copy(f32[32,90,128]{2,0,1:T(8,128)} %reshape.100) | data formatting | bytes 2949120 | tf_op jit(solution)/shard_map/reshape | solution.py:459
  40.5 1.1 fusion.25
  41.5 0.2 maximum_maximum_fusion.1
  42.1 0.8 copy-done
  42.9 0.5 copy-done.6
  43.6 3.1 %collective-permute-start.2 = (f32[2,45,928]{2,1,0:T(8,128)S(1)}, f32[2,45,928]{2,1,0:T(8,128)S(1)}, u32[]{:S(2)}, u32[]{:S(2)}) collective-permute-start(f32[2,45,928]{2,1,0:T(8,128)S(1)} %get-tuple-element.52), channel_id=1, source_target_pairs={{0,32},{32,64},{64,96},{96,128},{128,160},{160,192},{192,224},{224... | collective-permute-start | bytes 1002248 | tf_op jit(solution)/shard_map/ppermute | solution.py:23
  46.8 2.1 %collective-permute-start.3 = (f32[2,45,928]{2,1,0:T(8,128)S(1)}, f32[2,45,928]{2,1,0:T(8,128)S(1)}, u32[]{:S(2)}, u32[]{:S(2)}) collective-permute-start(f32[2,45,928]{2,1,0:T(8,128)S(1)} %get-tuple-element.53), channel_id=1, source_target_pairs={{32,0},{64,32},{96,64},{128,96},{160,128},{192,160},{224,192},{256... | collective-permute-start | bytes 1002248 | tf_op jit(solution)/shard_map/ppermute | solution.py:25
  48.9 0.9 fusion.21.group_ref
  49.9 1.6 collective-permute-done.2
  51.5 4.4 %collective-permute-done.3 = f32[2,45,928]{2,1,0:T(8,128)S(1)} collective-permute-done((f32[2,45,928]{2,1,0:T(8,128)S(1)}, f32[2,45,928]{2,1,0:T(8,128)S(1)}, u32[]{:S(2)}, u32[]{:S(2)}) %collective-permute-start.3) | collective-permute-done | bytes 334112 | tf_op jit(solution)/shard_map/ppermute | solution.py:25
  56.2 1.2 fusion.23
  57.4 0.3 maximum_maximum_fusion
  57.8 0.4 fusion
  58.2 1.0 copy-done.5
  59.2 1.1 slice_select_fusion
  60.3 16.7 %shard_map.105 = (f32[4,45,864]{2,1,0:T(8,128)}, f32[4,45,864]{2,1,0:T(8,128)}) custom-call(f32[4,45,864]{2,1,0:T(8,128)} %copy-done.4, f32[4,45,32]{2,1,0:T(8,128)} %copy-done.7, f32[4,45,864]{2,1,0:T(8,128)} %copy.61.cot_ref, f32[1,864]{1,0:T(1,128)} %broadcast_in_dim_tile.3.sat_ref, f32[32,864]{1,0:T(8,128)} %fusion.46.spread_ref, f32[864,32]{1,0:T(8,128)} %fusion.21.group_ref), custom_call_target="tpu_custom_call" | custom-call | tf_op jit(solution)/shard_map/pallas_call | solution.py:582
  77.0 4.5 %shard_map.104 = (f32[2,45,864]{2,1,0:T(8,128)}, f32[2,45,864]{2,1,0:T(8,128)}) custom-call(f32[2,45,864]{2,1,0:T(8,128)} %get-tuple-element.61.x_ref, f32[2,45,864]{2,1,0:T(8,128)} %get-tuple-element.60.c_ref, f32[2,45,32]{2,1,0:T(8,128)} %slice_select_fusion.6.s_ref, f32[1,128]{1,0:T(1,128)} %select_n.189.w_ref, f32[1,90]{1,0:T(1,128)} %broadcast_in_dim_reshape.3.m_ref, ...), custom_call_target="tpu_custom_call" | custom-call | tf_op jit(solution)/shard_map/pallas_call | solution.py:469
  81.6 1.0 slice_select_fusion.3
  82.7 0.3 fusion.5
  83.3 2.1 %collective-permute-start.4 = (f32[2,45,864]{2,1,0:T(8,128)S(1)}, f32[2,45,864]{2,1,0:T(8,128)S(1)}, u32[]{:S(2)}, u32[]{:S(2)}) collective-permute-start(f32[2,45,864]{2,1,0:T(8,128)S(1)} %slice.260), channel_id=1, source_target_pairs={{0,32},{32,64},{64,96},{96,128},{128,160},{160,192},{192,224},{224... | collective-permute-start | bytes 933128 | tf_op jit(solution)/shard_map/ppermute | solution.py:23
  85.4 93.1 %collective-permute-done.4 = f32[2,45,864]{2,1,0:T(8,128)S(1)} collective-permute-done((f32[2,45,864]{2,1,0:T(8,128)S(1)}, f32[2,45,864]{2,1,0:T(8,128)S(1)}, u32[]{:S(2)}, u32[]{:S(2)}) %collective-permute-start.4) | collective-permute-done | bytes 311072 | tf_op jit(solution)/shard_map/ppermute | solution.py:23
  178.5 2.0 %collective-permute-start.5 = (f32[2,45,864]{2,1,0:T(8,128)S(1)}, f32[2,45,864]{2,1,0:T(8,128)S(1)}, u32[]{:S(2)}, u32[]{:S(2)}) collective-permute-start(f32[2,45,864]{2,1,0:T(8,128)S(1)} %get-tuple-element.41), channel_id=1, source_target_pairs={{32,0},{64,32},{96,64},{128,96},{160,128},{192,160},{224,192},{256... | collective-permute-start | bytes 933128 | tf_op jit(solution)/shard_map/ppermute | solution.py:25
  180.8 1.1 copy.69
  181.8 5.3 %collective-permute-done.5 = f32[2,45,864]{2,1,0:T(8,128)S(1)} collective-permute-done((f32[2,45,864]{2,1,0:T(8,128)S(1)}, f32[2,45,864]{2,1,0:T(8,128)S(1)}, u32[]{:S(2)}, u32[]{:S(2)}) %collective-permute-start.5) | collective-permute-done | bytes 311072 | tf_op jit(solution)/shard_map/ppermute | solution.py:25
  187.6 1.9 collective-permute-start.6
  189.5 7.0 %collective-permute-start.7 = (f32[4,2,864]{2,1,0:T(2,128)S(1)}, f32[4,2,864]{2,1,0:T(2,128)S(1)}, u32[]{:S(2)}, u32[]{:S(2)}) collective-permute-start(f32[4,2,864]{2,1,0:T(2,128)S(1)} %get-tuple-element.39), channel_id=1, source_target_pairs={{1,0},{2,1},{3,2},{4,3},{5,4},{6,5},{7,6},{8,7},{9,8},{10,9},{11,1... | collective-permute-start | bytes 82952 | tf_op jit(solution)/shard_map/ppermute | solution.py:25
  196.5 0.3 pad_add_fusion.2
  196.9 0.5 collective-permute-done.7
  197.6 1.1 copy.70
  (68 shorter events, 3.0 us)
Async XLA Ops:
  0.6 21.2 %copy-start.11 = (f32[4,45,32]{1,2,0:T(8,128)S(1)}, f32[4,45,32]{1,2,0:T(8,128)}, u32[]{:S(2)}) copy-start(f32[4,45,32]{1,2,0:T(8,128)} %param.15) | copy-start | bytes 69124
  1.5 20.5 %copy-start.13 = (s32[4]{0:T(128)S(1)}, s32[4]{0:T(128)}, u32[]{:S(2)}) copy-start(s32[4]{0:T(128)} %param.14) | copy-start | bytes 52
  3.7 0.9 copy-start.2
  5.3 34.9 %collective-permute-start = (f32[4,2,928]{2,1,0:T(2,128)}, f32[4,2,928]{2,1,0:T(2,128)S(1)}, u32[]{:S(2)}, u32[]{:S(2)}) collective-permute-start(f32[4,2,928]{2,1,0:T(2,128)} %get-tuple-element.50), channel_id=1, source_target_pairs={{0,1},{1,2},{2,3},{3,4},{4,5},{5,6},{6,7},{7,8},{8,9},{9,10},{10,1... | collective-permute-start | bytes 89096 | tf_op jit(solution)/shard_map/ppermute | solution.py:23
  9.6 30.6 %collective-permute-start.1 = (f32[4,2,928]{2,1,0:T(2,128)S(1)}, f32[4,2,928]{2,1,0:T(2,128)S(1)}, u32[]{:S(2)}, u32[]{:S(2)}) collective-permute-start(f32[4,2,928]{2,1,0:T(2,128)S(1)} %get-tuple-element.51), channel_id=1, source_target_pairs={{1,0},{2,1},{3,2},{4,3},{5,4},{6,5},{7,6},{8,7},{9,8},{10,9},{11,1... | collective-permute-start | bytes 89096 | tf_op jit(solution)/shard_map/ppermute | solution.py:25
  22.0 4.7 %copy-start.7 = (f32[4,45,32]{2,1,0:T(8,128)}, f32[4,45,32]{2,1,0:T(8,128)S(1)}, u32[]{:S(2)}) copy-start(f32[4,45,32]{2,1,0:T(8,128)S(1)} %copy.63.seed_ref) | copy-start | bytes 69124
  26.7 1.6 copy-start.14
  26.7 4.3 %copy-start.12 = (s32[4,45,32]{1,2,0:T(8,128)S(1)}, s32[4,45,32]{1,2,0:T(8,128)}, u32[]{:S(2)}) copy-start(s32[4,45,32]{1,2,0:T(8,128)} %param.13) | copy-start | bytes 69124
  36.7 3.5 %copy-start.3 = (f32[4,45,864]{2,1,0:T(8,128)S(1)}, f32[4,45,864]{2,1,0:T(8,128)}, u32[]{:S(2)}) copy-start(f32[4,45,864]{2,1,0:T(8,128)} %copy-done.2) | copy-start | bytes 1866244
  41.5 1.4 copy-start
  41.8 1.6 copy-start.6
  43.6 7.8 %collective-permute-start.2 = (f32[2,45,928]{2,1,0:T(8,128)S(1)}, f32[2,45,928]{2,1,0:T(8,128)S(1)}, u32[]{:S(2)}, u32[]{:S(2)}) collective-permute-start(f32[2,45,928]{2,1,0:T(8,128)S(1)} %get-tuple-element.52), channel_id=1, source_target_pairs={{0,32},{32,64},{64,96},{96,128},{128,160},{160,192},{192,224},{224... | collective-permute-start | bytes 1002248 | tf_op jit(solution)/shard_map/ppermute | solution.py:23
  46.8 9.1 %collective-permute-start.3 = (f32[2,45,928]{2,1,0:T(8,128)S(1)}, f32[2,45,928]{2,1,0:T(8,128)S(1)}, u32[]{:S(2)}, u32[]{:S(2)}) collective-permute-start(f32[2,45,928]{2,1,0:T(8,128)S(1)} %get-tuple-element.53), channel_id=1, source_target_pairs={{32,0},{64,32},{96,64},{128,96},{160,128},{192,160},{224,192},{256... | collective-permute-start | bytes 1002248 | tf_op jit(solution)/shard_map/ppermute | solution.py:25
  58.1 1.1 copy-start.5
  59.2 1.1 copy-start.4
  77.0 4.6 %copy-start.9 = (f32[4,45,864]{2,1,0:T(8,128)S(1)}, f32[4,45,864]{2,1,0:T(8,128)}, u32[]{:S(2)}) copy-start(f32[4,45,864]{2,1,0:T(8,128)} %get-tuple-element.9) | copy-start | bytes 1866244
  83.2 97.3 %copy-start.8 = (f32[4,45,864]{2,1,0:T(8,128)S(1)}, f32[4,45,864]{2,1,0:T(8,128)}, u32[]{:S(2)}) copy-start(f32[4,45,864]{2,1,0:T(8,128)} %get-tuple-element.7) | copy-start | bytes 1866244
  83.3 97.3 %copy-start.10 = (f32[2,45,864]{2,1,0:T(8,128)S(1)}, f32[2,45,864]{2,1,0:T(8,128)}, u32[]{:S(2)}) copy-start(f32[2,45,864]{2,1,0:T(8,128)} %get-tuple-element.6) | copy-start | bytes 933124
  83.3 95.2 %collective-permute-start.4 = (f32[2,45,864]{2,1,0:T(8,128)S(1)}, f32[2,45,864]{2,1,0:T(8,128)S(1)}, u32[]{:S(2)}, u32[]{:S(2)}) collective-permute-start(f32[2,45,864]{2,1,0:T(8,128)S(1)} %slice.260), channel_id=1, source_target_pairs={{0,32},{32,64},{64,96},{96,128},{128,160},{160,192},{192,224},{224... | collective-permute-start | bytes 933128 | tf_op jit(solution)/shard_map/ppermute | solution.py:23
  178.5 8.6 %collective-permute-start.5 = (f32[2,45,864]{2,1,0:T(8,128)S(1)}, f32[2,45,864]{2,1,0:T(8,128)S(1)}, u32[]{:S(2)}, u32[]{:S(2)}) collective-permute-start(f32[2,45,864]{2,1,0:T(8,128)S(1)} %get-tuple-element.41), channel_id=1, source_target_pairs={{32,0},{64,32},{96,64},{128,96},{160,128},{192,160},{224,192},{256... | collective-permute-start | bytes 933128 | tf_op jit(solution)/shard_map/ppermute | solution.py:25
  181.8 5.4 %copy-start.1 = (f32[3,4,46,864]{3,2,1,0:T(8,128)S(1)}, f32[3,4,46,864]{3,2,1,0:T(8,128)}, u32[]{:S(2)}) copy-start(f32[3,4,46,864]{3,2,1,0:T(8,128)} %copy-done) | copy-start | bytes 5723140
  187.6 9.3 %collective-permute-start.6 = (f32[4,2,864]{2,1,0:T(2,128)S(1)}, f32[4,2,864]{2,1,0:T(2,128)S(1)}, u32[]{:S(2)}, u32[]{:S(2)}) collective-permute-start(f32[4,2,864]{2,1,0:T(2,128)S(1)} %get-tuple-element.38), channel_id=1, source_target_pairs={{0,1},{1,2},{2,3},{3,4},{4,5},{5,6},{6,7},{7,8},{8,9},{9,10},{10,1... | collective-permute-start | bytes 82952 | tf_op jit(solution)/shard_map/ppermute | solution.py:23
  189.5 7.9 %collective-permute-start.7 = (f32[4,2,864]{2,1,0:T(2,128)S(1)}, f32[4,2,864]{2,1,0:T(2,128)S(1)}, u32[]{:S(2)}, u32[]{:S(2)}) collective-permute-start(f32[4,2,864]{2,1,0:T(2,128)S(1)} %get-tuple-element.39), channel_id=1, source_target_pairs={{1,0},{2,1},{3,2},{4,3},{5,4},{6,5},{7,6},{8,7},{9,8},{10,9},{11,1... | collective-permute-start | bytes 82952 | tf_op jit(solution)/shard_map/ppermute | solution.py:25

commit v4 on v3

--- a/solution.py
+++ b/solution.py
@@ -524,6 +524,21 @@
 
 
 def chem_kernel(x_ref, seed_ref, cot_ref, sat_ref, spread_ref, group_ref, p_ref, g_ref):
+    row = pl.program_id(0)
+    rows = pl.num_programs(0)
+    band = lax.axis_index("lat")
+    bands = lax.axis_size("lat")
+    polar = jnp.logical_or(
+        jnp.logical_and(band == 0, row < POLAR),
+        jnp.logical_and(band == bands - 1, row >= rows - POLAR),
+    )
+
+    @pl.when(jnp.logical_not(polar))
+    def _():
+        chem_body(x_ref, seed_ref, cot_ref, sat_ref, spread_ref, group_ref, p_ref, g_ref)
+
+
+def chem_body(x_ref, seed_ref, cot_ref, sat_ref, spread_ref, group_ref, p_ref, g_ref):
     hi = lax.Precision.HIGHEST
     x = x_ref[0]
     seed = seed_ref[0]

time: 200 us -> 194 us (0.970)
  waiting for transfers between devices: 105 us -> 98.8 us
    ppermute x4, waiting for transfers between devices: 94.8 us -> 88.6 us  [with_halo(): lax.ppermute(tail, axis, [(i, (i + 1) % count) for i in range(ends)])]
  transfers between devices with their start and end apart: 8 -> 8, of which waited for: 5 -> 5; matrix products, arithmetic and copies ran while one was open for 10% -> 11% of each run, Pallas kernels for 0% -> 0%
where the time goes in v4:
time: 194 us; the launch traced here: 193 us
  waiting for transfers between devices  98.8 us (51%)
  starting transfers between devices  34.7 us (18%)
  Pallas kernels  21.4 us (11%)
  local copies, waits for them, and re-layouts  19.6 us (10%)
  other arithmetic  14.7 us (8%)
  matrix products  2.3 us (1%)
    ppermute x4, waiting for transfers between devices, with_halo(): lax.ppermute(tail, axis, [(i, (i + 1) % count) for i in range(ends)])  88.6 us
    ppermute x4, starting transfers between devices, with_halo(): lax.ppermute(head, axis, [((i + 1) % count, i) for i in range(ends)])  23.2 us
    pallas_call x1, Pallas kernels, chemistry_step(): pl.pallas_call(chem_kernel, grid=(rows,), in_specs=[big, small, big, pl.B...  16.9 us
    ppermute x4, starting transfers between devices, with_halo(): lax.ppermute(tail, axis, [(i, (i + 1) % count) for i in range(ends)])  11.5 us
    unnamed x37, local copies, waits for them, and re-layouts  10.5 us
    ppermute x4, waiting for transfers between devices, with_halo(): lax.ppermute(head, axis, [((i + 1) % count, i) for i in range(ends)])  10.2 us
    reshape x2, local copies, waits for them, and re-layouts, polar_step(): blocks = jnp.einsum('sjk,rR->srjRk', table, jnp.eye(polar_count, dtype=jn...  6.05 us
    pallas_call x1, Pallas kernels, polar_step(): pl.pallas_call(owner_kernel, out_shape=[end_shape, end_shape], in_specs=[...  4.54 us
  transfers between devices with their start and end apart: 8, of which 5 were waited for; matrix products, arithmetic and copies ran while one was open for 11% of the time, Pallas kernels for 0%

profile of v4, /device:TPU:1, one launch (start us, length us, event | category | flops | bytes accessed | tf_op | source)
XLA Modules:
  0.0 192.8 jit_solution(6972848060024234963)
XLA Ops:
  0.6 0.9 convert_element_type.30
  1.6 1.0 copy.51
  2.6 1.1 copy.56
  3.7 0.8 copy-done.2
  4.6 0.7 pad_maximum_fusion.19
  5.3 4.4 %collective-permute-start = (f32[4,2,928]{2,1,0:T(2,128)}, f32[4,2,928]{2,1,0:T(2,128)S(1)}, u32[]{:S(2)}, u32[]{:S(2)}) collective-permute-start(f32[4,2,928]{2,1,0:T(2,128)} %get-tuple-element.50), channel_id=1, source_target_pairs={{0,1},{1,2},{2,3},{3,4},{4,5},{5,6},{6,7},{7,8},{8,9},{9,10},{10,1... | collective-permute-start | bytes 89096 | tf_op jit(solution)/shard_map/ppermute | solution.py:23
  9.6 12.1 %collective-permute-start.1 = (f32[4,2,928]{2,1,0:T(2,128)S(1)}, f32[4,2,928]{2,1,0:T(2,128)S(1)}, u32[]{:S(2)}, u32[]{:S(2)}) collective-permute-start(f32[4,2,928]{2,1,0:T(2,128)S(1)} %get-tuple-element.51), channel_id=1, source_target_pairs={{1,0},{2,1},{3,2},{4,3},{5,4},{6,5},{7,6},{8,7},{9,8},{10,9},{11,1... | collective-permute-start | bytes 89096 | tf_op jit(solution)/shard_map/ppermute | solution.py:25
  22.1 0.6 slice_select_fusion.6.s_ref
  22.7 0.6 fusion.46.spread_ref
  23.3 3.1 %fusion.11 = (f32[32,45,32]{2,0,1:T(8,128)S(1)}, f32[32,45,32]{2,0,1:T(8,128)S(1)}) fusion(s32[32,45]{0,1:T(8,128)S(1)} %multiply_add_fusion), kind=kLoop, calls=%fused_computation.29 | loop fusion | flops 414720 | bytes 374400 | tf_op jit(solution)/shard_map/cos | solution.py:154
  26.4 0.3 pad_maximum_fusion.3
  26.7 1.5 multiply_bitcast_fusion
  28.4 0.6 select_n.189.w_ref
  29.0 0.7 broadcast_in_dim_reshape.3.m_ref
  29.7 0.7 copy.65.v_ref
  30.4 0.7 broadcast_in_dim_tile.3.sat_ref
  31.2 1.0 copy.57
  32.1 2.0 %copy.61.cot_ref = f32[4,45,864]{2,1,0:T(8,128)} copy(f32[4,45,864]{2,0,1:T(4,128)} %param.17) | data formatting | bytes 1244160 | tf_op args[8]
  34.1 2.6 %reshape.100 = f32[32,90,128]{2,0,1:T(8,128)} reshape(f32[32,2,45,2,64]{4,3,0,2,1:T(2,128)S(1)} %multiply_bitcast_fusion) | data formatting | bytes 2949120 | tf_op jit(solution)/shard_map/reshape | solution.py:459
  36.7 3.5 %copy.66.t_ref = f32[32,90,128]{2,1,0:T(8,128)} copy(f32[32,90,128]{2,0,1:T(8,128)} %reshape.100) | data formatting | bytes 2949120 | tf_op jit(solution)/shard_map/reshape | solution.py:459
  40.5 1.1 fusion.25
  41.5 0.2 maximum_maximum_fusion.1
  42.1 0.8 copy-done
  42.9 0.5 copy-done.6
  43.6 3.1 %collective-permute-start.2 = (f32[2,45,928]{2,1,0:T(8,128)S(1)}, f32[2,45,928]{2,1,0:T(8,128)S(1)}, u32[]{:S(2)}, u32[]{:S(2)}) collective-permute-start(f32[2,45,928]{2,1,0:T(8,128)S(1)} %get-tuple-element.52), channel_id=1, source_target_pairs={{0,32},{32,64},{64,96},{96,128},{128,160},{160,192},{192,224},{224... | collective-permute-start | bytes 1002248 | tf_op jit(solution)/shard_map/ppermute | solution.py:23
  46.8 2.1 %collective-permute-start.3 = (f32[2,45,928]{2,1,0:T(8,128)S(1)}, f32[2,45,928]{2,1,0:T(8,128)S(1)}, u32[]{:S(2)}, u32[]{:S(2)}) collective-permute-start(f32[2,45,928]{2,1,0:T(8,128)S(1)} %get-tuple-element.53), channel_id=1, source_target_pairs={{32,0},{64,32},{96,64},{128,96},{160,128},{192,160},{224,192},{256... | collective-permute-start | bytes 1002248 | tf_op jit(solution)/shard_map/ppermute | solution.py:25
  48.9 0.9 fusion.21.group_ref
  49.9 1.6 collective-permute-done.2
  51.5 4.4 %collective-permute-done.3 = f32[2,45,928]{2,1,0:T(8,128)S(1)} collective-permute-done((f32[2,45,928]{2,1,0:T(8,128)S(1)}, f32[2,45,928]{2,1,0:T(8,128)S(1)}, u32[]{:S(2)}, u32[]{:S(2)}) %collective-permute-start.3) | collective-permute-done | bytes 334112 | tf_op jit(solution)/shard_map/ppermute | solution.py:25
  56.2 1.2 fusion.23
  57.4 0.3 maximum_maximum_fusion
  57.8 0.4 fusion
  58.2 1.0 copy-done.5
  59.2 1.1 slice_select_fusion
  60.3 16.9 %shard_map.105 = (f32[4,45,864]{2,1,0:T(8,128)}, f32[4,45,864]{2,1,0:T(8,128)}) custom-call(f32[4,45,864]{2,1,0:T(8,128)} %copy-done.4, f32[4,45,32]{2,1,0:T(8,128)} %copy-done.7, f32[4,45,864]{2,1,0:T(8,128)} %copy.61.cot_ref, f32[1,864]{1,0:T(1,128)} %broadcast_in_dim_tile.3.sat_ref, f32[32,864]{1,0:T(8,128)} %fusion.46.spread_ref, f32[864,32]{1,0:T(8,128)} %fusion.21.group_ref), custom_call_target="tpu_custom_call" | custom-call | tf_op jit(solution)/shard_map/pallas_call | solution.py:597
  77.2 4.5 %shard_map.104 = (f32[2,45,864]{2,1,0:T(8,128)}, f32[2,45,864]{2,1,0:T(8,128)}) custom-call(f32[2,45,864]{2,1,0:T(8,128)} %get-tuple-element.61.x_ref, f32[2,45,864]{2,1,0:T(8,128)} %get-tuple-element.60.c_ref, f32[2,45,32]{2,1,0:T(8,128)} %slice_select_fusion.6.s_ref, f32[1,128]{1,0:T(1,128)} %select_n.189.w_ref, f32[1,90]{1,0:T(1,128)} %broadcast_in_dim_reshape.3.m_ref, ...), custom_call_target="tpu_custom_call" | custom-call | tf_op jit(solution)/shard_map/pallas_call | solution.py:469
  81.8 1.0 slice_select_fusion.3
  82.9 0.3 fusion.5
  83.5 2.1 %collective-permute-start.4 = (f32[2,45,864]{2,1,0:T(8,128)S(1)}, f32[2,45,864]{2,1,0:T(8,128)S(1)}, u32[]{:S(2)}, u32[]{:S(2)}) collective-permute-start(f32[2,45,864]{2,1,0:T(8,128)S(1)} %slice.260), channel_id=1, source_target_pairs={{0,32},{32,64},{64,96},{96,128},{128,160},{160,192},{192,224},{224... | collective-permute-start | bytes 933128 | tf_op jit(solution)/shard_map/ppermute | solution.py:23
  85.5 87.0 %collective-permute-done.4 = f32[2,45,864]{2,1,0:T(8,128)S(1)} collective-permute-done((f32[2,45,864]{2,1,0:T(8,128)S(1)}, f32[2,45,864]{2,1,0:T(8,128)S(1)}, u32[]{:S(2)}, u32[]{:S(2)}) %collective-permute-start.4) | collective-permute-done | bytes 311072 | tf_op jit(solution)/shard_map/ppermute | solution.py:23
  172.6 2.0 %collective-permute-start.5 = (f32[2,45,864]{2,1,0:T(8,128)S(1)}, f32[2,45,864]{2,1,0:T(8,128)S(1)}, u32[]{:S(2)}, u32[]{:S(2)}) collective-permute-start(f32[2,45,864]{2,1,0:T(8,128)S(1)} %get-tuple-element.41), channel_id=1, source_target_pairs={{32,0},{64,32},{96,64},{128,96},{160,128},{192,160},{224,192},{256... | collective-permute-start | bytes 933128 | tf_op jit(solution)/shard_map/ppermute | solution.py:25
  174.8 1.1 copy.69
  175.9 5.3 %collective-permute-done.5 = f32[2,45,864]{2,1,0:T(8,128)S(1)} collective-permute-done((f32[2,45,864]{2,1,0:T(8,128)S(1)}, f32[2,45,864]{2,1,0:T(8,128)S(1)}, u32[]{:S(2)}, u32[]{:S(2)}) %collective-permute-start.5) | collective-permute-done | bytes 311072 | tf_op jit(solution)/shard_map/ppermute | solution.py:25
  181.6 1.9 collective-permute-start.6
  183.6 7.0 %collective-permute-start.7 = (f32[4,2,864]{2,1,0:T(2,128)S(1)}, f32[4,2,864]{2,1,0:T(2,128)S(1)}, u32[]{:S(2)}, u32[]{:S(2)}) collective-permute-start(f32[4,2,864]{2,1,0:T(2,128)S(1)} %get-tuple-element.39), channel_id=1, source_target_pairs={{1,0},{2,1},{3,2},{4,3},{5,4},{6,5},{7,6},{8,7},{9,8},{10,9},{11,1... | collective-permute-start | bytes 82952 | tf_op jit(solution)/shard_map/ppermute | solution.py:25
  190.5 0.3 pad_add_fusion.2
  191.0 0.5 collective-permute-done.7
  191.7 1.1 copy.70
  (68 shorter events, 3.0 us)
Async XLA Ops:
  0.6 21.2 %copy-start.11 = (f32[4,45,32]{1,2,0:T(8,128)S(1)}, f32[4,45,32]{1,2,0:T(8,128)}, u32[]{:S(2)}) copy-start(f32[4,45,32]{1,2,0:T(8,128)} %param.15) | copy-start | bytes 69124
  1.5 20.5 %copy-start.13 = (s32[4]{0:T(128)S(1)}, s32[4]{0:T(128)}, u32[]{:S(2)}) copy-start(s32[4]{0:T(128)} %param.14) | copy-start | bytes 52
  3.7 0.9 copy-start.2
  5.3 34.9 %collective-permute-start = (f32[4,2,928]{2,1,0:T(2,128)}, f32[4,2,928]{2,1,0:T(2,128)S(1)}, u32[]{:S(2)}, u32[]{:S(2)}) collective-permute-start(f32[4,2,928]{2,1,0:T(2,128)} %get-tuple-element.50), channel_id=1, source_target_pairs={{0,1},{1,2},{2,3},{3,4},{4,5},{5,6},{6,7},{7,8},{8,9},{9,10},{10,1... | collective-permute-start | bytes 89096 | tf_op jit(solution)/shard_map/ppermute | solution.py:23
  9.6 30.6 %collective-permute-start.1 = (f32[4,2,928]{2,1,0:T(2,128)S(1)}, f32[4,2,928]{2,1,0:T(2,128)S(1)}, u32[]{:S(2)}, u32[]{:S(2)}) collective-permute-start(f32[4,2,928]{2,1,0:T(2,128)S(1)} %get-tuple-element.51), channel_id=1, source_target_pairs={{1,0},{2,1},{3,2},{4,3},{5,4},{6,5},{7,6},{8,7},{9,8},{10,9},{11,1... | collective-permute-start | bytes 89096 | tf_op jit(solution)/shard_map/ppermute | solution.py:25
  22.0 4.7 %copy-start.7 = (f32[4,45,32]{2,1,0:T(8,128)}, f32[4,45,32]{2,1,0:T(8,128)S(1)}, u32[]{:S(2)}) copy-start(f32[4,45,32]{2,1,0:T(8,128)S(1)} %copy.63.seed_ref) | copy-start | bytes 69124
  26.7 1.6 copy-start.14
  26.7 4.3 %copy-start.12 = (s32[4,45,32]{1,2,0:T(8,128)S(1)}, s32[4,45,32]{1,2,0:T(8,128)}, u32[]{:S(2)}) copy-start(s32[4,45,32]{1,2,0:T(8,128)} %param.13) | copy-start | bytes 69124
  36.7 3.5 %copy-start.3 = (f32[4,45,864]{2,1,0:T(8,128)S(1)}, f32[4,45,864]{2,1,0:T(8,128)}, u32[]{:S(2)}) copy-start(f32[4,45,864]{2,1,0:T(8,128)} %copy-done.2) | copy-start | bytes 1866244
  41.5 1.4 copy-start
  41.8 1.6 copy-start.6
  43.6 7.8 %collective-permute-start.2 = (f32[2,45,928]{2,1,0:T(8,128)S(1)}, f32[2,45,928]{2,1,0:T(8,128)S(1)}, u32[]{:S(2)}, u32[]{:S(2)}) collective-permute-start(f32[2,45,928]{2,1,0:T(8,128)S(1)} %get-tuple-element.52), channel_id=1, source_target_pairs={{0,32},{32,64},{64,96},{96,128},{128,160},{160,192},{192,224},{224... | collective-permute-start | bytes 1002248 | tf_op jit(solution)/shard_map/ppermute | solution.py:23
  46.8 9.1 %collective-permute-start.3 = (f32[2,45,928]{2,1,0:T(8,128)S(1)}, f32[2,45,928]{2,1,0:T(8,128)S(1)}, u32[]{:S(2)}, u32[]{:S(2)}) collective-permute-start(f32[2,45,928]{2,1,0:T(8,128)S(1)} %get-tuple-element.53), channel_id=1, source_target_pairs={{32,0},{64,32},{96,64},{128,96},{160,128},{192,160},{224,192},{256... | collective-permute-start | bytes 1002248 | tf_op jit(solution)/shard_map/ppermute | solution.py:25
  58.1 1.1 copy-start.5
  59.2 1.1 copy-start.4
  77.2 4.6 %copy-start.9 = (f32[4,45,864]{2,1,0:T(8,128)S(1)}, f32[4,45,864]{2,1,0:T(8,128)}, u32[]{:S(2)}) copy-start(f32[4,45,864]{2,1,0:T(8,128)} %get-tuple-element.9) | copy-start | bytes 1866244
  83.4 91.2 %copy-start.8 = (f32[4,45,864]{2,1,0:T(8,128)S(1)}, f32[4,45,864]{2,1,0:T(8,128)}, u32[]{:S(2)}) copy-start(f32[4,45,864]{2,1,0:T(8,128)} %get-tuple-element.7) | copy-start | bytes 1866244
  83.4 91.2 %copy-start.10 = (f32[2,45,864]{2,1,0:T(8,128)S(1)}, f32[2,45,864]{2,1,0:T(8,128)}, u32[]{:S(2)}) copy-start(f32[2,45,864]{2,1,0:T(8,128)} %get-tuple-element.6) | copy-start | bytes 933124
  83.5 89.0 %collective-permute-start.4 = (f32[2,45,864]{2,1,0:T(8,128)S(1)}, f32[2,45,864]{2,1,0:T(8,128)S(1)}, u32[]{:S(2)}, u32[]{:S(2)}) collective-permute-start(f32[2,45,864]{2,1,0:T(8,128)S(1)} %slice.260), channel_id=1, source_target_pairs={{0,32},{32,64},{64,96},{96,128},{128,160},{160,192},{192,224},{224... | collective-permute-start | bytes 933128 | tf_op jit(solution)/shard_map/ppermute | solution.py:23
  172.6 8.6 %collective-permute-start.5 = (f32[2,45,864]{2,1,0:T(8,128)S(1)}, f32[2,45,864]{2,1,0:T(8,128)S(1)}, u32[]{:S(2)}, u32[]{:S(2)}) collective-permute-start(f32[2,45,864]{2,1,0:T(8,128)S(1)} %get-tuple-element.41), channel_id=1, source_target_pairs={{32,0},{64,32},{96,64},{128,96},{160,128},{192,160},{224,192},{256... | collective-permute-start | bytes 933128 | tf_op jit(solution)/shard_map/ppermute | solution.py:25
  175.9 5.4 %copy-start.1 = (f32[3,4,46,864]{3,2,1,0:T(8,128)S(1)}, f32[3,4,46,864]{3,2,1,0:T(8,128)}, u32[]{:S(2)}) copy-start(f32[3,4,46,864]{3,2,1,0:T(8,128)} %copy-done) | copy-start | bytes 5723140
  181.6 9.3 %collective-permute-start.6 = (f32[4,2,864]{2,1,0:T(2,128)S(1)}, f32[4,2,864]{2,1,0:T(2,128)S(1)}, u32[]{:S(2)}, u32[]{:S(2)}) collective-permute-start(f32[4,2,864]{2,1,0:T(2,128)S(1)} %get-tuple-element.38), channel_id=1, source_target_pairs={{0,1},{1,2},{2,3},{3,4},{4,5},{5,6},{6,7},{7,8},{8,9},{9,10},{10,1... | collective-permute-start | bytes 82952 | tf_op jit(solution)/shard_map/ppermute | solution.py:23
  183.6 7.9 %collective-permute-start.7 = (f32[4,2,864]{2,1,0:T(2,128)S(1)}, f32[4,2,864]{2,1,0:T(2,128)S(1)}, u32[]{:S(2)}, u32[]{:S(2)}) collective-permute-start(f32[4,2,864]{2,1,0:T(2,128)S(1)} %get-tuple-element.39), channel_id=1, source_target_pairs={{1,0},{2,1},{3,2},{4,3},{5,4},{6,5},{7,6},{8,7},{9,8},{10,9},{11,1... | collective-permute-start | bytes 82952 | tf_op jit(solution)/shard_map/ppermute | solution.py:25

commit v5 on v4

--- a/solution.py
+++ b/solution.py
@@ -388,7 +388,7 @@
                                  preferred_element_type=jnp.float32)
 
         zero = jnp.zeros((padded, t_ref.shape[2]), jnp.float32)
-        coefficient = lax.fori_loop(0, count, analyse, zero) * w_ref[...]
+        coefficient = lax.fori_loop(0, count, analyse, zero, unroll=8) * w_ref[...]
         keep_lane = m_ref[...] > 0.5
         species_row = lax.broadcasted_iota(jnp.int32, (padded, lanes), 0)
         valid = species_row < chunk
@@ -400,7 +400,7 @@
             field_s[s] = jnp.where(keep_lane, smooth, land_go[s, 0:padded, :])
             return carry
 
-        lax.fori_loop(0, count, smooth_out, 0)
+        lax.fori_loop(0, count, smooth_out, 0, unroll=8)
         particle, gradient = column_chemistry(
             field_s[...],
             land_go[:, chunk : chunk + 1, :],
@@ -415,7 +415,7 @@
             return acc + jnp.dot(field_s[s], t_ref[s], precision=hi,
                                  preferred_element_type=jnp.float32)
 
-        adjoint_coef = lax.fori_loop(0, count, gather_adjoint, zero) * w_ref[...]
+        adjoint_coef = lax.fori_loop(0, count, gather_adjoint, zero, unroll=8) * w_ref[...]
 
         def synthesise(s, carry):
             smooth = lax.dot_general(adjoint_coef, t_ref[s], nt, precision=hi,
@@ -423,7 +423,7 @@
             out_back[s, padded:, :] = jnp.where(keep_lane, smooth, field_s[s])
             return carry
 
-        lax.fori_loop(0, count, synthesise, 0)
+        lax.fori_loop(0, count, synthesise, 0, unroll=8)
         round_trip(out_back, land_back, sem_c, sem_d)
         particle_back = land_back[:, 0:padded, :].reshape(count * padded, lanes)
         gradient_back = land_back[:, padded:, :].reshape(count * padded, lanes)

time: 194 us -> 180 us (0.928)
  waiting for transfers between devices: 98.8 us -> 85.2 us
    ppermute x4, waiting for transfers between devices: 88.6 us -> 75 us  [with_halo(): lax.ppermute(tail, axis, [(i, (i + 1) % count) for i in range(ends)])]
  transfers between devices with their start and end apart: 8 -> 8, of which waited for: 5 -> 5; matrix products, arithmetic and copies ran while one was open for 11% -> 12% of each run, Pallas kernels for 0% -> 0%
where the time goes in v5:
time: 180 us; the launch traced here: 179 us
  waiting for transfers between devices  85.2 us (47%)
  starting transfers between devices  34.7 us (19%)
  Pallas kernels  21.4 us (12%)
  local copies, waits for them, and re-layouts  19.6 us (11%)
  other arithmetic  14.7 us (8%)
  matrix products  2.3 us (1%)
    ppermute x4, waiting for transfers between devices, with_halo(): lax.ppermute(tail, axis, [(i, (i + 1) % count) for i in range(ends)])  75 us
    ppermute x4, starting transfers between devices, with_halo(): lax.ppermute(head, axis, [((i + 1) % count, i) for i in range(ends)])  23.2 us
    pallas_call x1, Pallas kernels, chemistry_step(): pl.pallas_call(chem_kernel, grid=(rows,), in_specs=[big, small, big, pl.B...  16.9 us
    ppermute x4, starting transfers between devices, with_halo(): lax.ppermute(tail, axis, [(i, (i + 1) % count) for i in range(ends)])  11.5 us
    unnamed x37, local copies, waits for them, and re-layouts  10.5 us
    ppermute x4, waiting for transfers between devices, with_halo(): lax.ppermute(head, axis, [((i + 1) % count, i) for i in range(ends)])  10.2 us
    reshape x2, local copies, waits for them, and re-layouts, polar_step(): blocks = jnp.einsum('sjk,rR->srjRk', table, jnp.eye(polar_count, dtype=jn...  6.05 us
    pallas_call x1, Pallas kernels, polar_step(): pl.pallas_call(owner_kernel, out_shape=[end_shape, end_shape], in_specs=[...  4.54 us
  transfers between devices with their start and end apart: 8, of which 5 were waited for; matrix products, arithmetic and copies ran while one was open for 12% of the time, Pallas kernels for 0%

profile of v5, /device:TPU:1, one launch (start us, length us, event | category | flops | bytes accessed | tf_op | source)
XLA Modules:
  0.0 179.2 jit_solution(1489955801017381831)
XLA Ops:
  0.6 0.9 convert_element_type.30
  1.6 1.0 copy.51
  2.6 1.1 copy.56
  3.7 0.8 copy-done.2
  4.6 0.7 pad_maximum_fusion.19
  5.3 4.4 %collective-permute-start = (f32[4,2,928]{2,1,0:T(2,128)}, f32[4,2,928]{2,1,0:T(2,128)S(1)}, u32[]{:S(2)}, u32[]{:S(2)}) collective-permute-start(f32[4,2,928]{2,1,0:T(2,128)} %get-tuple-element.50), channel_id=1, source_target_pairs={{0,1},{1,2},{2,3},{3,4},{4,5},{5,6},{6,7},{7,8},{8,9},{9,10},{10,1... | collective-permute-start | bytes 89096 | tf_op jit(solution)/shard_map/ppermute | solution.py:23
  9.6 12.1 %collective-permute-start.1 = (f32[4,2,928]{2,1,0:T(2,128)S(1)}, f32[4,2,928]{2,1,0:T(2,128)S(1)}, u32[]{:S(2)}, u32[]{:S(2)}) collective-permute-start(f32[4,2,928]{2,1,0:T(2,128)S(1)} %get-tuple-element.51), channel_id=1, source_target_pairs={{1,0},{2,1},{3,2},{4,3},{5,4},{6,5},{7,6},{8,7},{9,8},{10,9},{11,1... | collective-permute-start | bytes 89096 | tf_op jit(solution)/shard_map/ppermute | solution.py:25
  22.1 0.6 slice_select_fusion.6.s_ref
  22.7 0.6 fusion.46.spread_ref
  23.3 3.1 %fusion.11 = (f32[32,45,32]{2,0,1:T(8,128)S(1)}, f32[32,45,32]{2,0,1:T(8,128)S(1)}) fusion(s32[32,45]{0,1:T(8,128)S(1)} %multiply_add_fusion), kind=kLoop, calls=%fused_computation.29 | loop fusion | flops 414720 | bytes 374400 | tf_op jit(solution)/shard_map/cos | solution.py:154
  26.4 0.3 pad_maximum_fusion.3
  26.7 1.5 multiply_bitcast_fusion
  28.4 0.6 select_n.189.w_ref
  29.0 0.7 broadcast_in_dim_reshape.3.m_ref
  29.7 0.7 copy.65.v_ref
  30.4 0.7 broadcast_in_dim_tile.3.sat_ref
  31.2 1.0 copy.57
  32.1 2.0 %copy.61.cot_ref = f32[4,45,864]{2,1,0:T(8,128)} copy(f32[4,45,864]{2,0,1:T(4,128)} %param.17) | data formatting | bytes 1244160 | tf_op args[8]
  34.1 2.6 %reshape.100 = f32[32,90,128]{2,0,1:T(8,128)} reshape(f32[32,2,45,2,64]{4,3,0,2,1:T(2,128)S(1)} %multiply_bitcast_fusion) | data formatting | bytes 2949120 | tf_op jit(solution)/shard_map/reshape | solution.py:459
  36.7 3.5 %copy.66.t_ref = f32[32,90,128]{2,1,0:T(8,128)} copy(f32[32,90,128]{2,0,1:T(8,128)} %reshape.100) | data formatting | bytes 2949120 | tf_op jit(solution)/shard_map/reshape | solution.py:459
  40.5 1.1 fusion.25
  41.5 0.2 maximum_maximum_fusion.1
  42.1 0.8 copy-done
  42.9 0.5 copy-done.6
  43.6 3.1 %collective-permute-start.2 = (f32[2,45,928]{2,1,0:T(8,128)S(1)}, f32[2,45,928]{2,1,0:T(8,128)S(1)}, u32[]{:S(2)}, u32[]{:S(2)}) collective-permute-start(f32[2,45,928]{2,1,0:T(8,128)S(1)} %get-tuple-element.52), channel_id=1, source_target_pairs={{0,32},{32,64},{64,96},{96,128},{128,160},{160,192},{192,224},{224... | collective-permute-start | bytes 1002248 | tf_op jit(solution)/shard_map/ppermute | solution.py:23
  46.8 2.1 %collective-permute-start.3 = (f32[2,45,928]{2,1,0:T(8,128)S(1)}, f32[2,45,928]{2,1,0:T(8,128)S(1)}, u32[]{:S(2)}, u32[]{:S(2)}) collective-permute-start(f32[2,45,928]{2,1,0:T(8,128)S(1)} %get-tuple-element.53), channel_id=1, source_target_pairs={{32,0},{64,32},{96,64},{128,96},{160,128},{192,160},{224,192},{256... | collective-permute-start | bytes 1002248 | tf_op jit(solution)/shard_map/ppermute | solution.py:25
  48.9 0.9 fusion.21.group_ref
  49.9 1.6 collective-permute-done.2
  51.5 4.4 %collective-permute-done.3 = f32[2,45,928]{2,1,0:T(8,128)S(1)} collective-permute-done((f32[2,45,928]{2,1,0:T(8,128)S(1)}, f32[2,45,928]{2,1,0:T(8,128)S(1)}, u32[]{:S(2)}, u32[]{:S(2)}) %collective-permute-start.3) | collective-permute-done | bytes 334112 | tf_op jit(solution)/shard_map/ppermute | solution.py:25
  56.2 1.2 fusion.23
  57.4 0.3 maximum_maximum_fusion
  57.8 0.4 fusion
  58.2 1.0 copy-done.5
  59.2 1.1 slice_select_fusion
  60.3 16.9 %shard_map.105 = (f32[4,45,864]{2,1,0:T(8,128)}, f32[4,45,864]{2,1,0:T(8,128)}) custom-call(f32[4,45,864]{2,1,0:T(8,128)} %copy-done.4, f32[4,45,32]{2,1,0:T(8,128)} %copy-done.7, f32[4,45,864]{2,1,0:T(8,128)} %copy.61.cot_ref, f32[1,864]{1,0:T(1,128)} %broadcast_in_dim_tile.3.sat_ref, f32[32,864]{1,0:T(8,128)} %fusion.46.spread_ref, f32[864,32]{1,0:T(8,128)} %fusion.21.group_ref), custom_call_target="tpu_custom_call" | custom-call | tf_op jit(solution)/shard_map/pallas_call | solution.py:597
  77.2 4.5 %shard_map.104 = (f32[2,45,864]{2,1,0:T(8,128)}, f32[2,45,864]{2,1,0:T(8,128)}) custom-call(f32[2,45,864]{2,1,0:T(8,128)} %get-tuple-element.61.x_ref, f32[2,45,864]{2,1,0:T(8,128)} %get-tuple-element.60.c_ref, f32[2,45,32]{2,1,0:T(8,128)} %slice_select_fusion.6.s_ref, f32[1,128]{1,0:T(1,128)} %select_n.189.w_ref, f32[1,90]{1,0:T(1,128)} %broadcast_in_dim_reshape.3.m_ref, ...), custom_call_target="tpu_custom_call" | custom-call | tf_op jit(solution)/shard_map/pallas_call | solution.py:469
  81.8 1.0 slice_select_fusion.3
  82.9 0.3 fusion.5
  83.5 2.1 %collective-permute-start.4 = (f32[2,45,864]{2,1,0:T(8,128)S(1)}, f32[2,45,864]{2,1,0:T(8,128)S(1)}, u32[]{:S(2)}, u32[]{:S(2)}) collective-permute-start(f32[2,45,864]{2,1,0:T(8,128)S(1)} %slice.260), channel_id=1, source_target_pairs={{0,32},{32,64},{64,96},{96,128},{128,160},{160,192},{192,224},{224... | collective-permute-start | bytes 933128 | tf_op jit(solution)/shard_map/ppermute | solution.py:23
  85.5 73.4 %collective-permute-done.4 = f32[2,45,864]{2,1,0:T(8,128)S(1)} collective-permute-done((f32[2,45,864]{2,1,0:T(8,128)S(1)}, f32[2,45,864]{2,1,0:T(8,128)S(1)}, u32[]{:S(2)}, u32[]{:S(2)}) %collective-permute-start.4) | collective-permute-done | bytes 311072 | tf_op jit(solution)/shard_map/ppermute | solution.py:23
  159.0 2.0 %collective-permute-start.5 = (f32[2,45,864]{2,1,0:T(8,128)S(1)}, f32[2,45,864]{2,1,0:T(8,128)S(1)}, u32[]{:S(2)}, u32[]{:S(2)}) collective-permute-start(f32[2,45,864]{2,1,0:T(8,128)S(1)} %get-tuple-element.41), channel_id=1, source_target_pairs={{32,0},{64,32},{96,64},{128,96},{160,128},{192,160},{224,192},{256... | collective-permute-start | bytes 933128 | tf_op jit(solution)/shard_map/ppermute | solution.py:25
  161.2 1.1 copy.69
  162.3 5.3 %collective-permute-done.5 = f32[2,45,864]{2,1,0:T(8,128)S(1)} collective-permute-done((f32[2,45,864]{2,1,0:T(8,128)S(1)}, f32[2,45,864]{2,1,0:T(8,128)S(1)}, u32[]{:S(2)}, u32[]{:S(2)}) %collective-permute-start.5) | collective-permute-done | bytes 311072 | tf_op jit(solution)/shard_map/ppermute | solution.py:25
  168.0 1.9 %collective-permute-start.6 = (f32[4,2,864]{2,1,0:T(2,128)S(1)}, f32[4,2,864]{2,1,0:T(2,128)S(1)}, u32[]{:S(2)}, u32[]{:S(2)}) collective-permute-start(f32[4,2,864]{2,1,0:T(2,128)S(1)} %get-tuple-element.38), channel_id=1, source_target_pairs={{0,1},{1,2},{2,3},{3,4},{4,5},{5,6},{6,7},{7,8},{8,9},{9,10},{10,1... | collective-permute-start | bytes 82952 | tf_op jit(solution)/shard_map/ppermute | solution.py:23
  169.9 7.0 %collective-permute-start.7 = (f32[4,2,864]{2,1,0:T(2,128)S(1)}, f32[4,2,864]{2,1,0:T(2,128)S(1)}, u32[]{:S(2)}, u32[]{:S(2)}) collective-permute-start(f32[4,2,864]{2,1,0:T(2,128)S(1)} %get-tuple-element.39), channel_id=1, source_target_pairs={{1,0},{2,1},{3,2},{4,3},{5,4},{6,5},{7,6},{8,7},{9,8},{10,9},{11,1... | collective-permute-start | bytes 82952 | tf_op jit(solution)/shard_map/ppermute | solution.py:25
  176.9 0.3 pad_add_fusion.2
  177.4 0.5 collective-permute-done.7
  178.1 1.1 copy.70
  (68 shorter events, 3.0 us)
Async XLA Ops:
  0.6 21.2 %copy-start.11 = (f32[4,45,32]{1,2,0:T(8,128)S(1)}, f32[4,45,32]{1,2,0:T(8,128)}, u32[]{:S(2)}) copy-start(f32[4,45,32]{1,2,0:T(8,128)} %param.15) | copy-start | bytes 69124
  1.5 20.5 %copy-start.13 = (s32[4]{0:T(128)S(1)}, s32[4]{0:T(128)}, u32[]{:S(2)}) copy-start(s32[4]{0:T(128)} %param.14) | copy-start | bytes 52
  3.7 0.9 copy-start.2
  5.3 34.9 %collective-permute-start = (f32[4,2,928]{2,1,0:T(2,128)}, f32[4,2,928]{2,1,0:T(2,128)S(1)}, u32[]{:S(2)}, u32[]{:S(2)}) collective-permute-start(f32[4,2,928]{2,1,0:T(2,128)} %get-tuple-element.50), channel_id=1, source_target_pairs={{0,1},{1,2},{2,3},{3,4},{4,5},{5,6},{6,7},{7,8},{8,9},{9,10},{10,1... | collective-permute-start | bytes 89096 | tf_op jit(solution)/shard_map/ppermute | solution.py:23
  9.6 30.6 %collective-permute-start.1 = (f32[4,2,928]{2,1,0:T(2,128)S(1)}, f32[4,2,928]{2,1,0:T(2,128)S(1)}, u32[]{:S(2)}, u32[]{:S(2)}) collective-permute-start(f32[4,2,928]{2,1,0:T(2,128)S(1)} %get-tuple-element.51), channel_id=1, source_target_pairs={{1,0},{2,1},{3,2},{4,3},{5,4},{6,5},{7,6},{8,7},{9,8},{10,9},{11,1... | collective-permute-start | bytes 89096 | tf_op jit(solution)/shard_map/ppermute | solution.py:25
  22.0 4.7 %copy-start.7 = (f32[4,45,32]{2,1,0:T(8,128)}, f32[4,45,32]{2,1,0:T(8,128)S(1)}, u32[]{:S(2)}) copy-start(f32[4,45,32]{2,1,0:T(8,128)S(1)} %copy.63.seed_ref) | copy-start | bytes 69124
  26.7 1.6 copy-start.14
  26.7 4.3 %copy-start.12 = (s32[4,45,32]{1,2,0:T(8,128)S(1)}, s32[4,45,32]{1,2,0:T(8,128)}, u32[]{:S(2)}) copy-start(s32[4,45,32]{1,2,0:T(8,128)} %param.13) | copy-start | bytes 69124
  36.7 3.5 %copy-start.3 = (f32[4,45,864]{2,1,0:T(8,128)S(1)}, f32[4,45,864]{2,1,0:T(8,128)}, u32[]{:S(2)}) copy-start(f32[4,45,864]{2,1,0:T(8,128)} %copy-done.2) | copy-start | bytes 1866244
  41.5 1.4 copy-start
  41.8 1.6 copy-start.6
  43.6 7.8 %collective-permute-start.2 = (f32[2,45,928]{2,1,0:T(8,128)S(1)}, f32[2,45,928]{2,1,0:T(8,128)S(1)}, u32[]{:S(2)}, u32[]{:S(2)}) collective-permute-start(f32[2,45,928]{2,1,0:T(8,128)S(1)} %get-tuple-element.52), channel_id=1, source_target_pairs={{0,32},{32,64},{64,96},{96,128},{128,160},{160,192},{192,224},{224... | collective-permute-start | bytes 1002248 | tf_op jit(solution)/shard_map/ppermute | solution.py:23
  46.8 9.1 %collective-permute-start.3 = (f32[2,45,928]{2,1,0:T(8,128)S(1)}, f32[2,45,928]{2,1,0:T(8,128)S(1)}, u32[]{:S(2)}, u32[]{:S(2)}) collective-permute-start(f32[2,45,928]{2,1,0:T(8,128)S(1)} %get-tuple-element.53), channel_id=1, source_target_pairs={{32,0},{64,32},{96,64},{128,96},{160,128},{192,160},{224,192},{256... | collective-permute-start | bytes 1002248 | tf_op jit(solution)/shard_map/ppermute | solution.py:25
  58.1 1.1 copy-start.5
  59.2 1.1 copy-start.4
  77.2 4.6 %copy-start.9 = (f32[4,45,864]{2,1,0:T(8,128)S(1)}, f32[4,45,864]{2,1,0:T(8,128)}, u32[]{:S(2)}) copy-start(f32[4,45,864]{2,1,0:T(8,128)} %get-tuple-element.9) | copy-start | bytes 1866244
  83.4 77.6 %copy-start.8 = (f32[4,45,864]{2,1,0:T(8,128)S(1)}, f32[4,45,864]{2,1,0:T(8,128)}, u32[]{:S(2)}) copy-start(f32[4,45,864]{2,1,0:T(8,128)} %get-tuple-element.7) | copy-start | bytes 1866244
  83.4 77.6 %copy-start.10 = (f32[2,45,864]{2,1,0:T(8,128)S(1)}, f32[2,45,864]{2,1,0:T(8,128)}, u32[]{:S(2)}) copy-start(f32[2,45,864]{2,1,0:T(8,128)} %get-tuple-element.6) | copy-start | bytes 933124
  83.5 75.4 %collective-permute-start.4 = (f32[2,45,864]{2,1,0:T(8,128)S(1)}, f32[2,45,864]{2,1,0:T(8,128)S(1)}, u32[]{:S(2)}, u32[]{:S(2)}) collective-permute-start(f32[2,45,864]{2,1,0:T(8,128)S(1)} %slice.260), channel_id=1, source_target_pairs={{0,32},{32,64},{64,96},{96,128},{128,160},{160,192},{192,224},{224... | collective-permute-start | bytes 933128 | tf_op jit(solution)/shard_map/ppermute | solution.py:23
  159.0 8.6 %collective-permute-start.5 = (f32[2,45,864]{2,1,0:T(8,128)S(1)}, f32[2,45,864]{2,1,0:T(8,128)S(1)}, u32[]{:S(2)}, u32[]{:S(2)}) collective-permute-start(f32[2,45,864]{2,1,0:T(8,128)S(1)} %get-tuple-element.41), channel_id=1, source_target_pairs={{32,0},{64,32},{96,64},{128,96},{160,128},{192,160},{224,192},{256... | collective-permute-start | bytes 933128 | tf_op jit(solution)/shard_map/ppermute | solution.py:25
  162.3 5.4 %copy-start.1 = (f32[3,4,46,864]{3,2,1,0:T(8,128)S(1)}, f32[3,4,46,864]{3,2,1,0:T(8,128)}, u32[]{:S(2)}) copy-start(f32[3,4,46,864]{3,2,1,0:T(8,128)} %copy-done) | copy-start | bytes 5723140
  168.0 9.3 %collective-permute-start.6 = (f32[4,2,864]{2,1,0:T(2,128)S(1)}, f32[4,2,864]{2,1,0:T(2,128)S(1)}, u32[]{:S(2)}, u32[]{:S(2)}) collective-permute-start(f32[4,2,864]{2,1,0:T(2,128)S(1)} %get-tuple-element.38), channel_id=1, source_target_pairs={{0,1},{1,2},{2,3},{3,4},{4,5},{5,6},{6,7},{7,8},{8,9},{9,10},{10,1... | collective-permute-start | bytes 82952 | tf_op jit(solution)/shard_map/ppermute | solution.py:23
  169.9 7.9 %collective-permute-start.7 = (f32[4,2,864]{2,1,0:T(2,128)S(1)}, f32[4,2,864]{2,1,0:T(2,128)S(1)}, u32[]{:S(2)}, u32[]{:S(2)}) collective-permute-start(f32[4,2,864]{2,1,0:T(2,128)S(1)} %get-tuple-element.39), channel_id=1, source_target_pairs={{1,0},{2,1},{3,2},{4,3},{5,4},{6,5},{7,6},{8,7},{9,8},{10,9},{11,1... | collective-permute-start | bytes 82952 | tf_op jit(solution)/shard_map/ppermute | solution.py:25

commit v6 on v5

--- a/solution.py
+++ b/solution.py
@@ -388,7 +388,7 @@
                                  preferred_element_type=jnp.float32)
 
         zero = jnp.zeros((padded, t_ref.shape[2]), jnp.float32)
-        coefficient = lax.fori_loop(0, count, analyse, zero, unroll=8) * w_ref[...]
+        coefficient = lax.fori_loop(0, count, analyse, zero, unroll=True) * w_ref[...]
         keep_lane = m_ref[...] > 0.5
         species_row = lax.broadcasted_iota(jnp.int32, (padded, lanes), 0)
         valid = species_row < chunk
@@ -400,7 +400,7 @@
             field_s[s] = jnp.where(keep_lane, smooth, land_go[s, 0:padded, :])
             return carry
 
-        lax.fori_loop(0, count, smooth_out, 0, unroll=8)
+        lax.fori_loop(0, count, smooth_out, 0, unroll=True)
         particle, gradient = column_chemistry(
             field_s[...],
             land_go[:, chunk : chunk + 1, :],
@@ -415,7 +415,7 @@
             return acc + jnp.dot(field_s[s], t_ref[s], precision=hi,
                                  preferred_element_type=jnp.float32)
 
-        adjoint_coef = lax.fori_loop(0, count, gather_adjoint, zero, unroll=8) * w_ref[...]
+        adjoint_coef = lax.fori_loop(0, count, gather_adjoint, zero, unroll=True) * w_ref[...]
 
         def synthesise(s, carry):
             smooth = lax.dot_general(adjoint_coef, t_ref[s], nt, precision=hi,
@@ -423,7 +423,7 @@
             out_back[s, padded:, :] = jnp.where(keep_lane, smooth, field_s[s])
             return carry
 
-        lax.fori_loop(0, count, synthesise, 0, unroll=8)
+        lax.fori_loop(0, count, synthesise, 0, unroll=True)
         round_trip(out_back, land_back, sem_c, sem_d)
         particle_back = land_back[:, 0:padded, :].reshape(count * padded, lanes)
         gradient_back = land_back[:, padded:, :].reshape(count * padded, lanes)

time: 180 us -> 181 us (level)
  no operation moved by 1% of the time
where the time goes in v6:
time: 181 us; the launch traced here: 180 us
  waiting for transfers between devices  86 us (48%)
  starting transfers between devices  34.7 us (19%)
  Pallas kernels  21.5 us (12%)
  local copies, waits for them, and re-layouts  19.6 us (11%)
  other arithmetic  14.8 us (8%)
  matrix products  2.3 us (1%)
    ppermute x4, waiting for transfers between devices, with_halo(): lax.ppermute(tail, axis, [(i, (i + 1) % count) for i in range(ends)])  75.8 us
    ppermute x4, starting transfers between devices, with_halo(): lax.ppermute(head, axis, [((i + 1) % count, i) for i in range(ends)])  23.2 us
    pallas_call x1, Pallas kernels, chemistry_step(): pl.pallas_call(chem_kernel, grid=(rows,), in_specs=[big, small, big, pl.B...  16.9 us
    ppermute x4, starting transfers between devices, with_halo(): lax.ppermute(tail, axis, [(i, (i + 1) % count) for i in range(ends)])  11.5 us
    unnamed x37, local copies, waits for them, and re-layouts  10.5 us
    ppermute x4, waiting for transfers between devices, with_halo(): lax.ppermute(head, axis, [((i + 1) % count, i) for i in range(ends)])  10.2 us
    reshape x2, local copies, waits for them, and re-layouts, polar_step(): blocks = jnp.einsum('sjk,rR->srjRk', table, jnp.eye(polar_count, dtype=jn...  6.05 us
    pallas_call x1, Pallas kernels, polar_step(): pl.pallas_call(owner_kernel, out_shape=[end_shape, end_shape], in_specs=[...  4.54 us
  transfers between devices with their start and end apart: 8, of which 5 were waited for; matrix products, arithmetic and copies ran while one was open for 12% of the time, Pallas kernels for 0%

profile of v6, /device:TPU:1, one launch (start us, length us, event | category | flops | bytes accessed | tf_op | source)
XLA Modules:
  0.0 180.0 jit_solution(16123871855637904544)
XLA Ops:
  0.6 0.9 convert_element_type.30
  1.6 1.0 copy.51
  2.6 1.1 copy.56
  3.7 0.8 copy-done.2
  4.6 0.7 pad_maximum_fusion.19
  5.3 4.4 %collective-permute-start = (f32[4,2,928]{2,1,0:T(2,128)}, f32[4,2,928]{2,1,0:T(2,128)S(1)}, u32[]{:S(2)}, u32[]{:S(2)}) collective-permute-start(f32[4,2,928]{2,1,0:T(2,128)} %get-tuple-element.50), channel_id=1, source_target_pairs={{0,1},{1,2},{2,3},{3,4},{4,5},{5,6},{6,7},{7,8},{8,9},{9,10},{10,1... | collective-permute-start | bytes 89096 | tf_op jit(solution)/shard_map/ppermute | solution.py:23
  9.6 12.1 %collective-permute-start.1 = (f32[4,2,928]{2,1,0:T(2,128)S(1)}, f32[4,2,928]{2,1,0:T(2,128)S(1)}, u32[]{:S(2)}, u32[]{:S(2)}) collective-permute-start(f32[4,2,928]{2,1,0:T(2,128)S(1)} %get-tuple-element.51), channel_id=1, source_target_pairs={{1,0},{2,1},{3,2},{4,3},{5,4},{6,5},{7,6},{8,7},{9,8},{10,9},{11,1... | collective-permute-start | bytes 89096 | tf_op jit(solution)/shard_map/ppermute | solution.py:25
  22.1 0.6 slice_select_fusion.6.s_ref
  22.7 0.6 fusion.46.spread_ref
  23.3 3.1 %fusion.11 = (f32[32,45,32]{2,0,1:T(8,128)S(1)}, f32[32,45,32]{2,0,1:T(8,128)S(1)}) fusion(s32[32,45]{0,1:T(8,128)S(1)} %multiply_add_fusion), kind=kLoop, calls=%fused_computation.29 | loop fusion | flops 414720 | bytes 374400 | tf_op jit(solution)/shard_map/cos | solution.py:154
  26.4 0.3 pad_maximum_fusion.3
  26.7 1.5 multiply_bitcast_fusion
  28.4 0.6 select_n.189.w_ref
  29.0 0.7 broadcast_in_dim_reshape.3.m_ref
  29.7 0.7 copy.65.v_ref
  30.4 0.7 broadcast_in_dim_tile.3.sat_ref
  31.2 1.0 copy.57
  32.1 2.0 %copy.61.cot_ref = f32[4,45,864]{2,1,0:T(8,128)} copy(f32[4,45,864]{2,0,1:T(4,128)} %param.17) | data formatting | bytes 1244160 | tf_op args[8]
  34.1 2.6 %reshape.100 = f32[32,90,128]{2,0,1:T(8,128)} reshape(f32[32,2,45,2,64]{4,3,0,2,1:T(2,128)S(1)} %multiply_bitcast_fusion) | data formatting | bytes 2949120 | tf_op jit(solution)/shard_map/reshape | solution.py:459
  36.7 3.5 %copy.66.t_ref = f32[32,90,128]{2,1,0:T(8,128)} copy(f32[32,90,128]{2,0,1:T(8,128)} %reshape.100) | data formatting | bytes 2949120 | tf_op jit(solution)/shard_map/reshape | solution.py:459
  40.5 1.1 fusion.25
  41.5 0.2 maximum_maximum_fusion.1
  42.1 0.8 copy-done
  42.9 0.5 copy-done.6
  43.6 3.1 %collective-permute-start.2 = (f32[2,45,928]{2,1,0:T(8,128)S(1)}, f32[2,45,928]{2,1,0:T(8,128)S(1)}, u32[]{:S(2)}, u32[]{:S(2)}) collective-permute-start(f32[2,45,928]{2,1,0:T(8,128)S(1)} %get-tuple-element.52), channel_id=1, source_target_pairs={{0,32},{32,64},{64,96},{96,128},{128,160},{160,192},{192,224},{224... | collective-permute-start | bytes 1002248 | tf_op jit(solution)/shard_map/ppermute | solution.py:23
  46.8 2.1 %collective-permute-start.3 = (f32[2,45,928]{2,1,0:T(8,128)S(1)}, f32[2,45,928]{2,1,0:T(8,128)S(1)}, u32[]{:S(2)}, u32[]{:S(2)}) collective-permute-start(f32[2,45,928]{2,1,0:T(8,128)S(1)} %get-tuple-element.53), channel_id=1, source_target_pairs={{32,0},{64,32},{96,64},{128,96},{160,128},{192,160},{224,192},{256... | collective-permute-start | bytes 1002248 | tf_op jit(solution)/shard_map/ppermute | solution.py:25
  48.9 0.9 fusion.21.group_ref
  49.9 1.6 collective-permute-done.2
  51.5 4.4 %collective-permute-done.3 = f32[2,45,928]{2,1,0:T(8,128)S(1)} collective-permute-done((f32[2,45,928]{2,1,0:T(8,128)S(1)}, f32[2,45,928]{2,1,0:T(8,128)S(1)}, u32[]{:S(2)}, u32[]{:S(2)}) %collective-permute-start.3) | collective-permute-done | bytes 334112 | tf_op jit(solution)/shard_map/ppermute | solution.py:25
  56.2 1.2 fusion.23
  57.4 0.3 maximum_maximum_fusion
  57.8 0.4 fusion
  58.2 1.0 copy-done.5
  59.2 1.1 slice_select_fusion
  60.4 16.9 %shard_map.105 = (f32[4,45,864]{2,1,0:T(8,128)}, f32[4,45,864]{2,1,0:T(8,128)}) custom-call(f32[4,45,864]{2,1,0:T(8,128)} %copy-done.4, f32[4,45,32]{2,1,0:T(8,128)} %copy-done.7, f32[4,45,864]{2,1,0:T(8,128)} %copy.61.cot_ref, f32[1,864]{1,0:T(1,128)} %broadcast_in_dim_tile.3.sat_ref, f32[32,864]{1,0:T(8,128)} %fusion.46.spread_ref, f32[864,32]{1,0:T(8,128)} %fusion.21.group_ref), custom_call_target="tpu_custom_call" | custom-call | tf_op jit(solution)/shard_map/pallas_call | solution.py:597
  77.3 4.5 %shard_map.104 = (f32[2,45,864]{2,1,0:T(8,128)}, f32[2,45,864]{2,1,0:T(8,128)}) custom-call(f32[2,45,864]{2,1,0:T(8,128)} %get-tuple-element.61.x_ref, f32[2,45,864]{2,1,0:T(8,128)} %get-tuple-element.60.c_ref, f32[2,45,32]{2,1,0:T(8,128)} %slice_select_fusion.6.s_ref, f32[1,128]{1,0:T(1,128)} %select_n.189.w_ref, f32[1,90]{1,0:T(1,128)} %broadcast_in_dim_reshape.3.m_ref, ...), custom_call_target="tpu_custom_call" | custom-call | tf_op jit(solution)/shard_map/pallas_call | solution.py:469
  81.8 1.0 slice_select_fusion.3
  83.0 0.3 fusion.5
  83.6 2.1 %collective-permute-start.4 = (f32[2,45,864]{2,1,0:T(8,128)S(1)}, f32[2,45,864]{2,1,0:T(8,128)S(1)}, u32[]{:S(2)}, u32[]{:S(2)}) collective-permute-start(f32[2,45,864]{2,1,0:T(8,128)S(1)} %slice.260), channel_id=1, source_target_pairs={{0,32},{32,64},{64,96},{96,128},{128,160},{160,192},{192,224},{224... | collective-permute-start | bytes 933128 | tf_op jit(solution)/shard_map/ppermute | solution.py:23
  85.6 74.1 %collective-permute-done.4 = f32[2,45,864]{2,1,0:T(8,128)S(1)} collective-permute-done((f32[2,45,864]{2,1,0:T(8,128)S(1)}, f32[2,45,864]{2,1,0:T(8,128)S(1)}, u32[]{:S(2)}, u32[]{:S(2)}) %collective-permute-start.4) | collective-permute-done | bytes 311072 | tf_op jit(solution)/shard_map/ppermute | solution.py:23
  159.8 2.0 %collective-permute-start.5 = (f32[2,45,864]{2,1,0:T(8,128)S(1)}, f32[2,45,864]{2,1,0:T(8,128)S(1)}, u32[]{:S(2)}, u32[]{:S(2)}) collective-permute-start(f32[2,45,864]{2,1,0:T(8,128)S(1)} %get-tuple-element.41), channel_id=1, source_target_pairs={{32,0},{64,32},{96,64},{128,96},{160,128},{192,160},{224,192},{256... | collective-permute-start | bytes 933128 | tf_op jit(solution)/shard_map/ppermute | solution.py:25
  162.0 1.1 copy.69
  163.1 5.3 %collective-permute-done.5 = f32[2,45,864]{2,1,0:T(8,128)S(1)} collective-permute-done((f32[2,45,864]{2,1,0:T(8,128)S(1)}, f32[2,45,864]{2,1,0:T(8,128)S(1)}, u32[]{:S(2)}, u32[]{:S(2)}) %collective-permute-start.5) | collective-permute-done | bytes 311072 | tf_op jit(solution)/shard_map/ppermute | solution.py:25
  168.8 1.9 %collective-permute-start.6 = (f32[4,2,864]{2,1,0:T(2,128)S(1)}, f32[4,2,864]{2,1,0:T(2,128)S(1)}, u32[]{:S(2)}, u32[]{:S(2)}) collective-permute-start(f32[4,2,864]{2,1,0:T(2,128)S(1)} %get-tuple-element.38), channel_id=1, source_target_pairs={{0,1},{1,2},{2,3},{3,4},{4,5},{5,6},{6,7},{7,8},{8,9},{9,10},{10,1... | collective-permute-start | bytes 82952 | tf_op jit(solution)/shard_map/ppermute | solution.py:23
  170.7 7.0 %collective-permute-start.7 = (f32[4,2,864]{2,1,0:T(2,128)S(1)}, f32[4,2,864]{2,1,0:T(2,128)S(1)}, u32[]{:S(2)}, u32[]{:S(2)}) collective-permute-start(f32[4,2,864]{2,1,0:T(2,128)S(1)} %get-tuple-element.39), channel_id=1, source_target_pairs={{1,0},{2,1},{3,2},{4,3},{5,4},{6,5},{7,6},{8,7},{9,8},{10,9},{11,1... | collective-permute-start | bytes 82952 | tf_op jit(solution)/shard_map/ppermute | solution.py:25
  177.7 0.3 pad_add_fusion.2
  178.2 0.5 collective-permute-done.7
  178.9 1.1 copy.70
  (68 shorter events, 3.0 us)
Async XLA Ops:
  0.6 21.2 %copy-start.11 = (f32[4,45,32]{1,2,0:T(8,128)S(1)}, f32[4,45,32]{1,2,0:T(8,128)}, u32[]{:S(2)}) copy-start(f32[4,45,32]{1,2,0:T(8,128)} %param.15) | copy-start | bytes 69124
  1.5 20.5 %copy-start.13 = (s32[4]{0:T(128)S(1)}, s32[4]{0:T(128)}, u32[]{:S(2)}) copy-start(s32[4]{0:T(128)} %param.14) | copy-start | bytes 52
  3.7 0.9 copy-start.2
  5.3 34.9 %collective-permute-start = (f32[4,2,928]{2,1,0:T(2,128)}, f32[4,2,928]{2,1,0:T(2,128)S(1)}, u32[]{:S(2)}, u32[]{:S(2)}) collective-permute-start(f32[4,2,928]{2,1,0:T(2,128)} %get-tuple-element.50), channel_id=1, source_target_pairs={{0,1},{1,2},{2,3},{3,4},{4,5},{5,6},{6,7},{7,8},{8,9},{9,10},{10,1... | collective-permute-start | bytes 89096 | tf_op jit(solution)/shard_map/ppermute | solution.py:23
  9.6 30.6 %collective-permute-start.1 = (f32[4,2,928]{2,1,0:T(2,128)S(1)}, f32[4,2,928]{2,1,0:T(2,128)S(1)}, u32[]{:S(2)}, u32[]{:S(2)}) collective-permute-start(f32[4,2,928]{2,1,0:T(2,128)S(1)} %get-tuple-element.51), channel_id=1, source_target_pairs={{1,0},{2,1},{3,2},{4,3},{5,4},{6,5},{7,6},{8,7},{9,8},{10,9},{11,1... | collective-permute-start | bytes 89096 | tf_op jit(solution)/shard_map/ppermute | solution.py:25
  22.0 4.7 %copy-start.7 = (f32[4,45,32]{2,1,0:T(8,128)}, f32[4,45,32]{2,1,0:T(8,128)S(1)}, u32[]{:S(2)}) copy-start(f32[4,45,32]{2,1,0:T(8,128)S(1)} %copy.63.seed_ref) | copy-start | bytes 69124
  26.7 1.6 copy-start.14
  26.7 4.3 %copy-start.12 = (s32[4,45,32]{1,2,0:T(8,128)S(1)}, s32[4,45,32]{1,2,0:T(8,128)}, u32[]{:S(2)}) copy-start(s32[4,45,32]{1,2,0:T(8,128)} %param.13) | copy-start | bytes 69124
  36.7 3.5 %copy-start.3 = (f32[4,45,864]{2,1,0:T(8,128)S(1)}, f32[4,45,864]{2,1,0:T(8,128)}, u32[]{:S(2)}) copy-start(f32[4,45,864]{2,1,0:T(8,128)} %copy-done.2) | copy-start | bytes 1866244
  41.5 1.4 copy-start
  41.8 1.6 copy-start.6
  43.6 7.8 %collective-permute-start.2 = (f32[2,45,928]{2,1,0:T(8,128)S(1)}, f32[2,45,928]{2,1,0:T(8,128)S(1)}, u32[]{:S(2)}, u32[]{:S(2)}) collective-permute-start(f32[2,45,928]{2,1,0:T(8,128)S(1)} %get-tuple-element.52), channel_id=1, source_target_pairs={{0,32},{32,64},{64,96},{96,128},{128,160},{160,192},{192,224},{224... | collective-permute-start | bytes 1002248 | tf_op jit(solution)/shard_map/ppermute | solution.py:23
  46.8 9.1 %collective-permute-start.3 = (f32[2,45,928]{2,1,0:T(8,128)S(1)}, f32[2,45,928]{2,1,0:T(8,128)S(1)}, u32[]{:S(2)}, u32[]{:S(2)}) collective-permute-start(f32[2,45,928]{2,1,0:T(8,128)S(1)} %get-tuple-element.53), channel_id=1, source_target_pairs={{32,0},{64,32},{96,64},{128,96},{160,128},{192,160},{224,192},{256... | collective-permute-start | bytes 1002248 | tf_op jit(solution)/shard_map/ppermute | solution.py:25
  58.1 1.1 copy-start.5
  59.2 1.1 copy-start.4
  77.3 4.6 %copy-start.9 = (f32[4,45,864]{2,1,0:T(8,128)S(1)}, f32[4,45,864]{2,1,0:T(8,128)}, u32[]{:S(2)}) copy-start(f32[4,45,864]{2,1,0:T(8,128)} %get-tuple-element.9) | copy-start | bytes 1866244
  83.5 78.3 %copy-start.8 = (f32[4,45,864]{2,1,0:T(8,128)S(1)}, f32[4,45,864]{2,1,0:T(8,128)}, u32[]{:S(2)}) copy-start(f32[4,45,864]{2,1,0:T(8,128)} %get-tuple-element.7) | copy-start | bytes 1866244
  83.5 78.3 %copy-start.10 = (f32[2,45,864]{2,1,0:T(8,128)S(1)}, f32[2,45,864]{2,1,0:T(8,128)}, u32[]{:S(2)}) copy-start(f32[2,45,864]{2,1,0:T(8,128)} %get-tuple-element.6) | copy-start | bytes 933124
  83.6 76.2 %collective-permute-start.4 = (f32[2,45,864]{2,1,0:T(8,128)S(1)}, f32[2,45,864]{2,1,0:T(8,128)S(1)}, u32[]{:S(2)}, u32[]{:S(2)}) collective-permute-start(f32[2,45,864]{2,1,0:T(8,128)S(1)} %slice.260), channel_id=1, source_target_pairs={{0,32},{32,64},{64,96},{96,128},{128,160},{160,192},{192,224},{224... | collective-permute-start | bytes 933128 | tf_op jit(solution)/shard_map/ppermute | solution.py:23
  159.8 8.6 %collective-permute-start.5 = (f32[2,45,864]{2,1,0:T(8,128)S(1)}, f32[2,45,864]{2,1,0:T(8,128)S(1)}, u32[]{:S(2)}, u32[]{:S(2)}) collective-permute-start(f32[2,45,864]{2,1,0:T(8,128)S(1)} %get-tuple-element.41), channel_id=1, source_target_pairs={{32,0},{64,32},{96,64},{128,96},{160,128},{192,160},{224,192},{256... | collective-permute-start | bytes 933128 | tf_op jit(solution)/shard_map/ppermute | solution.py:25
  163.1 5.4 %copy-start.1 = (f32[3,4,46,864]{3,2,1,0:T(8,128)S(1)}, f32[3,4,46,864]{3,2,1,0:T(8,128)}, u32[]{:S(2)}) copy-start(f32[3,4,46,864]{3,2,1,0:T(8,128)} %copy-done) | copy-start | bytes 5723140
  168.8 9.3 %collective-permute-start.6 = (f32[4,2,864]{2,1,0:T(2,128)S(1)}, f32[4,2,864]{2,1,0:T(2,128)S(1)}, u32[]{:S(2)}, u32[]{:S(2)}) collective-permute-start(f32[4,2,864]{2,1,0:T(2,128)S(1)} %get-tuple-element.38), channel_id=1, source_target_pairs={{0,1},{1,2},{2,3},{3,4},{4,5},{5,6},{6,7},{7,8},{8,9},{9,10},{10,1... | collective-permute-start | bytes 82952 | tf_op jit(solution)/shard_map/ppermute | solution.py:23
  170.7 7.9 %collective-permute-start.7 = (f32[4,2,864]{2,1,0:T(2,128)S(1)}, f32[4,2,864]{2,1,0:T(2,128)S(1)}, u32[]{:S(2)}, u32[]{:S(2)}) collective-permute-start(f32[4,2,864]{2,1,0:T(2,128)S(1)} %get-tuple-element.39), channel_id=1, source_target_pairs={{1,0},{2,1},{3,2},{4,3},{5,4},{6,5},{7,6},{8,7},{9,8},{10,9},{11,1... | collective-permute-start | bytes 82952 | tf_op jit(solution)/shard_map/ppermute | solution.py:25

commit v7 on v5

--- a/solution.py
+++ b/solution.py
@@ -529,20 +529,21 @@
     band = lax.axis_index("lat")
     bands = lax.axis_size("lat")
     polar = jnp.logical_or(
-        jnp.logical_and(band == 0, row < POLAR),
-        jnp.logical_and(band == bands - 1, row >= rows - POLAR),
+        jnp.logical_and(band == 0, row == 0),
+        jnp.logical_and(band == bands - 1, row == rows - 1),
     )
 
     @pl.when(jnp.logical_not(polar))
     def _():
-        chem_body(x_ref, seed_ref, cot_ref, sat_ref, spread_ref, group_ref, p_ref, g_ref)
-
-
-def chem_body(x_ref, seed_ref, cot_ref, sat_ref, spread_ref, group_ref, p_ref, g_ref):
+        for part in range(POLAR):
+            chem_body(part, x_ref, seed_ref, cot_ref, sat_ref, spread_ref, group_ref, p_ref, g_ref)
+
+
+def chem_body(part, x_ref, seed_ref, cot_ref, sat_ref, spread_ref, group_ref, p_ref, g_ref):
     hi = lax.Precision.HIGHEST
-    x = x_ref[0]
-    seed = seed_ref[0]
-    cot = cot_ref[0]
+    x = x_ref[part]
+    seed = seed_ref[part]
+    cot = cot_ref[part]
     sat = sat_ref[...]
     spread_m = spread_ref[...].astype(jnp.bfloat16)
     group_m = group_ref[...].astype(jnp.bfloat16)
@@ -570,7 +571,7 @@
         aerosol = aerosol - residue / derivative
     aerosol_q = up(aerosol)
     final_den = aerosol_q + sat
-    p_ref[0] = mass * aerosol_q / final_den
+    p_ref[part] = mass * aerosol_q / final_den
     mass_bar = cot * aerosol_q / final_den
     aerosol_bar = down(cot * mass * sat / (final_den * final_den))
     for newton_step in reversed(range(NEWTON)):
@@ -582,7 +583,7 @@
         over_g2 = over_g * residue / derivative
         mass_bar = mass_bar + up(over_g) * inverse + up(over_g2) * inverse * inverse
         aerosol_bar = over_g2 * slope
-    g_ref[0] = mass_bar * 0.5 * (1.0 + x / root)
+    g_ref[part] = mass_bar * 0.5 * (1.0 + x / root)
 
 
 def chemistry_step(filtered, seed_aerosol, volatility, cotangent):
@@ -592,11 +593,11 @@
     group_m = level_table(levels, species)
     spread_m = group_m.T
     sat = jnp.tile(volatility, levels)[None, :]
-    big = pl.BlockSpec((1, cols, channels), lambda i: (i, 0, 0))
-    small = pl.BlockSpec((1, cols, levels), lambda i: (i, 0, 0))
+    big = pl.BlockSpec((POLAR, cols, channels), lambda i: (i, 0, 0))
+    small = pl.BlockSpec((POLAR, cols, levels), lambda i: (i, 0, 0))
     return pl.pallas_call(
         chem_kernel,
-        grid=(rows,),
+        grid=(rows // POLAR,),
         in_specs=[
             big,
             small,

time: 180 us -> 179 us (level)
  no operation moved by 1% of the time
where the time goes in v7:
time: 179 us; the launch traced here: 178 us
  waiting for transfers between devices  84.3 us (47%)
  starting transfers between devices  34.7 us (19%)
  Pallas kernels  21.2 us (12%)
  local copies, waits for them, and re-layouts  19.6 us (11%)
  other arithmetic  14.8 us (8%)
  matrix products  2.3 us (1%)
    ppermute x4, waiting for transfers between devices, with_halo(): lax.ppermute(tail, axis, [(i, (i + 1) % count) for i in range(ends)])  74.1 us
    ppermute x4, starting transfers between devices, with_halo(): lax.ppermute(head, axis, [((i + 1) % count, i) for i in range(ends)])  23.2 us
    pallas_call x1, Pallas kernels, chemistry_step(): pl.pallas_call(chem_kernel, grid=(rows // POLAR,), in_specs=[big, small,...  16.6 us
    ppermute x4, starting transfers between devices, with_halo(): lax.ppermute(tail, axis, [(i, (i + 1) % count) for i in range(ends)])  11.5 us
    unnamed x37, local copies, waits for them, and re-layouts  10.5 us
    ppermute x4, waiting for transfers between devices, with_halo(): lax.ppermute(head, axis, [((i + 1) % count, i) for i in range(ends)])  10.2 us
    reshape x2, local copies, waits for them, and re-layouts, polar_step(): blocks = jnp.einsum('sjk,rR->srjRk', table, jnp.eye(polar_count, dtype=jn...  6.05 us
    pallas_call x1, Pallas kernels, polar_step(): pl.pallas_call(owner_kernel, out_shape=[end_shape, end_shape], in_specs=[...  4.54 us
  transfers between devices with their start and end apart: 8, of which 5 were waited for; matrix products, arithmetic and copies ran while one was open for 12% of the time, Pallas kernels for 0%

profile of v7, /device:TPU:1, one launch (start us, length us, event | category | flops | bytes accessed | tf_op | source)
XLA Modules:
  0.0 178.0 jit_solution(12107952405828422004)
XLA Ops:
  0.6 0.9 convert_element_type.30
  1.6 1.0 copy.51
  2.6 1.1 copy.56
  3.7 0.8 copy-done.2
  4.6 0.7 pad_maximum_fusion.19
  5.3 4.4 %collective-permute-start = (f32[4,2,928]{2,1,0:T(2,128)}, f32[4,2,928]{2,1,0:T(2,128)S(1)}, u32[]{:S(2)}, u32[]{:S(2)}) collective-permute-start(f32[4,2,928]{2,1,0:T(2,128)} %get-tuple-element.50), channel_id=1, source_target_pairs={{0,1},{1,2},{2,3},{3,4},{4,5},{5,6},{6,7},{7,8},{8,9},{9,10},{10,1... | collective-permute-start | bytes 89096 | tf_op jit(solution)/shard_map/ppermute | solution.py:23
  9.6 12.1 %collective-permute-start.1 = (f32[4,2,928]{2,1,0:T(2,128)S(1)}, f32[4,2,928]{2,1,0:T(2,128)S(1)}, u32[]{:S(2)}, u32[]{:S(2)}) collective-permute-start(f32[4,2,928]{2,1,0:T(2,128)S(1)} %get-tuple-element.51), channel_id=1, source_target_pairs={{1,0},{2,1},{3,2},{4,3},{5,4},{6,5},{7,6},{8,7},{9,8},{10,9},{11,1... | collective-permute-start | bytes 89096 | tf_op jit(solution)/shard_map/ppermute | solution.py:25
  22.1 0.6 slice_select_fusion.6.s_ref
  22.7 0.6 fusion.46.spread_ref
  23.3 3.1 %fusion.11 = (f32[32,45,32]{2,0,1:T(8,128)S(1)}, f32[32,45,32]{2,0,1:T(8,128)S(1)}) fusion(s32[32,45]{0,1:T(8,128)S(1)} %multiply_add_fusion), kind=kLoop, calls=%fused_computation.29 | loop fusion | flops 414720 | bytes 374400 | tf_op jit(solution)/shard_map/cos | solution.py:154
  26.4 0.3 pad_maximum_fusion.3
  26.7 1.5 multiply_bitcast_fusion
  28.4 0.6 select_n.189.w_ref
  29.0 0.7 broadcast_in_dim_reshape.3.m_ref
  29.7 0.7 copy.65.v_ref
  30.4 0.7 broadcast_in_dim_tile.3.sat_ref
  31.2 1.0 copy.57
  32.1 2.0 %copy.61.cot_ref = f32[4,45,864]{2,1,0:T(8,128)} copy(f32[4,45,864]{2,0,1:T(4,128)} %param.17) | data formatting | bytes 1244160 | tf_op args[8]
  34.1 2.6 %reshape.100 = f32[32,90,128]{2,0,1:T(8,128)} reshape(f32[32,2,45,2,64]{4,3,0,2,1:T(2,128)S(1)} %multiply_bitcast_fusion) | data formatting | bytes 2949120 | tf_op jit(solution)/shard_map/reshape | solution.py:459
  36.7 3.5 %copy.66.t_ref = f32[32,90,128]{2,1,0:T(8,128)} copy(f32[32,90,128]{2,0,1:T(8,128)} %reshape.100) | data formatting | bytes 2949120 | tf_op jit(solution)/shard_map/reshape | solution.py:459
  40.5 1.1 fusion.25
  41.5 0.2 maximum_maximum_fusion.1
  42.1 0.8 copy-done
  42.9 0.5 copy-done.6
  43.6 3.1 %collective-permute-start.2 = (f32[2,45,928]{2,1,0:T(8,128)S(1)}, f32[2,45,928]{2,1,0:T(8,128)S(1)}, u32[]{:S(2)}, u32[]{:S(2)}) collective-permute-start(f32[2,45,928]{2,1,0:T(8,128)S(1)} %get-tuple-element.52), channel_id=1, source_target_pairs={{0,32},{32,64},{64,96},{96,128},{128,160},{160,192},{192,224},{224... | collective-permute-start | bytes 1002248 | tf_op jit(solution)/shard_map/ppermute | solution.py:23
  46.8 2.1 %collective-permute-start.3 = (f32[2,45,928]{2,1,0:T(8,128)S(1)}, f32[2,45,928]{2,1,0:T(8,128)S(1)}, u32[]{:S(2)}, u32[]{:S(2)}) collective-permute-start(f32[2,45,928]{2,1,0:T(8,128)S(1)} %get-tuple-element.53), channel_id=1, source_target_pairs={{32,0},{64,32},{96,64},{128,96},{160,128},{192,160},{224,192},{256... | collective-permute-start | bytes 1002248 | tf_op jit(solution)/shard_map/ppermute | solution.py:25
  48.9 0.9 fusion.21.group_ref
  49.9 1.6 collective-permute-done.2
  51.5 4.4 %collective-permute-done.3 = f32[2,45,928]{2,1,0:T(8,128)S(1)} collective-permute-done((f32[2,45,928]{2,1,0:T(8,128)S(1)}, f32[2,45,928]{2,1,0:T(8,128)S(1)}, u32[]{:S(2)}, u32[]{:S(2)}) %collective-permute-start.3) | collective-permute-done | bytes 334112 | tf_op jit(solution)/shard_map/ppermute | solution.py:25
  56.2 1.2 fusion.23
  57.4 0.3 maximum_maximum_fusion
  57.8 0.4 fusion
  58.2 1.0 copy-done.5
  59.2 1.1 slice_select_fusion
  60.4 16.6 %shard_map.105 = (f32[4,45,864]{2,1,0:T(8,128)}, f32[4,45,864]{2,1,0:T(8,128)}) custom-call(f32[4,45,864]{2,1,0:T(8,128)} %copy-done.4, f32[4,45,32]{2,1,0:T(8,128)} %copy-done.7, f32[4,45,864]{2,1,0:T(8,128)} %copy.61.cot_ref, f32[1,864]{1,0:T(1,128)} %broadcast_in_dim_tile.3.sat_ref, f32[32,864]{1,0:T(8,128)} %fusion.46.spread_ref, f32[864,32]{1,0:T(8,128)} %fusion.21.group_ref), custom_call_target="tpu_custom_call" | custom-call | tf_op jit(solution)/shard_map/pallas_call | solution.py:598
  77.0 4.5 %shard_map.104 = (f32[2,45,864]{2,1,0:T(8,128)}, f32[2,45,864]{2,1,0:T(8,128)}) custom-call(f32[2,45,864]{2,1,0:T(8,128)} %get-tuple-element.61.x_ref, f32[2,45,864]{2,1,0:T(8,128)} %get-tuple-element.60.c_ref, f32[2,45,32]{2,1,0:T(8,128)} %slice_select_fusion.6.s_ref, f32[1,128]{1,0:T(1,128)} %select_n.189.w_ref, f32[1,90]{1,0:T(1,128)} %broadcast_in_dim_reshape.3.m_ref, ...), custom_call_target="tpu_custom_call" | custom-call | tf_op jit(solution)/shard_map/pallas_call | solution.py:469
  81.5 1.0 slice_select_fusion.3
  82.7 0.3 fusion.5
  83.2 2.1 %collective-permute-start.4 = (f32[2,45,864]{2,1,0:T(8,128)S(1)}, f32[2,45,864]{2,1,0:T(8,128)S(1)}, u32[]{:S(2)}, u32[]{:S(2)}) collective-permute-start(f32[2,45,864]{2,1,0:T(8,128)S(1)} %slice.260), channel_id=1, source_target_pairs={{0,32},{32,64},{64,96},{96,128},{128,160},{160,192},{192,224},{224... | collective-permute-start | bytes 933128 | tf_op jit(solution)/shard_map/ppermute | solution.py:23
  85.3 72.5 %collective-permute-done.4 = f32[2,45,864]{2,1,0:T(8,128)S(1)} collective-permute-done((f32[2,45,864]{2,1,0:T(8,128)S(1)}, f32[2,45,864]{2,1,0:T(8,128)S(1)}, u32[]{:S(2)}, u32[]{:S(2)}) %collective-permute-start.4) | collective-permute-done | bytes 311072 | tf_op jit(solution)/shard_map/ppermute | solution.py:23
  157.9 2.0 %collective-permute-start.5 = (f32[2,45,864]{2,1,0:T(8,128)S(1)}, f32[2,45,864]{2,1,0:T(8,128)S(1)}, u32[]{:S(2)}, u32[]{:S(2)}) collective-permute-start(f32[2,45,864]{2,1,0:T(8,128)S(1)} %get-tuple-element.41), channel_id=1, source_target_pairs={{32,0},{64,32},{96,64},{128,96},{160,128},{192,160},{224,192},{256... | collective-permute-start | bytes 933128 | tf_op jit(solution)/shard_map/ppermute | solution.py:25
  160.1 1.1 copy.69
  161.2 5.3 %collective-permute-done.5 = f32[2,45,864]{2,1,0:T(8,128)S(1)} collective-permute-done((f32[2,45,864]{2,1,0:T(8,128)S(1)}, f32[2,45,864]{2,1,0:T(8,128)S(1)}, u32[]{:S(2)}, u32[]{:S(2)}) %collective-permute-start.5) | collective-permute-done | bytes 311072 | tf_op jit(solution)/shard_map/ppermute | solution.py:25
  166.9 1.9 %collective-permute-start.6 = (f32[4,2,864]{2,1,0:T(2,128)S(1)}, f32[4,2,864]{2,1,0:T(2,128)S(1)}, u32[]{:S(2)}, u32[]{:S(2)}) collective-permute-start(f32[4,2,864]{2,1,0:T(2,128)S(1)} %get-tuple-element.38), channel_id=1, source_target_pairs={{0,1},{1,2},{2,3},{3,4},{4,5},{5,6},{6,7},{7,8},{8,9},{9,10},{10,1... | collective-permute-start | bytes 82952 | tf_op jit(solution)/shard_map/ppermute | solution.py:23
  168.8 7.0 %collective-permute-start.7 = (f32[4,2,864]{2,1,0:T(2,128)S(1)}, f32[4,2,864]{2,1,0:T(2,128)S(1)}, u32[]{:S(2)}, u32[]{:S(2)}) collective-permute-start(f32[4,2,864]{2,1,0:T(2,128)S(1)} %get-tuple-element.39), channel_id=1, source_target_pairs={{1,0},{2,1},{3,2},{4,3},{5,4},{6,5},{7,6},{8,7},{9,8},{10,9},{11,1... | collective-permute-start | bytes 82952 | tf_op jit(solution)/shard_map/ppermute | solution.py:25
  175.8 0.3 pad_add_fusion.2
  176.2 0.5 collective-permute-done.7
  177.0 1.1 copy.70
  (68 shorter events, 3.0 us)
Async XLA Ops:
  0.6 21.2 %copy-start.11 = (f32[4,45,32]{1,2,0:T(8,128)S(1)}, f32[4,45,32]{1,2,0:T(8,128)}, u32[]{:S(2)}) copy-start(f32[4,45,32]{1,2,0:T(8,128)} %param.15) | copy-start | bytes 69124
  1.5 20.5 %copy-start.13 = (s32[4]{0:T(128)S(1)}, s32[4]{0:T(128)}, u32[]{:S(2)}) copy-start(s32[4]{0:T(128)} %param.14) | copy-start | bytes 52
  3.7 0.9 copy-start.2
  5.3 34.9 %collective-permute-start = (f32[4,2,928]{2,1,0:T(2,128)}, f32[4,2,928]{2,1,0:T(2,128)S(1)}, u32[]{:S(2)}, u32[]{:S(2)}) collective-permute-start(f32[4,2,928]{2,1,0:T(2,128)} %get-tuple-element.50), channel_id=1, source_target_pairs={{0,1},{1,2},{2,3},{3,4},{4,5},{5,6},{6,7},{7,8},{8,9},{9,10},{10,1... | collective-permute-start | bytes 89096 | tf_op jit(solution)/shard_map/ppermute | solution.py:23
  9.6 30.6 %collective-permute-start.1 = (f32[4,2,928]{2,1,0:T(2,128)S(1)}, f32[4,2,928]{2,1,0:T(2,128)S(1)}, u32[]{:S(2)}, u32[]{:S(2)}) collective-permute-start(f32[4,2,928]{2,1,0:T(2,128)S(1)} %get-tuple-element.51), channel_id=1, source_target_pairs={{1,0},{2,1},{3,2},{4,3},{5,4},{6,5},{7,6},{8,7},{9,8},{10,9},{11,1... | collective-permute-start | bytes 89096 | tf_op jit(solution)/shard_map/ppermute | solution.py:25
  22.0 4.7 %copy-start.7 = (f32[4,45,32]{2,1,0:T(8,128)}, f32[4,45,32]{2,1,0:T(8,128)S(1)}, u32[]{:S(2)}) copy-start(f32[4,45,32]{2,1,0:T(8,128)S(1)} %copy.63.seed_ref) | copy-start | bytes 69124
  26.7 1.6 copy-start.14
  26.7 4.3 %copy-start.12 = (s32[4,45,32]{1,2,0:T(8,128)S(1)}, s32[4,45,32]{1,2,0:T(8,128)}, u32[]{:S(2)}) copy-start(s32[4,45,32]{1,2,0:T(8,128)} %param.13) | copy-start | bytes 69124
  36.7 3.5 %copy-start.3 = (f32[4,45,864]{2,1,0:T(8,128)S(1)}, f32[4,45,864]{2,1,0:T(8,128)}, u32[]{:S(2)}) copy-start(f32[4,45,864]{2,1,0:T(8,128)} %copy-done.2) | copy-start | bytes 1866244
  41.5 1.4 copy-start
  41.8 1.6 copy-start.6
  43.6 7.8 %collective-permute-start.2 = (f32[2,45,928]{2,1,0:T(8,128)S(1)}, f32[2,45,928]{2,1,0:T(8,128)S(1)}, u32[]{:S(2)}, u32[]{:S(2)}) collective-permute-start(f32[2,45,928]{2,1,0:T(8,128)S(1)} %get-tuple-element.52), channel_id=1, source_target_pairs={{0,32},{32,64},{64,96},{96,128},{128,160},{160,192},{192,224},{224... | collective-permute-start | bytes 1002248 | tf_op jit(solution)/shard_map/ppermute | solution.py:23
  46.8 9.1 %collective-permute-start.3 = (f32[2,45,928]{2,1,0:T(8,128)S(1)}, f32[2,45,928]{2,1,0:T(8,128)S(1)}, u32[]{:S(2)}, u32[]{:S(2)}) collective-permute-start(f32[2,45,928]{2,1,0:T(8,128)S(1)} %get-tuple-element.53), channel_id=1, source_target_pairs={{32,0},{64,32},{96,64},{128,96},{160,128},{192,160},{224,192},{256... | collective-permute-start | bytes 1002248 | tf_op jit(solution)/shard_map/ppermute | solution.py:25
  58.1 1.1 copy-start.5
  59.2 1.1 copy-start.4
  77.0 4.6 %copy-start.9 = (f32[4,45,864]{2,1,0:T(8,128)S(1)}, f32[4,45,864]{2,1,0:T(8,128)}, u32[]{:S(2)}) copy-start(f32[4,45,864]{2,1,0:T(8,128)} %get-tuple-element.9) | copy-start | bytes 1866244
  83.2 76.7 %copy-start.8 = (f32[4,45,864]{2,1,0:T(8,128)S(1)}, f32[4,45,864]{2,1,0:T(8,128)}, u32[]{:S(2)}) copy-start(f32[4,45,864]{2,1,0:T(8,128)} %get-tuple-element.7) | copy-start | bytes 1866244
  83.2 76.7 %copy-start.10 = (f32[2,45,864]{2,1,0:T(8,128)S(1)}, f32[2,45,864]{2,1,0:T(8,128)}, u32[]{:S(2)}) copy-start(f32[2,45,864]{2,1,0:T(8,128)} %get-tuple-element.6) | copy-start | bytes 933124
  83.2 74.5 %collective-permute-start.4 = (f32[2,45,864]{2,1,0:T(8,128)S(1)}, f32[2,45,864]{2,1,0:T(8,128)S(1)}, u32[]{:S(2)}, u32[]{:S(2)}) collective-permute-start(f32[2,45,864]{2,1,0:T(8,128)S(1)} %slice.260), channel_id=1, source_target_pairs={{0,32},{32,64},{64,96},{96,128},{128,160},{160,192},{192,224},{224... | collective-permute-start | bytes 933128 | tf_op jit(solution)/shard_map/ppermute | solution.py:23
  157.9 8.6 %collective-permute-start.5 = (f32[2,45,864]{2,1,0:T(8,128)S(1)}, f32[2,45,864]{2,1,0:T(8,128)S(1)}, u32[]{:S(2)}, u32[]{:S(2)}) collective-permute-start(f32[2,45,864]{2,1,0:T(8,128)S(1)} %get-tuple-element.41), channel_id=1, source_target_pairs={{32,0},{64,32},{96,64},{128,96},{160,128},{192,160},{224,192},{256... | collective-permute-start | bytes 933128 | tf_op jit(solution)/shard_map/ppermute | solution.py:25
  161.2 5.4 %copy-start.1 = (f32[3,4,46,864]{3,2,1,0:T(8,128)S(1)}, f32[3,4,46,864]{3,2,1,0:T(8,128)}, u32[]{:S(2)}) copy-start(f32[3,4,46,864]{3,2,1,0:T(8,128)} %copy-done) | copy-start | bytes 5723140
  166.9 9.3 %collective-permute-start.6 = (f32[4,2,864]{2,1,0:T(2,128)S(1)}, f32[4,2,864]{2,1,0:T(2,128)S(1)}, u32[]{:S(2)}, u32[]{:S(2)}) collective-permute-start(f32[4,2,864]{2,1,0:T(2,128)S(1)} %get-tuple-element.38), channel_id=1, source_target_pairs={{0,1},{1,2},{2,3},{3,4},{4,5},{5,6},{6,7},{7,8},{8,9},{9,10},{10,1... | collective-permute-start | bytes 82952 | tf_op jit(solution)/shard_map/ppermute | solution.py:23
  168.8 7.9 %collective-permute-start.7 = (f32[4,2,864]{2,1,0:T(2,128)S(1)}, f32[4,2,864]{2,1,0:T(2,128)S(1)}, u32[]{:S(2)}, u32[]{:S(2)}) collective-permute-start(f32[4,2,864]{2,1,0:T(2,128)S(1)} %get-tuple-element.39), channel_id=1, source_target_pairs={{1,0},{2,1},{3,2},{4,3},{5,4},{6,5},{7,6},{8,7},{9,8},{10,9},{11,1... | collective-permute-start | bytes 82952 | tf_op jit(solution)/shard_map/ppermute | solution.py:25

commit v8 on v7

--- a/solution.py
+++ b/solution.py
@@ -335,7 +335,7 @@
     band = lax.axis_index("lat")
     bands = lax.axis_size("lat")
     active = jnp.logical_or(band == 0, band == bands - 1)
-    hi = lax.Precision.HIGHEST
+    hi = lax.Precision.HIGH
     mesh_id = pl.DeviceIdType.MESH
     nt = (((1,), (1,)), ((), ()))
 

time: 179 us -> 175 us (0.978)
  waiting for transfers between devices: 84.3 us -> 80.6 us
    ppermute x4, waiting for transfers between devices: 74.1 us -> 70.4 us  [with_halo(): lax.ppermute(tail, axis, [(i, (i + 1) % count) for i in range(ends)])]
where the time goes in v8:
time: 175 us; the launch traced here: 174 us
  waiting for transfers between devices  80.6 us (46%)
  starting transfers between devices  34.7 us (20%)
  Pallas kernels  21.2 us (12%)
  local copies, waits for them, and re-layouts  19.6 us (11%)
  other arithmetic  14.7 us (8%)
  matrix products  2.3 us (1%)
    ppermute x4, waiting for transfers between devices, with_halo(): lax.ppermute(tail, axis, [(i, (i + 1) % count) for i in range(ends)])  70.4 us
    ppermute x4, starting transfers between devices, with_halo(): lax.ppermute(head, axis, [((i + 1) % count, i) for i in range(ends)])  23.2 us
    pallas_call x1, Pallas kernels, chemistry_step(): pl.pallas_call(chem_kernel, grid=(rows // POLAR,), in_specs=[big, small,...  16.6 us
    ppermute x4, starting transfers between devices, with_halo(): lax.ppermute(tail, axis, [(i, (i + 1) % count) for i in range(ends)])  11.5 us
    unnamed x37, local copies, waits for them, and re-layouts  10.5 us
    ppermute x4, waiting for transfers between devices, with_halo(): lax.ppermute(head, axis, [((i + 1) % count, i) for i in range(ends)])  10.2 us
    reshape x2, local copies, waits for them, and re-layouts, polar_step(): blocks = jnp.einsum('sjk,rR->srjRk', table, jnp.eye(polar_count, dtype=jn...  6.05 us
    pallas_call x1, Pallas kernels, polar_step(): pl.pallas_call(owner_kernel, out_shape=[end_shape, end_shape], in_specs=[...  4.54 us
  transfers between devices with their start and end apart: 8, of which 5 were waited for; matrix products, arithmetic and copies ran while one was open for 12% of the time, Pallas kernels for 0%

profile of v8, /device:TPU:1, one launch (start us, length us, event | category | flops | bytes accessed | tf_op | source)
XLA Modules:
  0.0 174.3 jit_solution(13095391763441093884)
XLA Ops:
  0.6 0.9 convert_element_type.30
  1.6 1.0 copy.51
  2.6 1.1 copy.56
  3.7 0.8 copy-done.2
  4.6 0.7 pad_maximum_fusion.19
  5.3 4.4 %collective-permute-start = (f32[4,2,928]{2,1,0:T(2,128)}, f32[4,2,928]{2,1,0:T(2,128)S(1)}, u32[]{:S(2)}, u32[]{:S(2)}) collective-permute-start(f32[4,2,928]{2,1,0:T(2,128)} %get-tuple-element.50), channel_id=1, source_target_pairs={{0,1},{1,2},{2,3},{3,4},{4,5},{5,6},{6,7},{7,8},{8,9},{9,10},{10,1... | collective-permute-start | bytes 89096 | tf_op jit(solution)/shard_map/ppermute | solution.py:23
  9.6 12.1 %collective-permute-start.1 = (f32[4,2,928]{2,1,0:T(2,128)S(1)}, f32[4,2,928]{2,1,0:T(2,128)S(1)}, u32[]{:S(2)}, u32[]{:S(2)}) collective-permute-start(f32[4,2,928]{2,1,0:T(2,128)S(1)} %get-tuple-element.51), channel_id=1, source_target_pairs={{1,0},{2,1},{3,2},{4,3},{5,4},{6,5},{7,6},{8,7},{9,8},{10,9},{11,1... | collective-permute-start | bytes 89096 | tf_op jit(solution)/shard_map/ppermute | solution.py:25
  22.1 0.6 slice_select_fusion.6.s_ref
  22.7 0.6 fusion.46.spread_ref
  23.3 3.1 %fusion.11 = (f32[32,45,32]{2,0,1:T(8,128)S(1)}, f32[32,45,32]{2,0,1:T(8,128)S(1)}) fusion(s32[32,45]{0,1:T(8,128)S(1)} %multiply_add_fusion), kind=kLoop, calls=%fused_computation.29 | loop fusion | flops 414720 | bytes 374400 | tf_op jit(solution)/shard_map/cos | solution.py:154
  26.4 0.3 pad_maximum_fusion.3
  26.7 1.5 multiply_bitcast_fusion
  28.4 0.6 select_n.189.w_ref
  29.0 0.7 broadcast_in_dim_reshape.3.m_ref
  29.7 0.7 copy.65.v_ref
  30.4 0.7 broadcast_in_dim_tile.3.sat_ref
  31.2 1.0 copy.57
  32.1 2.0 %copy.61.cot_ref = f32[4,45,864]{2,1,0:T(8,128)} copy(f32[4,45,864]{2,0,1:T(4,128)} %param.17) | data formatting | bytes 1244160 | tf_op args[8]
  34.1 2.6 %reshape.100 = f32[32,90,128]{2,0,1:T(8,128)} reshape(f32[32,2,45,2,64]{4,3,0,2,1:T(2,128)S(1)} %multiply_bitcast_fusion) | data formatting | bytes 2949120 | tf_op jit(solution)/shard_map/reshape | solution.py:459
  36.7 3.5 %copy.66.t_ref = f32[32,90,128]{2,1,0:T(8,128)} copy(f32[32,90,128]{2,0,1:T(8,128)} %reshape.100) | data formatting | bytes 2949120 | tf_op jit(solution)/shard_map/reshape | solution.py:459
  40.5 1.1 fusion.25
  41.5 0.2 maximum_maximum_fusion.1
  42.1 0.8 copy-done
  42.9 0.5 copy-done.6
  43.6 3.1 %collective-permute-start.2 = (f32[2,45,928]{2,1,0:T(8,128)S(1)}, f32[2,45,928]{2,1,0:T(8,128)S(1)}, u32[]{:S(2)}, u32[]{:S(2)}) collective-permute-start(f32[2,45,928]{2,1,0:T(8,128)S(1)} %get-tuple-element.52), channel_id=1, source_target_pairs={{0,32},{32,64},{64,96},{96,128},{128,160},{160,192},{192,224},{224... | collective-permute-start | bytes 1002248 | tf_op jit(solution)/shard_map/ppermute | solution.py:23
  46.8 2.1 %collective-permute-start.3 = (f32[2,45,928]{2,1,0:T(8,128)S(1)}, f32[2,45,928]{2,1,0:T(8,128)S(1)}, u32[]{:S(2)}, u32[]{:S(2)}) collective-permute-start(f32[2,45,928]{2,1,0:T(8,128)S(1)} %get-tuple-element.53), channel_id=1, source_target_pairs={{32,0},{64,32},{96,64},{128,96},{160,128},{192,160},{224,192},{256... | collective-permute-start | bytes 1002248 | tf_op jit(solution)/shard_map/ppermute | solution.py:25
  48.9 0.9 fusion.21.group_ref
  49.9 1.6 collective-permute-done.2
  51.5 4.4 %collective-permute-done.3 = f32[2,45,928]{2,1,0:T(8,128)S(1)} collective-permute-done((f32[2,45,928]{2,1,0:T(8,128)S(1)}, f32[2,45,928]{2,1,0:T(8,128)S(1)}, u32[]{:S(2)}, u32[]{:S(2)}) %collective-permute-start.3) | collective-permute-done | bytes 334112 | tf_op jit(solution)/shard_map/ppermute | solution.py:25
  56.2 1.2 fusion.23
  57.4 0.3 maximum_maximum_fusion
  57.8 0.4 fusion
  58.2 1.0 copy-done.5
  59.2 1.1 slice_select_fusion
  60.3 16.6 %shard_map.105 = (f32[4,45,864]{2,1,0:T(8,128)}, f32[4,45,864]{2,1,0:T(8,128)}) custom-call(f32[4,45,864]{2,1,0:T(8,128)} %copy-done.4, f32[4,45,32]{2,1,0:T(8,128)} %copy-done.7, f32[4,45,864]{2,1,0:T(8,128)} %copy.61.cot_ref, f32[1,864]{1,0:T(1,128)} %broadcast_in_dim_tile.3.sat_ref, f32[32,864]{1,0:T(8,128)} %fusion.46.spread_ref, f32[864,32]{1,0:T(8,128)} %fusion.21.group_ref), custom_call_target="tpu_custom_call" | custom-call | tf_op jit(solution)/shard_map/pallas_call | solution.py:598
  76.9 4.5 %shard_map.104 = (f32[2,45,864]{2,1,0:T(8,128)}, f32[2,45,864]{2,1,0:T(8,128)}) custom-call(f32[2,45,864]{2,1,0:T(8,128)} %get-tuple-element.61.x_ref, f32[2,45,864]{2,1,0:T(8,128)} %get-tuple-element.60.c_ref, f32[2,45,32]{2,1,0:T(8,128)} %slice_select_fusion.6.s_ref, f32[1,128]{1,0:T(1,128)} %select_n.189.w_ref, f32[1,90]{1,0:T(1,128)} %broadcast_in_dim_reshape.3.m_ref, ...), custom_call_target="tpu_custom_call" | custom-call | tf_op jit(solution)/shard_map/pallas_call | solution.py:469
  81.5 1.0 slice_select_fusion.3
  82.7 0.3 fusion.5
  83.2 2.1 %collective-permute-start.4 = (f32[2,45,864]{2,1,0:T(8,128)S(1)}, f32[2,45,864]{2,1,0:T(8,128)S(1)}, u32[]{:S(2)}, u32[]{:S(2)}) collective-permute-start(f32[2,45,864]{2,1,0:T(8,128)S(1)} %slice.260), channel_id=1, source_target_pairs={{0,32},{32,64},{64,96},{96,128},{128,160},{160,192},{192,224},{224... | collective-permute-start | bytes 933128 | tf_op jit(solution)/shard_map/ppermute | solution.py:23
  85.3 68.8 %collective-permute-done.4 = f32[2,45,864]{2,1,0:T(8,128)S(1)} collective-permute-done((f32[2,45,864]{2,1,0:T(8,128)S(1)}, f32[2,45,864]{2,1,0:T(8,128)S(1)}, u32[]{:S(2)}, u32[]{:S(2)}) %collective-permute-start.4) | collective-permute-done | bytes 311072 | tf_op jit(solution)/shard_map/ppermute | solution.py:23
  154.1 2.0 %collective-permute-start.5 = (f32[2,45,864]{2,1,0:T(8,128)S(1)}, f32[2,45,864]{2,1,0:T(8,128)S(1)}, u32[]{:S(2)}, u32[]{:S(2)}) collective-permute-start(f32[2,45,864]{2,1,0:T(8,128)S(1)} %get-tuple-element.41), channel_id=1, source_target_pairs={{32,0},{64,32},{96,64},{128,96},{160,128},{192,160},{224,192},{256... | collective-permute-start | bytes 933128 | tf_op jit(solution)/shard_map/ppermute | solution.py:25
  156.3 1.1 copy.69
  157.4 5.3 %collective-permute-done.5 = f32[2,45,864]{2,1,0:T(8,128)S(1)} collective-permute-done((f32[2,45,864]{2,1,0:T(8,128)S(1)}, f32[2,45,864]{2,1,0:T(8,128)S(1)}, u32[]{:S(2)}, u32[]{:S(2)}) %collective-permute-start.5) | collective-permute-done | bytes 311072 | tf_op jit(solution)/shard_map/ppermute | solution.py:25
  163.1 1.9 %collective-permute-start.6 = (f32[4,2,864]{2,1,0:T(2,128)S(1)}, f32[4,2,864]{2,1,0:T(2,128)S(1)}, u32[]{:S(2)}, u32[]{:S(2)}) collective-permute-start(f32[4,2,864]{2,1,0:T(2,128)S(1)} %get-tuple-element.38), channel_id=1, source_target_pairs={{0,1},{1,2},{2,3},{3,4},{4,5},{5,6},{6,7},{7,8},{8,9},{9,10},{10,1... | collective-permute-start | bytes 82952 | tf_op jit(solution)/shard_map/ppermute | solution.py:23
  165.1 7.0 %collective-permute-start.7 = (f32[4,2,864]{2,1,0:T(2,128)S(1)}, f32[4,2,864]{2,1,0:T(2,128)S(1)}, u32[]{:S(2)}, u32[]{:S(2)}) collective-permute-start(f32[4,2,864]{2,1,0:T(2,128)S(1)} %get-tuple-element.39), channel_id=1, source_target_pairs={{1,0},{2,1},{3,2},{4,3},{5,4},{6,5},{7,6},{8,7},{9,8},{10,9},{11,1... | collective-permute-start | bytes 82952 | tf_op jit(solution)/shard_map/ppermute | solution.py:25
  172.0 0.3 pad_add_fusion.2
  172.5 0.5 collective-permute-done.7
  173.2 1.1 copy.70
  (68 shorter events, 3.0 us)
Async XLA Ops:
  0.6 21.2 %copy-start.11 = (f32[4,45,32]{1,2,0:T(8,128)S(1)}, f32[4,45,32]{1,2,0:T(8,128)}, u32[]{:S(2)}) copy-start(f32[4,45,32]{1,2,0:T(8,128)} %param.15) | copy-start | bytes 69124
  1.5 20.5 %copy-start.13 = (s32[4]{0:T(128)S(1)}, s32[4]{0:T(128)}, u32[]{:S(2)}) copy-start(s32[4]{0:T(128)} %param.14) | copy-start | bytes 52
  3.7 0.9 copy-start.2
  5.3 34.9 %collective-permute-start = (f32[4,2,928]{2,1,0:T(2,128)}, f32[4,2,928]{2,1,0:T(2,128)S(1)}, u32[]{:S(2)}, u32[]{:S(2)}) collective-permute-start(f32[4,2,928]{2,1,0:T(2,128)} %get-tuple-element.50), channel_id=1, source_target_pairs={{0,1},{1,2},{2,3},{3,4},{4,5},{5,6},{6,7},{7,8},{8,9},{9,10},{10,1... | collective-permute-start | bytes 89096 | tf_op jit(solution)/shard_map/ppermute | solution.py:23
  9.6 30.6 %collective-permute-start.1 = (f32[4,2,928]{2,1,0:T(2,128)S(1)}, f32[4,2,928]{2,1,0:T(2,128)S(1)}, u32[]{:S(2)}, u32[]{:S(2)}) collective-permute-start(f32[4,2,928]{2,1,0:T(2,128)S(1)} %get-tuple-element.51), channel_id=1, source_target_pairs={{1,0},{2,1},{3,2},{4,3},{5,4},{6,5},{7,6},{8,7},{9,8},{10,9},{11,1... | collective-permute-start | bytes 89096 | tf_op jit(solution)/shard_map/ppermute | solution.py:25
  22.0 4.7 %copy-start.7 = (f32[4,45,32]{2,1,0:T(8,128)}, f32[4,45,32]{2,1,0:T(8,128)S(1)}, u32[]{:S(2)}) copy-start(f32[4,45,32]{2,1,0:T(8,128)S(1)} %copy.63.seed_ref) | copy-start | bytes 69124
  26.7 1.6 copy-start.14
  26.7 4.3 %copy-start.12 = (s32[4,45,32]{1,2,0:T(8,128)S(1)}, s32[4,45,32]{1,2,0:T(8,128)}, u32[]{:S(2)}) copy-start(s32[4,45,32]{1,2,0:T(8,128)} %param.13) | copy-start | bytes 69124
  36.7 3.5 %copy-start.3 = (f32[4,45,864]{2,1,0:T(8,128)S(1)}, f32[4,45,864]{2,1,0:T(8,128)}, u32[]{:S(2)}) copy-start(f32[4,45,864]{2,1,0:T(8,128)} %copy-done.2) | copy-start | bytes 1866244
  41.5 1.4 copy-start
  41.8 1.6 copy-start.6
  43.6 7.8 %collective-permute-start.2 = (f32[2,45,928]{2,1,0:T(8,128)S(1)}, f32[2,45,928]{2,1,0:T(8,128)S(1)}, u32[]{:S(2)}, u32[]{:S(2)}) collective-permute-start(f32[2,45,928]{2,1,0:T(8,128)S(1)} %get-tuple-element.52), channel_id=1, source_target_pairs={{0,32},{32,64},{64,96},{96,128},{128,160},{160,192},{192,224},{224... | collective-permute-start | bytes 1002248 | tf_op jit(solution)/shard_map/ppermute | solution.py:23
  46.8 9.1 %collective-permute-start.3 = (f32[2,45,928]{2,1,0:T(8,128)S(1)}, f32[2,45,928]{2,1,0:T(8,128)S(1)}, u32[]{:S(2)}, u32[]{:S(2)}) collective-permute-start(f32[2,45,928]{2,1,0:T(8,128)S(1)} %get-tuple-element.53), channel_id=1, source_target_pairs={{32,0},{64,32},{96,64},{128,96},{160,128},{192,160},{224,192},{256... | collective-permute-start | bytes 1002248 | tf_op jit(solution)/shard_map/ppermute | solution.py:25
  58.1 1.1 copy-start.5
  59.2 1.1 copy-start.4
  76.9 4.6 %copy-start.9 = (f32[4,45,864]{2,1,0:T(8,128)S(1)}, f32[4,45,864]{2,1,0:T(8,128)}, u32[]{:S(2)}) copy-start(f32[4,45,864]{2,1,0:T(8,128)} %get-tuple-element.9) | copy-start | bytes 1866244
  83.2 73.0 %copy-start.8 = (f32[4,45,864]{2,1,0:T(8,128)S(1)}, f32[4,45,864]{2,1,0:T(8,128)}, u32[]{:S(2)}) copy-start(f32[4,45,864]{2,1,0:T(8,128)} %get-tuple-element.7) | copy-start | bytes 1866244
  83.2 73.0 %copy-start.10 = (f32[2,45,864]{2,1,0:T(8,128)S(1)}, f32[2,45,864]{2,1,0:T(8,128)}, u32[]{:S(2)}) copy-start(f32[2,45,864]{2,1,0:T(8,128)} %get-tuple-element.6) | copy-start | bytes 933124
  83.2 70.8 %collective-permute-start.4 = (f32[2,45,864]{2,1,0:T(8,128)S(1)}, f32[2,45,864]{2,1,0:T(8,128)S(1)}, u32[]{:S(2)}, u32[]{:S(2)}) collective-permute-start(f32[2,45,864]{2,1,0:T(8,128)S(1)} %slice.260), channel_id=1, source_target_pairs={{0,32},{32,64},{64,96},{96,128},{128,160},{160,192},{192,224},{224... | collective-permute-start | bytes 933128 | tf_op jit(solution)/shard_map/ppermute | solution.py:23
  154.1 8.6 %collective-permute-start.5 = (f32[2,45,864]{2,1,0:T(8,128)S(1)}, f32[2,45,864]{2,1,0:T(8,128)S(1)}, u32[]{:S(2)}, u32[]{:S(2)}) collective-permute-start(f32[2,45,864]{2,1,0:T(8,128)S(1)} %get-tuple-element.41), channel_id=1, source_target_pairs={{32,0},{64,32},{96,64},{128,96},{160,128},{192,160},{224,192},{256... | collective-permute-start | bytes 933128 | tf_op jit(solution)/shard_map/ppermute | solution.py:25
  157.4 5.4 %copy-start.1 = (f32[3,4,46,864]{3,2,1,0:T(8,128)S(1)}, f32[3,4,46,864]{3,2,1,0:T(8,128)}, u32[]{:S(2)}) copy-start(f32[3,4,46,864]{3,2,1,0:T(8,128)} %copy-done) | copy-start | bytes 5723140
  163.1 9.3 %collective-permute-start.6 = (f32[4,2,864]{2,1,0:T(2,128)S(1)}, f32[4,2,864]{2,1,0:T(2,128)S(1)}, u32[]{:S(2)}, u32[]{:S(2)}) collective-permute-start(f32[4,2,864]{2,1,0:T(2,128)S(1)} %get-tuple-element.38), channel_id=1, source_target_pairs={{0,1},{1,2},{2,3},{3,4},{4,5},{5,6},{6,7},{7,8},{8,9},{9,10},{10,1... | collective-permute-start | bytes 82952 | tf_op jit(solution)/shard_map/ppermute | solution.py:23
  165.1 7.9 %collective-permute-start.7 = (f32[4,2,864]{2,1,0:T(2,128)S(1)}, f32[4,2,864]{2,1,0:T(2,128)S(1)}, u32[]{:S(2)}, u32[]{:S(2)}) collective-permute-start(f32[4,2,864]{2,1,0:T(2,128)S(1)} %get-tuple-element.39), channel_id=1, source_target_pairs={{1,0},{2,1},{3,2},{4,3},{5,4},{6,5},{7,6},{8,7},{9,8},{10,9},{11,1... | collective-permute-start | bytes 82952 | tf_op jit(solution)/shard_map/ppermute | solution.py:25
